TPU v7x, 32 devices: a whole 2x2x4 slice. The times are simulated.
32 devices in a mesh: dp: 2 (over core), ctx: 4 (over y, x), tp: 4 (over z).
Axes of the slice: x: 2, y: 2, z: 4, core: 2. Of those that a mesh axis runs over, the one named last changes fastest.
Arguments:
- tokens: bfloat16 [4, 1024, 768], P('dp', ('ctx', 'tp')), may hold values from -6 to 6
- timesteps: int32 [4, 4], P('dp', 'ctx'), may hold values from 0 to 999
- query_weight: bfloat16 [768, 768], P('dp', 'tp'), may hold values from -0.21875 to 0.21875
- key_weight: bfloat16 [768, 768], P('dp', 'tp'), may hold values from -0.21875 to 0.21875
- value_weight: bfloat16 [768, 768], P('dp', 'tp'), may hold values from -0.21875 to 0.21875
- out_weight: bfloat16 [768, 768], P('dp', 'tp'), may hold values from -6 to 6
- up_weight: bfloat16 [768, 3072], P('dp', 'tp'), may hold values from -0.21875 to 0.21875
- down_weight: bfloat16 [768, 3072], P('dp', 'tp'), may hold values from -0.21875 to 0.21875
- modulation_weight: bfloat16 [768, 4608], P('dp'), may hold values from -0.4375 to 0.4375
- cotangent: bfloat16 [4, 1024, 768], P('dp', ('ctx', 'tp')), may hold values from -6 to 6
Outputs:
- result: bfloat16 [4, 1024, 768], P('dp', ('ctx', 'tp'))
- grad_tokens: float32 [4, 1024, 768], P('dp', ('ctx', 'tp'))
- grad_query: float32 [768, 768], P('dp', 'tp')
- grad_key: float32 [768, 768], P('dp', 'tp')
- grad_value: float32 [768, 768], P('dp', 'tp')
- grad_out: float32 [768, 768], P('dp', 'tp')
- grad_up: float32 [768, 3072], P('dp', 'tp')
- grad_down: float32 [768, 3072], P('dp', 'tp')
- grad_modulation: float32 [768, 4608], P('dp', 'tp')
All inputs are finite; a program needn't handle non-finite values.
Results may differ from a plain program's by a relative error of at most 0.019.
Values may be sent and summed in bfloat16 or wider, within the bound.
A program may use at most 128 MiB of HBM per device.

v0:
```python
import math

import jax
import jax.numpy as jnp
from jax import lax
from jax.sharding import PartitionSpec as P

HEAD_DIM = 64


norm_eps = 1e-06
big_negative = -1e30
contract_rows = (((0,), (0,)), ((), ()))
contract_cols = (((1,), (1,)), ((), ()))


def norm_rows(row_data):
    center = row_data - jnp.mean(row_data, axis=-1, keepdims=True)
    spread = jnp.mean(center * center, axis=-1, keepdims=True)
    return center * lax.rsqrt(spread + norm_eps)


def modulate(row_data, shift_vec, scale_vec):
    return norm_rows(row_data) * (1.0 + scale_vec) + shift_vec


def rotate(row_data, places, turn_sign):
    half_dim = row_data.shape[-1] // 2
    freq_rates = jnp.exp(
        jnp.arange(half_dim, dtype=jnp.float32) * (-2.0 * math.log(10000.0) / row_data.shape[-1])
    )
    angles = places.astype(jnp.float32)[:, None] * freq_rates[None, :]
    cosine = jnp.cos(angles)[:, None, :]
    sine_part = turn_sign * jnp.sin(angles)[:, None, :]
    first_half = row_data[..., :half_dim]
    second_half = row_data[..., half_dim:]
    return jnp.concatenate(
        [
            first_half * cosine - second_half * sine_part,
            first_half * sine_part + second_half * cosine,
        ],
        axis=-1,
    )


def time_embed(step_ids, model_width):
    half_dim = model_width // 2
    freq_rates = jnp.exp(jnp.arange(half_dim, dtype=jnp.float32) * (-math.log(10000.0) / half_dim))
    angles = step_ids.astype(jnp.float32)[..., None] * freq_rates
    return jnp.concatenate([jnp.sin(angles), jnp.cos(angles)], axis=-1)


def gather_rows(row_data):
    return lax.all_gather(row_data, "tp", axis=1, tiled=True)


def share_sums(row_data):
    return lax.psum_scatter(
        row_data.astype(jnp.bfloat16), "tp", scatter_dimension=1, tiled=True
    ).astype(jnp.float32)


def split_blocks(pieces, block_len, head_count):
    block_count = pieces.shape[1] // block_len
    return pieces.reshape(pieces.shape[0], block_count, block_len, head_count, HEAD_DIM).transpose(
        1, 0, 2, 3, 4
    )


def shards(
    tokens,
    timesteps,
    query_weight,
    key_weight,
    value_weight,
    out_weight,
    up_weight,
    down_weight,
    modulation_weight,
    cotangent,
):
    seq_count, row_count, model_width = tokens.shape
    block_len = row_count * lax.axis_size("tp")
    head_count = query_weight.shape[1] // HEAD_DIM
    score_scale = HEAD_DIM ** (-0.5)
    my_block = lax.axis_index("ctx")
    places = jnp.tile(my_block * block_len + jnp.arange(block_len, dtype=jnp.int32), seq_count)
    token_rows = seq_count * block_len
    full_query, full_key, full_value, full_out, full_up, full_down, full_mod = (
        lax.all_gather(query_weight, "dp", axis=0, tiled=True),
        lax.all_gather(key_weight, "dp", axis=0, tiled=True),
        lax.all_gather(value_weight, "dp", axis=0, tiled=True),
        lax.all_gather(out_weight, "dp", axis=0, tiled=True),
        lax.all_gather(up_weight, "dp", axis=0, tiled=True),
        lax.all_gather(down_weight, "dp", axis=0, tiled=True),
        lax.all_gather(modulation_weight, "dp", axis=0, tiled=True),
    )
    embed_low = jax.nn.silu(time_embed(timesteps[:, 0], model_width)).astype(jnp.bfloat16)
    modulation = jnp.dot(embed_low, full_mod, preferred_element_type=jnp.float32).reshape(
        seq_count, 6, 1, model_width
    )
    shift_one, scale_one, gate_one = (modulation[:, 0], modulation[:, 1], modulation[:, 2])
    shift_two, scale_two, gate_two = (modulation[:, 3], modulation[:, 4], modulation[:, 5])
    residual = tokens.astype(jnp.float32)
    normed = modulate(residual, shift_one, scale_one).astype(jnp.bfloat16)
    normed_all = gather_rows(normed).reshape(token_rows, model_width)
    flat_heads = (token_rows, head_count, HEAD_DIM)
    head_shape = (seq_count, block_len, head_count, HEAD_DIM)
    wide_shape = (seq_count, block_len, head_count * HEAD_DIM)
    query_pre = jnp.dot(normed_all, full_query, preferred_element_type=jnp.float32).reshape(
        flat_heads
    )
    key_pre = jnp.dot(normed_all, full_key, preferred_element_type=jnp.float32).reshape(flat_heads)
    queries = rotate(query_pre, places, 1.0).astype(jnp.bfloat16).reshape(head_shape)
    key_rows = rotate(key_pre, places, 1.0).astype(jnp.bfloat16).reshape(head_shape)
    values = (
        jnp.dot(normed_all, full_value, preferred_element_type=jnp.float32)
        .astype(jnp.bfloat16)
        .reshape(head_shape)
    )
    stat_shape = (seq_count, head_count, block_len)
    start_state = (
        jnp.full(stat_shape, big_negative, jnp.float32),
        jnp.zeros(stat_shape, jnp.float32),
        jnp.zeros(stat_shape + (HEAD_DIM,), jnp.float32),
    )
    carried = start_state
    pieces = (
        lax.all_gather(key_rows.reshape(wide_shape), "ctx", axis=1, tiled=True),
        lax.all_gather(values.reshape(wide_shape), "ctx", axis=1, tiled=True),
    )
    key_blocks = split_blocks(pieces[0], block_len, head_count)
    value_blocks = split_blocks(pieces[1], block_len, head_count)
    block_order = jnp.arange(key_blocks.shape[0], dtype=jnp.int32)

    def forward_one_block(running, block_item):
        key_blk, value_blk, block_idx = block_item
        allowed = block_idx <= my_block
        run_max, denom_sum, weighted = running
        scores = (
            jnp.einsum("sqhd,skhd->shqk", queries, key_blk, preferred_element_type=jnp.float32)
            * score_scale
        )
        new_max = jnp.where(allowed, jnp.maximum(run_max, jnp.max(scores, axis=-1)), run_max)
        prob_tile = jnp.where(allowed, jnp.exp(scores - new_max[..., None]), 0.0)
        fade = jnp.exp(run_max - new_max)
        denom_sum = denom_sum * fade + jnp.sum(prob_tile, axis=-1)
        weighted = weighted * fade[..., None] + jnp.einsum(
            "shqk,skhd->shqd",
            prob_tile.astype(jnp.bfloat16),
            value_blk,
            preferred_element_type=jnp.float32,
        )
        return ((new_max, denom_sum, weighted), None)

    carried, unused = lax.scan(forward_one_block, carried, (key_blocks, value_blocks, block_order))
    run_max, denom_sum, weighted = carried
    log_norm = run_max + jnp.log(denom_sum)
    attended = weighted / denom_sum[..., None]
    attended_low = (
        attended.astype(jnp.bfloat16)
        .transpose(0, 2, 1, 3)
        .reshape(token_rows, head_count * HEAD_DIM)
    )
    branch = share_sums(
        lax.dot_general(
            attended_low, full_out, contract_cols, preferred_element_type=jnp.float32
        ).reshape(seq_count, block_len, model_width)
    )
    middle = residual + gate_one * branch
    normed_two = modulate(middle, shift_two, scale_two).astype(jnp.bfloat16)
    normed_two_all = gather_rows(normed_two).reshape(token_rows, model_width)
    hidden = jnp.dot(normed_two_all, full_up, preferred_element_type=jnp.float32)
    active = jax.nn.gelu(hidden).astype(jnp.bfloat16)
    mlp_branch = share_sums(
        lax.dot_general(
            active, full_down, contract_cols, preferred_element_type=jnp.float32
        ).reshape(seq_count, block_len, model_width)
    )
    result = (middle + gate_two * mlp_branch).astype(jnp.bfloat16)
    back_query, back_key, back_value, back_out, back_up, back_down = (
        lax.all_gather(query_weight, "dp", axis=0, tiled=True),
        lax.all_gather(key_weight, "dp", axis=0, tiled=True),
        lax.all_gather(value_weight, "dp", axis=0, tiled=True),
        lax.all_gather(out_weight, "dp", axis=0, tiled=True),
        lax.all_gather(up_weight, "dp", axis=0, tiled=True),
        lax.all_gather(down_weight, "dp", axis=0, tiled=True),
    )
    upstream = cotangent.astype(jnp.float32)
    grad_gate_two = jnp.sum(upstream * mlp_branch, axis=1)
    mlp_grad = gather_rows((gate_two * upstream).astype(jnp.bfloat16)).reshape(
        token_rows, model_width
    )
    active_grad = jnp.dot(mlp_grad, back_down, preferred_element_type=jnp.float32)
    grad_down = lax.dot_general(mlp_grad, active, contract_rows, preferred_element_type=jnp.float32)
    gelu_pull = jax.vjp(jax.nn.gelu, hidden)[1]
    hidden_grad = gelu_pull(active_grad)[0].astype(jnp.bfloat16)
    grad_up = lax.dot_general(
        normed_two_all, hidden_grad, contract_rows, preferred_element_type=jnp.float32
    )
    normed_two_grad = share_sums(
        lax.dot_general(
            hidden_grad, back_up, contract_cols, preferred_element_type=jnp.float32
        ).reshape(seq_count, block_len, model_width)
    )
    pull_two = jax.vjp(modulate, middle, shift_two, scale_two)[1]
    middle_norm, grad_shift_two, grad_scale_two = pull_two(normed_two_grad)
    middle_grad = upstream + middle_norm
    grad_gate_one = jnp.sum(middle_grad * branch, axis=1)
    branch_grad = gather_rows((gate_one * middle_grad).astype(jnp.bfloat16)).reshape(
        token_rows, model_width
    )
    grad_out = lax.dot_general(
        branch_grad, attended_low, contract_rows, preferred_element_type=jnp.float32
    )
    out_grads = (
        jnp.dot(branch_grad, back_out, preferred_element_type=jnp.float32)
        .astype(jnp.bfloat16)
        .reshape(head_shape)
    )
    row_delta = jnp.einsum("sqhd,shqd->shq", out_grads.astype(jnp.float32), attended)
    log_all, delta_all = (
        lax.all_gather(log_norm, "ctx", axis=2, tiled=True),
        lax.all_gather(row_delta, "ctx", axis=2, tiled=True),
    )
    carried = jnp.zeros(head_shape, jnp.float32)
    pieces = (
        lax.all_gather(key_rows.reshape(wide_shape), "ctx", axis=1, tiled=True),
        lax.all_gather(values.reshape(wide_shape), "ctx", axis=1, tiled=True),
    )
    key_blocks = split_blocks(pieces[0], block_len, head_count)
    value_blocks = split_blocks(pieces[1], block_len, head_count)
    block_order = jnp.arange(key_blocks.shape[0], dtype=jnp.int32)

    def query_one_block(running, block_item):
        key_blk, value_blk, block_idx = block_item
        allowed = block_idx <= my_block
        scores = (
            jnp.einsum("sqhd,skhd->shqk", queries, key_blk, preferred_element_type=jnp.float32)
            * score_scale
        )
        prob_tile = jnp.where(allowed, jnp.exp(scores - log_norm[..., None]), 0.0)
        prob_grad = jnp.einsum(
            "sqhd,skhd->shqk", out_grads, value_blk, preferred_element_type=jnp.float32
        )
        score_grad = (prob_tile * (prob_grad - row_delta[..., None]) * score_scale).astype(
            jnp.bfloat16
        )
        return (
            running
            + jnp.einsum(
                "shqk,skhd->sqhd", score_grad, key_blk, preferred_element_type=jnp.float32
            ),
            None,
        )

    carried, unused = lax.scan(query_one_block, carried, (key_blocks, value_blocks, block_order))
    query_grad = carried
    carried = (jnp.zeros(head_shape, jnp.float32), jnp.zeros(head_shape, jnp.float32))
    pieces = (
        lax.all_gather(queries.reshape(wide_shape), "ctx", axis=1, tiled=True),
        lax.all_gather(out_grads.reshape(wide_shape), "ctx", axis=1, tiled=True),
    )
    query_blocks = split_blocks(pieces[0], block_len, head_count)
    grad_blocks = split_blocks(pieces[1], block_len, head_count)
    block_count = query_blocks.shape[0]
    log_blocks = log_all.reshape(seq_count, head_count, block_count, block_len).transpose(
        2, 0, 1, 3
    )
    delta_blocks = delta_all.reshape(seq_count, head_count, block_count, block_len).transpose(
        2, 0, 1, 3
    )
    block_order = jnp.arange(block_count, dtype=jnp.int32)

    def key_one_block(running, block_item):
        query_blk, grad_blk, log_blk, delta_blk, block_idx = block_item
        allowed = block_idx >= my_block
        key_acc, value_acc = running
        scores = (
            jnp.einsum("sqhd,skhd->shqk", query_blk, key_rows, preferred_element_type=jnp.float32)
            * score_scale
        )
        prob_tile = jnp.where(allowed, jnp.exp(scores - log_blk[..., None]), 0.0)
        value_acc = value_acc + jnp.einsum(
            "shqk,sqhd->skhd",
            prob_tile.astype(jnp.bfloat16),
            grad_blk,
            preferred_element_type=jnp.float32,
        )
        prob_grad = jnp.einsum(
            "sqhd,skhd->shqk", grad_blk, values, preferred_element_type=jnp.float32
        )
        score_grad = (prob_tile * (prob_grad - delta_blk[..., None]) * score_scale).astype(
            jnp.bfloat16
        )
        key_acc = key_acc + jnp.einsum(
            "shqk,sqhd->skhd", score_grad, query_blk, preferred_element_type=jnp.float32
        )
        return ((key_acc, value_acc), None)

    carried, unused = lax.scan(
        key_one_block, carried, (query_blocks, grad_blocks, log_blocks, delta_blocks, block_order)
    )
    key_grad, value_grad = carried
    head_width = head_count * HEAD_DIM
    query_back = (
        rotate(query_grad.reshape(flat_heads), places, -1.0)
        .astype(jnp.bfloat16)
        .reshape(token_rows, head_width)
    )
    key_back = (
        rotate(key_grad.reshape(flat_heads), places, -1.0)
        .astype(jnp.bfloat16)
        .reshape(token_rows, head_width)
    )
    value_back = value_grad.astype(jnp.bfloat16).reshape(token_rows, head_width)
    normed_partial = lax.dot_general(
        query_back, back_query, contract_cols, preferred_element_type=jnp.float32
    )
    normed_partial = normed_partial + lax.dot_general(
        key_back, back_key, contract_cols, preferred_element_type=jnp.float32
    )
    normed_partial = normed_partial + lax.dot_general(
        value_back, back_value, contract_cols, preferred_element_type=jnp.float32
    )
    normed_grad = share_sums(normed_partial.reshape(seq_count, block_len, model_width))
    grad_query = lax.dot_general(
        normed_all, query_back, contract_rows, preferred_element_type=jnp.float32
    )
    grad_key = lax.dot_general(
        normed_all, key_back, contract_rows, preferred_element_type=jnp.float32
    )
    grad_value = lax.dot_general(
        normed_all, value_back, contract_rows, preferred_element_type=jnp.float32
    )
    pull_one = jax.vjp(modulate, residual, shift_one, scale_one)[1]
    residual_norm, grad_shift_one, grad_scale_one = pull_one(normed_grad)
    grad_tokens = middle_grad + residual_norm
    modulation_grad = jnp.stack(
        [
            grad_shift_one[:, 0],
            grad_scale_one[:, 0],
            grad_gate_one,
            grad_shift_two[:, 0],
            grad_scale_two[:, 0],
            grad_gate_two,
        ],
        axis=1,
    ).reshape(seq_count, 6 * model_width)
    modulation_total = lax.psum(modulation_grad.astype(jnp.bfloat16), "tp").astype(jnp.float32)
    col_count = 6 * model_width // lax.axis_size("tp")
    modulation_cols = lax.dynamic_slice_in_dim(
        modulation_total, lax.axis_index("tp") * col_count, col_count, 1
    )
    grad_modulation = lax.dot_general(
        embed_low.astype(jnp.float32),
        modulation_cols,
        contract_rows,
        precision=lax.Precision.HIGHEST,
    )
    totals = lax.psum(
        (grad_query, grad_key, grad_value, grad_out, grad_up, grad_down, grad_modulation),
        ("dp", "ctx"),
    )
    half_rows = model_width // lax.axis_size("dp")
    first_row = lax.axis_index("dp") * half_rows
    shares = tuple(
        (lax.dynamic_slice_in_dim(grad_total, first_row, half_rows, 0) for grad_total in totals)
    )
    return (
        result,
        grad_tokens,
        shares[0],
        shares[1],
        shares[2],
        shares[3],
        shares[4],
        shares[5],
        shares[6],
    )


def solution(mesh):
    return jax.shard_map(
        shards,
        mesh=mesh,
        in_specs=(
            P("dp", ("ctx", "tp"), None),
            P("dp", "ctx"),
            P("dp", "tp"),
            P("dp", "tp"),
            P("dp", "tp"),
            P("dp", "tp"),
            P("dp", "tp"),
            P("dp", "tp"),
            P("dp", None),
            P("dp", ("ctx", "tp"), None),
        ),
        out_specs=(
            P("dp", ("ctx", "tp"), None),
            P("dp", ("ctx", "tp"), None),
            P("dp", "tp"),
            P("dp", "tp"),
            P("dp", "tp"),
            P("dp", "tp"),
            P("dp", "tp"),
            P("dp", "tp"),
            P("dp", "tp"),
        ),
        check_vma=False,
    )
```

profile of v0, /device:TPU:0, one launch (start us, length us, event | category | flops | bytes accessed | tf_op | source)
XLA Modules:
  0.0 545.9 jit_solution(7815384014327641498)
XLA Ops:
  9.3 2.1 all_gather.63
  11.4 2.0 all_gather.61
  13.4 2.0 all_gather.64
  15.4 2.0 all_gather.66
  18.6 11.6 %all-gather.4.cloned.1.call-done = bf16[768,4608]{1,0:T(8,128)(2,1)} async-done(((bf16[384,4608]{1,0:T(8,128)(2,1)}), bf16[768,4608]{1,0:T(8,128)(2,1)}) %all-gather.4.cloned.1.call-update) | async-done | bytes 7077904 | tf_op jit(solution)/shard_map/all_gather | solution.py:96
  30.2 4.0 fusion.100
  35.2 19.8 %all_gather.60 = bf16[2,256,768]{2,1,0:T(8,128)(2,1)S(1)} all-gather(bf16[2,64,768]{2,1,0:T(8,128)(2,1)S(1)} %fusion.76), channel_id=1, replica_groups=mesh['dp'=2,'ctx'=4,'tp'=4] {'tp'}, dimensions={1}, use_global_device_ids=true | all-gather | bytes 983040 | tf_op jit(solution)/shard_map/all_gather | solution.py:54
  58.0 14.7 %all_gather.62 = bf16[2,1024,192]{1,2,0:T(8,128)(2,1)S(1)} all-gather(bf16[2,256,192]{1,2,0:T(8,128)(2,1)S(1)} %copy.57), channel_id=1, replica_groups=mesh['dp'=2,'ctx'=4,'tp'=4] {'ctx'}, dimensions={1}, use_global_device_ids=true | all-gather | bytes 983040 | tf_op jit(solution)/shard_map/all_gather | solution.py:129
  74.3 14.8 %all_gather.65 = bf16[2,1024,192]{1,2,0:T(8,128)(2,1)} all-gather(bf16[2,256,192]{1,2,0:T(8,128)(2,1)S(1)} %bitcast.309), channel_id=1, replica_groups=mesh['dp'=2,'ctx'=4,'tp'=4] {'ctx'}, dimensions={1}, use_global_device_ids=true | all-gather | bytes 983040 | tf_op jit(solution)/shard_map/all_gather | solution.py:130
  89.1 1.9 reshape.309
  92.0 13.5 %while.39 = (s32[]{:T(128)}, f32[2,3,256]{2,1,0:T(4,128)S(1)}, f32[2,3,256]{2,1,0:T(4,128)S(1)}, f32[2,3,256,64]{2,3,1,0:T(8,128)S(1)}, s32[4]{0:T(128)S(1)}, /*...) while((s32[]{:T(128)}, f32[2,3,256]{2,1,0:T(4,128)S(1)}, ...), condition=%wide.region_5.6_spmd.clone, body=%wide.region_2.5_spmd.clone.sunk | while | flops 104113152 | bytes 6193313 | solution.py:156
  94.1 1.3 convolution_add_fusion.2
  97.4 1.3 convolution_add_fusion.2
  100.8 1.3 convolution_add_fusion.2
  104.2 1.3 convolution_add_fusion.2
  107.7 27.1 %all_gather.70 = bf16[2,256,768]{2,1,0:T(8,128)(2,1)S(1)} all-gather(bf16[2,64,768]{2,1,0:T(8,128)(2,1)S(1)} %fusion.85), channel_id=1, replica_groups=mesh['dp'=2,'ctx'=4,'tp'=4] {'tp'}, dimensions={1}, use_global_device_ids=true | all-gather | bytes 983040 | tf_op jit(solution)/shard_map/all_gather | solution.py:54
  134.9 3.4 fusion.106
  141.6 19.6 %all_gather.67 = bf16[2,256,768]{2,1,0:T(8,128)(2,1)S(1)} all-gather(bf16[2,64,768]{2,1,0:T(8,128)(2,1)S(1)} %add_convert_fusion.1), channel_id=1, replica_groups=mesh['dp'=2,'ctx'=4,'tp'=4] {'tp'}, dimensions={1}, use_global_device_ids=true | all-gather | bytes 983040 | tf_op jit(solution)/shard_map/all_gather | solution.py:54
  161.2 4.7 fusion.66
  165.9 1.7 convolution_convert_fusion
  168.6 13.4 %all_gather.72 = bf16[2,1024,192]{1,2,0:T(8,128)(2,1)} all-gather(bf16[2,256,192]{1,2,0:T(8,128)(2,1)S(1)} %copy.67), channel_id=1, replica_groups=mesh['dp'=2,'ctx'=4,'tp'=4] {'ctx'}, dimensions={1}, use_global_device_ids=true | all-gather | bytes 983040 | tf_op jit(solution)/shard_map/all_gather | solution.py:261
  182.0 2.0 reshape.315
  185.1 8.9 %all_gather.73 = f32[2,3,1024]{2,1,0:T(4,128)S(1)} all-gather(f32[2,3,256]{2,1,0:T(4,128)S(1)} %log_add_fusion), channel_id=1, replica_groups=mesh['dp'=2,'ctx'=4,'tp'=4] {'ctx'}, dimensions={2}, use_global_device_ids=true | all-gather | bytes 30720 | tf_op jit(solution)/shard_map/all_gather | solution.py:223
  200.5 15.7 %all_gather.71 = bf16[2,256,768]{2,1,0:T(8,128)(2,1)S(1)} all-gather(bf16[2,64,768]{2,1,0:T(8,128)(2,1)S(1)} %multiply_convert_fusion.3), channel_id=1, replica_groups=mesh['dp'=2,'ctx'=4,'tp'=4] {'tp'}, dimensions={1}, use_global_device_ids=true | all-gather | bytes 983040 | tf_op jit(solution)/shard_map/all_gather | solution.py:54
  218.5 8.8 %all_gather.75 = f32[2,3,1024]{2,1,0:T(4,128)} all-gather(f32[2,3,256]{2,1,0:T(4,128)S(1)} %multiply_reduce_fusion), channel_id=1, replica_groups=mesh['dp'=2,'ctx'=4,'tp'=4] {'ctx'}, dimensions={2}, use_global_device_ids=true | all-gather | bytes 30720 | tf_op jit(solution)/shard_map/all_gather | solution.py:224
  227.9 24.7 %while.40 = (s32[]{:T(128)}, f32[2,256,3,64]{1,3,2,0:T(8,128)}, bf16[4,2,256,3,64]{2,4,3,1,0:T(8,128)(2,1)}, s32[4]{0:T(128)}, s32[]{:T(128)}, /*index=5*/bf16[2...) while((s32[]{:T(128)}, f32[2,256,3,64]{1,3,2,0:T(8,128)}, ...), condition=%wide.region_14.15_spmd.clone, body=%wide.region_13.14_spmd.clone.sunk | while | flops 153944064 | bytes 4931743 | solution.py:257
  227.9 1.3 dynamic_slice.149
  229.9 1.3 fusion.185
  231.3 2.7 fusion.186
  233.9 1.3 dynamic_slice.149
  236.0 1.3 fusion.185
  237.3 2.8 fusion.186
  240.2 1.3 dynamic_slice.149
  242.2 1.3 fusion.185
  243.5 2.8 fusion.186
  246.4 1.3 dynamic_slice.149
  248.4 1.3 fusion.185
  249.8 2.8 fusion.186
  252.6 1.8 copy.105
  254.4 1.4 reshape.333
  256.7 13.4 %all_gather.74 = bf16[2,1024,192]{1,2,0:T(8,128)(2,1)S(1)} all-gather(bf16[2,256,192]{1,2,0:T(8,128)(2,1)S(1)} %bitcast.310), channel_id=1, replica_groups=mesh['dp'=2,'ctx'=4,'tp'=4] {'ctx'}, dimensions={1}, use_global_device_ids=true | all-gather | bytes 983040 | tf_op jit(solution)/shard_map/all_gather | solution.py:262
  272.2 31.7 %while.41 = (s32[]{:T(128)}, f32[2,256,3,64]{1,3,2,0:T(8,128)}, f32[2,256,3,64]{1,3,2,0:T(8,128)S(1)}, bf16[4,2,256,3,64]{2,4,3,1,0:T(8,128)(2,1)}, s32[4]{0:T(1...) while((s32[]{:T(128)}, f32[2,256,3,64]{1,3,2,0:T(8,128)}, ...), condition=%wide.region_16.17_spmd.clone, body=%wide.region_15.16_spmd.clone.sunk | while | flops 204865536 | bytes 7534257 | solution.py:301
  274.9 1.5 exponential_select_fusion.2
  276.4 2.3 fusion.194
  282.7 1.5 exponential_select_fusion.2
  284.2 2.5 fusion.194
  290.7 1.5 exponential_select_fusion.2
  292.2 2.5 fusion.194
  298.6 1.5 exponential_select_fusion.2
  300.1 2.5 fusion.194
  309.0 3.6 fusion.109
  312.6 2.0 convolution_convert_fusion.1
  314.5 2.3 fusion.102
  321.8 9.1 %reduce-scatter.11.cloned.1.call-done = bf16[2,64,768]{2,1,0:T(8,128)(2,1)} async-done(((bf16[2,256,768]{2,1,0:T(8,128)(2,1)}), bf16[2,64,768]{2,1,0:T(8,128)(2,1)}) %reduce-scatter.11.cloned.1.call-update) | async-done | bytes 196624 | tf_op jit(solution)/shard_map/reduce_scatter | solution.py:58
  333.0 23.4 %reduce-scatter.7.cloned.1.call-done = bf16[2,64,768]{2,1,0:T(8,128)(2,1)} async-done(((bf16[2,256,768]{2,1,0:T(8,128)(2,1)}), bf16[2,64,768]{2,1,0:T(8,128)(2,1)}) %reduce-scatter.7.cloned.1.call-update) | async-done | bytes 196624 | tf_op jit(solution)/shard_map/reduce_scatter | solution.py:58
  356.5 2.3 fusion.81
  358.9 17.5 %psum.62 = bf16[2,4608]{1,0:T(2,128)(2,1)S(1)} all-reduce(bf16[2,4608]{1,0:T(2,128)(2,1)S(1)} %bitcast.327), channel_id=1, replica_groups=mesh['dp'=2,'ctx'=4,'tp'=4] {'tp'}, use_global_device_ids=true, to_apply=%region_32.33 | all-reduce | flops 9216 | bytes 36864 | tf_op jit(solution)/shard_map/psum | solution.py:350
  376.4 2.5 fusion.94
  380.9 147.2 %all-reduce.3.cloned.1.call-done = (f32[768,192]{0,1:T(8,128)}, f32[768,192]{0,1:T(8,128)}, f32[768,192]{0,1:T(8,128)}, f32[768,192]{0,1:T(8,128)}, f32[768,768]...) async-done(((f32[768,192]{0,1:T(8,128)}, f32[768,192]{0,1:T(8,128)}, f32[768,192]{0,1:T(8,128)}, f32[768,192]{0,1:T(8,128)}, f32[768,768]{1,0:T(8,128)}, ...) | async-done | bytes 10616848 | tf_op jit(solution)/shard_map/psum | solution.py:361
  528.1 1.8 constant_dynamic-slice_fusion.8
  529.9 1.7 constant_dynamic-slice_fusion.7
  531.5 1.8 constant_dynamic-slice_fusion.6
  534.1 2.5 constant_dynamic-slice_fusion.4
  537.7 1.3 constant_dynamic-slice_fusion.2
  (333 shorter events, 63.1 us)
Async XLA Ops:
  7.2 4.2 copy-start.47
  7.2 23.0 %all-gather.4.cloned.1.call-start = ((), (), s32[]{:S(2)}) async-start(), calls=%async_computation.4 | async-start | bytes 10616832 | tf_op jit(solution)/shard_map/all_gather | solution.py:96
  8.0 5.5 %copy-start.48 = (bf16[384,192]{0,1:T(8,128)(2,1)S(1)}, bf16[384,192]{0,1:T(8,128)(2,1)}, u32[]{:S(2)}) copy-start(bf16[384,192]{0,1:T(8,128)(2,1)} %param.20) | copy-start | bytes 442372
  8.0 7.5 %copy-start.49 = (bf16[384,192]{0,1:T(8,128)(2,1)S(1)}, bf16[384,192]{0,1:T(8,128)(2,1)}, u32[]{:S(2)}) copy-start(bf16[384,192]{0,1:T(8,128)(2,1)} %param.21) | copy-start | bytes 442372
  8.0 126.9 %all-gather.8.cloned.1.call-start = ((), (), s32[]{:S(2)}) async-start(), calls=%async_computation.7 | async-start | bytes 1769472 | tf_op jit(solution)/shard_map/all_gather | solution.py:95
  8.7 129.6 %reduce-scatter.5.cloned.1.call-start = ((), (), s32[]{:S(2)}) async-start(), calls=%async_computation.5 | async-start | bytes 983040 | tf_op jit(solution)/shard_map/reduce_scatter | solution.py:58
  9.0 26.0 %copy-start.56 = (f32[2,64]{1,0:T(2,128)}, f32[2,64]{1,0:T(2,128)S(1)}, u32[]{:S(2)}) copy-start(f32[2,64]{1,0:T(2,128)S(1)} %broadcast_multiply_fusion.2) | copy-start | bytes 1540
  9.2 6.2 %copy-start.76 = (f32[2,64]{1,0:T(2,128)}, f32[2,64]{1,0:T(2,128)S(1)}, u32[]{:S(2)}) copy-start(f32[2,64]{1,0:T(2,128)S(1)} %fusion.83) | copy-start | bytes 1540
  9.3 25.7 %copy-start.72 = (f32[2,64]{1,0:T(2,128)}, f32[2,64]{1,0:T(2,128)S(1)}, u32[]{:S(2)}) copy-start(f32[2,64]{1,0:T(2,128)S(1)} %fusion.97) | copy-start | bytes 1540
  11.4 44.7 %copy-start.16 = (bf16[768,192]{0,1:T(8,128)(2,1)}, bf16[768,192]{0,1:T(8,128)(2,1)S(1)}, u32[]{:S(2)}) copy-start(bf16[768,192]{0,1:T(8,128)(2,1)S(1)} %all_gather.63) | copy-start | bytes 884740
  13.4 43.1 %copy-start.18 = (bf16[768,192]{0,1:T(8,128)(2,1)}, bf16[768,192]{0,1:T(8,128)(2,1)S(1)}, u32[]{:S(2)}) copy-start(bf16[768,192]{0,1:T(8,128)(2,1)S(1)} %all_gather.61) | copy-start | bytes 884740
  15.4 39.5 %copy-start.14 = (bf16[768,192]{0,1:T(8,128)(2,1)}, bf16[768,192]{0,1:T(8,128)(2,1)S(1)}, u32[]{:S(2)}) copy-start(bf16[768,192]{0,1:T(8,128)(2,1)S(1)} %all_gather.64) | copy-start | bytes 884740
  17.6 16.7 %copy-start.62 = (f32[2,384]{1,0:T(2,128)}, f32[2,384]{1,0:T(2,128)S(1)}, u32[]{:S(2)}) copy-start(f32[2,384]{1,0:T(2,128)S(1)} %get-tuple-element.465) | copy-start | bytes 9220
  17.6 16.7 %copy-start.64 = (f32[2,384]{1,0:T(2,128)}, f32[2,384]{1,0:T(2,128)S(1)}, u32[]{:S(2)}) copy-start(f32[2,384]{1,0:T(2,128)S(1)} %get-tuple-element.466) | copy-start | bytes 9220
  35.0 21.6 %copy-start.44 = (f32[2,1,1,768]{3,0,1,2:T(2,128)}, f32[2,1,1,768]{3,0,1,2:T(2,128)S(1)}, u32[]{:S(2)}) copy-start(f32[2,1,1,768]{3,0,1,2:T(2,128)S(1)} %copy.131) | copy-start | bytes 18436
  106.9 27.8 %copy-start.68 = (f32[2,1,1,768]{3,1,0,2:T(1,128)S(1)}, f32[2,1,1,768]{3,1,0,2:T(1,128)}, u32[]{:S(2)}) copy-start(f32[2,1,1,768]{3,1,0,2:T(1,128)} %get-tuple-element.457) | copy-start | bytes 18436
  106.9 27.9 %copy-start.69 = (f32[2,1,1,768]{3,1,0,2:T(1,128)S(1)}, f32[2,1,1,768]{3,1,0,2:T(1,128)}, u32[]{:S(2)}) copy-start(f32[2,1,1,768]{3,1,0,2:T(1,128)} %get-tuple-element.458) | copy-start | bytes 18436
  107.0 54.2 %all-gather.6.cloned.1.call-start = ((), (), s32[]{:S(2)}) async-start(), calls=%async_computation.6 | async-start | bytes 1769472 | tf_op jit(solution)/shard_map/all_gather | solution.py:94
  107.6 88.7 %reduce-scatter.9.cloned.1.call-start = ((), (), s32[]{:S(2)}) async-start(), calls=%async_computation.9 | async-start | bytes 983040 | tf_op jit(solution)/shard_map/reduce_scatter | solution.py:58
  107.6 27.2 %copy-start.54 = (f32[2,1,1,768]{3,0,1,2:T(2,128)}, f32[2,1,1,768]{3,0,1,2:T(2,128)S(1)}, u32[]{:S(2)}) copy-start(f32[2,1,1,768]{3,0,1,2:T(2,128)S(1)} %copy.129) | copy-start | bytes 18436
  107.7 32.9 %copy-start.36 = (f32[2,1,1,768]{3,0,1,2:T(2,128)}, f32[2,1,1,768]{3,0,1,2:T(2,128)S(1)}, u32[]{:S(2)}) copy-start(f32[2,1,1,768]{3,0,1,2:T(2,128)S(1)} %copy.132) | copy-start | bytes 18436
  134.8 3.5 copy-start.29
  134.8 5.7 %copy-start.39 = (f32[2,768]{1,0:T(2,128)}, f32[2,768]{1,0:T(2,128)S(1)}, u32[]{:S(2)}) copy-start(f32[2,768]{1,0:T(2,128)S(1)} %get-tuple-element.470) | copy-start | bytes 18436
  139.4 26.5 %copy-start.51 = (f32[2,64]{1,0:T(2,128)}, f32[2,64]{1,0:T(2,128)S(1)}, u32[]{:S(2)}) copy-start(f32[2,64]{1,0:T(2,128)S(1)} %broadcast_multiply_fusion.1) | copy-start | bytes 1540
  140.5 25.4 %copy-start.78 = (f32[2,64]{1,0:T(2,128)}, f32[2,64]{1,0:T(2,128)S(1)}, u32[]{:S(2)}) copy-start(f32[2,64]{1,0:T(2,128)S(1)} %multiply_reduce_fusion.1) | copy-start | bytes 1540
  140.5 25.4 %copy-start.58 = (f32[2,64]{1,0:T(2,128)}, f32[2,64]{1,0:T(2,128)S(1)}, u32[]{:S(2)}) copy-start(f32[2,64]{1,0:T(2,128)S(1)} %fusion.98) | copy-start | bytes 1540
  161.2 4.7 copy-start.9
  161.2 4.7 copy-start.80
  167.6 163.2 %reduce-scatter.11.cloned.1.call-start = ((), (), s32[]{:S(2)}) async-start(), calls=%async_computation.10 | async-start | bytes 983040 | tf_op jit(solution)/shard_map/reduce_scatter | solution.py:58
  182.0 12.6 %copy-start.25 = (bf16[512,3,32]{0,2,1:T(8,128)(2,1)S(1)}, bf16[512,3,32]{0,2,1:T(8,128)(2,1)}, u32[]{:S(2)}) copy-start(bf16[512,3,32]{0,2,1:T(8,128)(2,1)} %copy-done.24) | copy-start | bytes 294916
  184.0 12.2 %copy-start.2 = (bf16[2,64,768]{2,1,0:T(8,128)(2,1)S(1)}, bf16[2,64,768]{2,1,0:T(8,128)(2,1)}, u32[]{:S(2)}) copy-start(bf16[2,64,768]{2,1,0:T(8,128)(2,1)} %reduce-scatter.5.cloned.1.call-done) | copy-start | bytes 589828
  185.0 14.3 %copy-start.37 = (f32[2,1,1,768]{3,0,1,2:T(2,128)S(1)}, f32[2,1,1,768]{3,0,1,2:T(2,128)}, u32[]{:S(2)}) copy-start(f32[2,1,1,768]{3,0,1,2:T(2,128)} %copy-done.36) | copy-start | bytes 18436
  185.0 14.3 %copy-start.40 = (f32[2,768]{1,0:T(2,128)S(1)}, f32[2,768]{1,0:T(2,128)}, u32[]{:S(2)}) copy-start(f32[2,768]{1,0:T(2,128)} %copy-done.39) | copy-start | bytes 18436
  185.0 14.3 %copy-start.52 = (f32[2,64]{1,0:T(2,128)S(1)}, f32[2,64]{1,0:T(2,128)}, u32[]{:S(2)}) copy-start(f32[2,64]{1,0:T(2,128)} %copy-done.51) | copy-start | bytes 1540
  185.0 14.3 %copy-start.59 = (f32[2,64]{1,0:T(2,128)S(1)}, f32[2,64]{1,0:T(2,128)}, u32[]{:S(2)}) copy-start(f32[2,64]{1,0:T(2,128)} %copy-done.58) | copy-start | bytes 1540
  185.0 9.6 %copy-start.61 = (f32[2,3,256]{2,1,0:T(4,128)}, f32[2,3,256]{2,1,0:T(4,128)S(1)}, u32[]{:S(2)}) copy-start(f32[2,3,256]{2,1,0:T(4,128)S(1)} %log_add_fusion) | copy-start | bytes 18436
  198.1 19.5 %copy-start.66 = (f32[2,64]{1,0:T(2,128)}, f32[2,64]{1,0:T(2,128)S(1)}, u32[]{:S(2)}) copy-start(f32[2,64]{1,0:T(2,128)S(1)} %multiply_multiply_fusion.3) | copy-start | bytes 1540
  199.3 18.2 %copy-start.74 = (f32[2,64]{1,0:T(2,128)}, f32[2,64]{1,0:T(2,128)S(1)}, u32[]{:S(2)}) copy-start(f32[2,64]{1,0:T(2,128)S(1)} %negate_multiply_fusion.1) | copy-start | bytes 1540
  217.6 10.3 %copy-start.22 = (bf16[512,192]{0,1:T(8,128)(2,1)}, bf16[512,192]{0,1:T(8,128)(2,1)S(1)}, u32[]{:S(2)}) copy-start(bf16[512,192]{0,1:T(8,128)(2,1)S(1)} %convolution_convert_fusion.3) | copy-start | bytes 589828
  270.1 2.1 copy-start.5
  307.9 48.5 %reduce-scatter.7.cloned.1.call-start = ((), (), s32[]{:S(2)}) async-start(), calls=%async_computation.8 | async-start | bytes 983040 | tf_op jit(solution)/shard_map/reduce_scatter | solution.py:58
  309.0 3.6 copy-start.79
  309.0 3.6 copy-start.82
  314.5 2.4 copy-start.8
  316.9 211.2 %all-reduce.3.cloned.1.call-start = ((), (), s32[]{:S(2)}) async-start(), calls=%async_computation.11 | async-start | bytes 21233664 | tf_op jit(solution)/shard_map/psum | solution.py:361
  318.1 2.4 copy-start.7
  319.3 12.5 %copy-start.45 = (f32[2,1,1,768]{3,0,1,2:T(2,128)S(1)}, f32[2,1,1,768]{3,0,1,2:T(2,128)}, u32[]{:S(2)}) copy-start(f32[2,1,1,768]{3,0,1,2:T(2,128)} %copy-done.44) | copy-start | bytes 18436
  319.3 12.5 %copy-start.57 = (f32[2,64]{1,0:T(2,128)S(1)}, f32[2,64]{1,0:T(2,128)}, u32[]{:S(2)}) copy-start(f32[2,64]{1,0:T(2,128)} %copy-done.56) | copy-start | bytes 1540
  319.3 13.7 %copy-start.77 = (f32[2,64]{1,0:T(2,128)S(1)}, f32[2,64]{1,0:T(2,128)}, u32[]{:S(2)}) copy-start(f32[2,64]{1,0:T(2,128)} %copy-done.76) | copy-start | bytes 1540
  319.3 37.1 %copy-start.3 = (bf16[2,64,768]{2,1,0:T(8,128)(2,1)S(1)}, bf16[2,64,768]{2,1,0:T(8,128)(2,1)}, u32[]{:S(2)}) copy-start(bf16[2,64,768]{2,1,0:T(8,128)(2,1)} %reduce-scatter.5.cloned.1.call-done) | copy-start | bytes 589828
  319.3 37.1 %copy-start.13 = (bf16[2,64,768]{2,1,0:T(8,128)(2,1)S(1)}, bf16[2,64,768]{2,1,0:T(8,128)(2,1)}, u32[]{:S(2)}) copy-start(bf16[2,64,768]{2,1,0:T(8,128)(2,1)} %param.25) | copy-start | bytes 589828
  319.3 37.1 %copy-start.38 = (f32[2,1,1,768]{3,0,1,2:T(2,128)S(1)}, f32[2,1,1,768]{3,0,1,2:T(2,128)}, u32[]{:S(2)}) copy-start(f32[2,1,1,768]{3,0,1,2:T(2,128)} %copy-done.36) | copy-start | bytes 18436
  319.3 37.1 %copy-start.41 = (f32[2,768]{1,0:T(2,128)S(1)}, f32[2,768]{1,0:T(2,128)}, u32[]{:S(2)}) copy-start(f32[2,768]{1,0:T(2,128)} %copy-done.39) | copy-start | bytes 18436
  319.4 37.1 %copy-start.53 = (f32[2,64]{1,0:T(2,128)S(1)}, f32[2,64]{1,0:T(2,128)}, u32[]{:S(2)}) copy-start(f32[2,64]{1,0:T(2,128)} %copy-done.51) | copy-start | bytes 1540
  319.4 37.1 %copy-start.55 = (f32[2,1,1,768]{3,0,1,2:T(2,128)S(1)}, f32[2,1,1,768]{3,0,1,2:T(2,128)}, u32[]{:S(2)}) copy-start(f32[2,1,1,768]{3,0,1,2:T(2,128)} %copy-done.54) | copy-start | bytes 18436
  319.4 37.1 %copy-start.60 = (f32[2,64]{1,0:T(2,128)S(1)}, f32[2,64]{1,0:T(2,128)}, u32[]{:S(2)}) copy-start(f32[2,64]{1,0:T(2,128)} %copy-done.58) | copy-start | bytes 1540
  319.4 37.1 %copy-start.67 = (f32[2,64]{1,0:T(2,128)S(1)}, f32[2,64]{1,0:T(2,128)}, u32[]{:S(2)}) copy-start(f32[2,64]{1,0:T(2,128)} %copy-done.66) | copy-start | bytes 1540
  319.4 37.1 %copy-start.73 = (f32[2,64]{1,0:T(2,128)S(1)}, f32[2,64]{1,0:T(2,128)}, u32[]{:S(2)}) copy-start(f32[2,64]{1,0:T(2,128)} %copy-done.72) | copy-start | bytes 1540
  319.4 37.1 %copy-start.75 = (f32[2,64]{1,0:T(2,128)S(1)}, f32[2,64]{1,0:T(2,128)}, u32[]{:S(2)}) copy-start(f32[2,64]{1,0:T(2,128)} %copy-done.74) | copy-start | bytes 1540
  320.6 55.8 %copy-start.63 = (f32[2,384]{1,0:T(2,128)S(1)}, f32[2,384]{1,0:T(2,128)}, u32[]{:S(2)}) copy-start(f32[2,384]{1,0:T(2,128)} %copy-done.62) | copy-start | bytes 9220
  320.6 55.8 %copy-start.65 = (f32[2,384]{1,0:T(2,128)S(1)}, f32[2,384]{1,0:T(2,128)}, u32[]{:S(2)}) copy-start(f32[2,384]{1,0:T(2,128)} %copy-done.64) | copy-start | bytes 9220
  528.1 5.3 copy-start.50
  531.5 5.1 copy-start.35
  534.1 3.6 copy-start.27
  (27 other events, 36.4 us)
Sparse Core Ops, SparseCore 0:
  9.6 20.6 all-gather.3
  31.8 10.3 all-gather.7
  107.1 30.6 reduce-scatter.4
  139.2 8.0 all-gather.5
  167.8 20.7 reduce-scatter.8
  308.0 22.7 reduce-scatter.10
  333.7 22.6 reduce-scatter.6
  379.0 149.0 all-reduce.2
where the time goes:
time: 548 us; the launch traced here: 546 us
  waiting for transfers between devices  193 us (35%)
  blocking collectives  182 us (33%)
  matrix products  78.2 us (14%)
  local copies, waits for them, and re-layouts  49.8 us (9%)
  other arithmetic  18.6 us (3%)
  between operations  15.4 us (3%)
  loops' own time  8.35 us (2%)
    psum x1, waiting for transfers between devices, shards(): lax.psum((grad_query, grad_key, grad_value, grad_out, grad_up, grad_down,...  147 us
    all_gather x4, blocking collectives, gather_rows(): return lax.all_gather(row_data, 'tp', axis=1, tiled=True)  82.2 us
    reduce_scatter x4, waiting for transfers between devices, share_sums(): lax.psum_scatter(row_data.astype(jnp.bfloat16), 'tp', scatter_dimension=1...  32.5 us
    psum x1, blocking collectives, shards(): lax.psum(modulation_grad.astype(jnp.bfloat16), 'tp').astype(jnp.float32)  17.5 us
    all_gather x1, blocking collectives, shards(): lax.all_gather(values.reshape(wide_shape), 'ctx', axis=1, tiled=True)  14.8 us
    all_gather x1, blocking collectives, shards(): lax.all_gather(key_rows.reshape(wide_shape), 'ctx', axis=1, tiled=True)  14.7 us
    all_gather x1, blocking collectives, shards(): lax.all_gather(out_grads.reshape(wide_shape), 'ctx', axis=1, tiled=True)  13.4 us
    all_gather x1, blocking collectives, shards(): lax.all_gather(queries.reshape(wide_shape), 'ctx', axis=1, tiled=True)  13.4 us
  transfers between devices with their start and end apart: 8, of which 4 were waited for; matrix products, arithmetic and copies ran while one was open for 10% of the time, Pallas kernels for 0%

commit v1 on v0

v1 whole, which is shorter than its diff:
```python
import functools
import math

import jax
import jax.numpy as jnp
from jax import lax
from jax.experimental import pallas as pl
from jax.experimental.pallas import tpu as pltpu
from jax.sharding import PartitionSpec as P

MESH = pl.DeviceIdType.MESH
HEAD_DIM = 64
WIN = 256
LANES = 128
EPS = 1e-06
NEG = -1e30
GELU_C = 0.7978845608028654
GELU_A = 0.044715
F32 = jnp.float32
BF16 = jnp.bfloat16
VMEM_BYTES = 62 * 1024 * 1024

NN = (((1,), (0,)), ((), ()))
NT = (((1,), (1,)), ((), ()))
TN = (((0,), (0,)), ((), ()))


def mm(a, b, dims=NN):
    return lax.dot_general(a, b, dims, preferred_element_type=F32)


def norm_parts(x):
    center = x - jnp.mean(x, axis=-1, keepdims=True)
    rstd = lax.rsqrt(jnp.mean(center * center, axis=-1, keepdims=True) + EPS)
    return center * rstd, rstd


def norm_back(grad, unit, rstd, scale):
    dn = grad * (1.0 + scale)
    return rstd * (
        dn
        - jnp.mean(dn, axis=-1, keepdims=True)
        - unit * jnp.mean(dn * unit, axis=-1, keepdims=True)
    )


def remote(src, dst, send, recv, **dev):
    return pltpu.make_async_remote_copy(
        src_ref=src, dst_ref=dst, send_sem=send, recv_sem=recv, device_id=dev, device_id_type=MESH
    )


def chunk_rows(count, devices):
    return 16 * -(-(count // 16) // devices)


class Dims:
    def __init__(self, mesh, tokens, query, up, mod):
        self.nc = mesh.shape["ctx"]
        self.nt = mesh.shape["tp"]
        self.seqs, self.rows, self.width = tokens
        self.block = self.rows * self.nt
        self.hw, self.half = query
        self.heads = self.hw // HEAD_DIM
        self.ff = up[1]
        self.mod = mod[1]
        self.kvw = 2 * self.hw
        self.vlo = self.kvw - WIN
        self.voff = self.hw - self.vlo
        self.wide = 2 * self.ff
        self.heads_rows = 4 * self.hw
        self.mcols = self.mod // self.nt


def scratch_table(z):
    vm = lambda shape, dtype=BF16: pltpu.VMEM(shape, dtype)
    sem = lambda *shape: pltpu.SemaphoreType.DMA(shape)
    full = (z.seqs, z.block, z.width)
    own = (z.seqs, z.rows, z.width)
    parts = (z.nt,) + own
    return dict(
        tok=vm(full),
        cot=vm(full),
        wqt=vm((WIN, z.width)),
        wkvt=vm((z.kvw, z.width)),
        wot=vm((WIN, z.width)),
        wu=vm((z.width, z.ff)),
        wd=vm((z.width, z.ff)),
        wm=vm((z.half, z.mod)),
        emb_s=vm((8, z.half), F32),
        emb_r=vm((8, z.half), F32),
        emb=vm((z.nc, 8, z.half), F32),
        mod_s=vm((8, z.mod), F32),
        mod_r=vm((8, z.mod), F32),
        mod=vm((8, z.mod), F32),
        cosine=vm((z.block, LANES), F32),
        sine=vm((z.block, LANES), F32),
        nrm=vm(full),
        q=vm((z.seqs, z.block, WIN)),
        kv=vm((z.nc, z.seqs, z.block, z.kvw)),
        vt=vm((WIN, z.block)),
        stat=vm((2, 8, z.block), F32),
        acc=vm((z.hw, z.block), F32),
        att=vm((z.seqs, z.hw, z.block), F32),
        attl=vm((z.seqs, z.block, WIN)),
        lse=vm((z.seqs, 8, z.block), F32),
        delta=vm((z.seqs, 8, z.block), F32),
        part=vm(full),
        br_r=vm(parts),
        branch=vm(own, F32),
        middle=vm(own, F32),
        n2=vm(full),
        act=vm((z.seqs, z.block, z.ff)),
        hgrad=vm((z.seqs, z.block, z.ff)),
        mgrad=vm(full),
        g2p=vm(full),
        g2_r=vm(parts),
        mlp=vm(full),
        ml_r=vm(parts),
        midg=vm(own, F32),
        bg=vm(full),
        do=vm((z.seqs, z.block, WIN)),
        dot=vm((WIN, z.block)),
        dqt=vm((z.hw, z.block), F32),
        dq=vm((z.seqs, z.block, WIN), F32),
        dkv=vm((z.seqs, z.block, z.kvw), F32),
        dkv_r=vm((z.nc, z.seqs, z.block, z.kvw)),
        qb=vm((z.seqs, z.block, WIN)),
        kvb=vm((z.seqs, z.block, z.kvw)),
        n1_r=vm(parts),
        ga_s=vm((z.half, z.wide)),
        ga_o=vm((z.half, z.wide)),
        ga_r=vm((z.half, z.wide)),
        ga_c=vm((z.nc, chunk_rows(z.half, z.nc), z.wide)),
        ga_t=vm((z.half, z.wide)),
        gb_s=vm((z.heads_rows, z.half)),
        gb_o=vm((z.heads_rows, z.half)),
        gb_r=vm((z.heads_rows, z.half)),
        gb_c=vm((z.nc, chunk_rows(z.heads_rows, z.nc), z.half)),
        gb_t=vm((z.heads_rows, z.half)),
        msum=vm((8, z.mod), F32),
        mt_r=vm((z.nt, 8, z.mcols), F32),
        md_s=vm((8, z.mcols), F32),
        md_r=vm((8, z.mcols), F32),
        mg=vm((z.nc, 8, z.mcols), F32),
        res=vm(own),
        gtok=vm(own, F32),
        s_loc=sem(16),
        s_w=sem(2, 6),
        s_e=sem(2),
        s_ec=sem(2, z.nc),
        s_m=sem(2, 2),
        s_tok=sem(2, z.nt),
        r_tok=sem(z.nt),
        s_cot=sem(2, z.nt),
        s_kv=sem(z.nc, z.nt),
        r_kv=sem(z.nc, z.nt),
        s_br=sem(z.seqs, z.nt),
        r_br=sem(z.seqs, z.nt),
        s_n2=sem(2, z.nt),
        r_n2=sem(z.nt),
        s_g2=sem(2, z.nt),
        s_ml=sem(2, z.nt),
        s_bg=sem(2, z.nt),
        r_bg=sem(z.nt),
        s_dk=sem(z.nc, z.seqs),
        r_dk=sem(z.nc, z.seqs),
        s_n1=sem(2, z.nt),
        s_ga=sem(2),
        s_gac=sem(2, z.nc),
        s_gag=sem(2, z.nc),
        s_gb=sem(2),
        s_gbc=sem(2, z.nc),
        s_gbg=sem(2, z.nc),
        s_mt=sem(2, z.nt),
        s_md=sem(2),
        s_mc=sem(2, z.nc),
    )


class Box:
    pass


def layer_kernel(z, names, *refs):
    r = Box()
    for name, ref in zip(names, refs):
        setattr(r, name, ref)
    d, c, t = lax.axis_index("dp"), lax.axis_index("ctx"), lax.axis_index("tp")
    other = 1 - d
    nt, nc, rows, block, width, hw = z.nt, z.nc, z.rows, z.block, z.width, z.hw
    seqs, half = z.seqs, z.half

    def each(count, body, first=0):
        def step(i, carry):
            body(i)
            return carry

        lax.fori_loop(first, count, step, 0)

    def span(idx):
        return pl.ds(pl.multiple_of(idx * rows, rows), rows)

    def slot(ref, idx):
        return ref.at[:, span(idx), :]

    def flat(x):
        return x.reshape(x.shape[0] * x.shape[1], x.shape[2])

    def lanes_of(shape, axis=1):
        return lax.broadcasted_iota(jnp.int32, shape, axis)

    local = []

    def fetch(src, dst):
        cp = pltpu.make_async_copy(src, dst, r.s_loc.at[len(local)])
        cp.start()
        local.append(cp)
        return cp

    my_half = pl.ds(pl.multiple_of(d * half, LANES), half)
    weights = [
        (r.wq_in, r.wqt.at[0:hw, my_half]),
        (r.wk_in, r.wkvt.at[0:hw, my_half]),
        (r.wv_in, r.wkvt.at[hw : z.kvw, my_half]),
        (r.wo_in, r.wot.at[z.voff : z.voff + hw, my_half]),
        (r.wu_in, r.wu.at[my_half, :]),
        (r.wd_in, r.wd.at[my_half, :]),
    ]
    first_cols = 2 * width
    cp_tok = fetch(r.tok_in, slot(r.tok, t))
    cp_wm1 = fetch(r.wm_in.at[:, 0:first_cols], r.wm.at[:, 0:first_cols])
    cp_w = [fetch(src, dst) for src, dst in weights]
    cp_wm2 = fetch(r.wm_in.at[:, first_cols : z.mod], r.wm.at[:, first_cols : z.mod])
    cp_cot = fetch(r.cot_in, slot(r.cot, t))

    r.wqt[hw:WIN, :] = jnp.zeros((WIN - hw, width), BF16)
    r.wot[0 : z.voff, :] = jnp.zeros((z.voff, width), BF16)

    bar = pltpu.get_barrier_semaphore()
    pl.semaphore_signal(bar, inc=1, device_id={"dp": other}, device_id_type=MESH)
    for k in range(1, nt):
        pl.semaphore_signal(bar, inc=1, device_id={"tp": (t + k) % nt}, device_id_type=MESH)

    def greet(k):
        pl.semaphore_signal(bar, inc=1, device_id={"ctx": (c + k) % nc}, device_id_type=MESH)

    each(nc, greet, 1)

    row8 = lanes_of((8, half), 0)
    step_of = jnp.where(
        row8 % 2 == 0, r.ts_in[0, 0].astype(F32), r.ts_in[1, 0].astype(F32)
    )
    angle = step_of * r.rate_in[...]
    sin_e, cos_e = jnp.sin(angle), jnp.cos(angle)

    def silu_low(v):
        return (v / (1.0 + jnp.exp(-v))).astype(BF16).astype(F32)

    sin_e, cos_e = silu_low(sin_e), silu_low(cos_e)
    first = d == 0
    own_half = jnp.where(row8 < 2, jnp.where(first, sin_e, cos_e), 0.0)
    r.emb_s[...] = jnp.where(
        (row8 >= 2) & (row8 < 4), jnp.where(first, cos_e, sin_e), 0.0
    )
    pl.semaphore_wait(bar, 1 + (nt - 1) + (nc - 1))

    def line_send(src, buf, send, recv, idx, side):
        to = t + 1 - 2 * side

        @pl.when((to >= 0) & (to < nt))
        def _():
            remote(src, slot(buf, idx), send.at[side, idx], recv.at[idx], tp=to).start()

    def line_open(src, buf, send, recv):
        line_send(src, buf, send, recv, t, 0)
        line_send(src, buf, send, recv, t, 1)

    def line_rest(buf, send, recv, work):
        def far(dist):
            def take(side):
                idx = t + (2 * side - 1) * dist

                @pl.when((idx >= 0) & (idx < nt))
                def _():
                    here = slot(buf, idx)
                    remote(here, here, send.at[side, idx], recv.at[idx], tp=idx).wait_recv()
                    line_send(here, buf, send, recv, idx, side)

            def run(side):
                idx = t + (2 * side - 1) * dist

                @pl.when((idx >= 0) & (idx < nt))
                def _():
                    work(idx)

            each(2, take)
            each(2, run)

        each(nt, far, 1)

    def line_close(buf, send, recv):
        def one(j):
            idx, side = j // 2, j % 2
            to = t + 1 - 2 * side
            passed = ((1 - 2 * side) * (t - idx) >= 0) & (to >= 0) & (to < nt)

            @pl.when(passed)
            def _():
                here = slot(buf, idx)
                remote(here, here, send.at[side, idx], recv.at[idx], tp=to).wait_send()

        each(2 * nt, one)

    def push(src_of, buf, sems, idx):
        remote(src_of(idx), buf.at[t], sems.at[0, idx], sems.at[1, t], tp=idx).start()

    def pull(buf, sems, idx):
        remote(buf.at[idx], buf.at[idx], sems.at[0, idx], sems.at[1, idx], tp=idx).wait_recv()

    def push_done(src_of, buf, sems):
        for k in range(1, nt):
            idx = (t + k) % nt
            remote(src_of(idx), buf.at[t], sems.at[0, idx], sems.at[1, t], tp=idx).wait_send()

    def summed(part, buf):
        total = part[:, span(t), :].astype(F32)
        for k in range(1, nt):
            total = total + buf[(t + k) % nt].astype(F32)
        return total

    line_open(r.tok_in, r.tok, r.s_tok, r.r_tok)
    send_emb = remote(r.emb_s, r.emb_r, r.s_e.at[0], r.s_e.at[1], dp=other)
    send_emb.start()
    send_w = [
        remote(src, dst, r.s_w.at[0, i], r.s_w.at[1, i], dp=other)
        for i, (src, dst) in enumerate(weights)
    ]
    for cp in send_w[:3]:
        cp.start()

    send_emb.wait()
    emb4 = own_half + r.emb_r[...]
    r.emb[pl.ds(c, 1)] = emb4[None]
    emb_low = emb4.astype(BF16)

    def mod_part(lo, hi, which, ready):
        ready.wait()
        r.mod_s[:, lo:hi] = mm(emb_low, r.wm[:, lo:hi])
        cp = remote(
            r.mod_s.at[:, lo:hi], r.mod_r.at[:, lo:hi], r.s_m.at[0, which], r.s_m.at[1, which], dp=other
        )
        cp.start()
        return cp

    def mod_take(lo, hi, cp):
        cp.wait()
        for s in range(seqs):
            r.mod[s : s + 1, lo:hi] = r.mod_s[s : s + 1, lo:hi] + r.mod_r[s + 2 : s + 3, lo:hi]

    def vec(slot_idx):
        lo = slot_idx * width
        return r.mod[0:seqs, lo : lo + width][:, None, :]

    mod1 = mod_part(0, first_cols, 0, cp_wm1)
    for cp in send_w[3:]:
        cp.start()

    def send_ctx_emb(k):
        to = (c + k) % nc
        remote(r.emb.at[c], r.emb.at[c], r.s_ec.at[0, to], r.s_ec.at[1, c], ctx=to).start()

    each(nc, send_ctx_emb, 1)

    place = (c * block + lanes_of((block, LANES), 0)).astype(F32)
    turn = place * r.rope_in[...]
    low_lane = lanes_of((block, LANES)) % HEAD_DIM < HEAD_DIM // 2
    r.cosine[...] = jnp.cos(turn)
    r.sine[...] = jnp.where(low_lane, -jnp.sin(turn), jnp.sin(turn))

    def swap(x):
        low = lanes_of(x.shape) % HEAD_DIM < HEAD_DIM // 2
        return jnp.where(
            low,
            pltpu.roll(x, LANES - HEAD_DIM // 2, 1),
            pltpu.roll(x, HEAD_DIM // 2, 1),
        )

    for i in range(3):
        cp_w[i].wait()
        send_w[i].wait_recv()
    mod_take(0, first_cols, mod1)

    def make_qkv(idx):
        at = span(idx)
        unit, _ = norm_parts(r.tok[:, at, :].astype(F32))
        low = (unit * (1.0 + vec(1)) + vec(0)).astype(BF16)
        r.nrm[:, at, :] = low
        low = flat(low)
        cos1, sin1 = r.cosine[at, :], r.sine[at, :]
        cos2 = jnp.concatenate([cos1] * seqs, axis=0)
        sin2 = jnp.concatenate([sin1] * seqs, axis=0)
        q_pre = mm(low, r.wqt[...], NT)
        kv_pre = mm(low, r.wkvt[...], NT)
        shape = (seqs, rows, LANES)
        for j in range(WIN // LANES):
            x = q_pre[:, j * LANES : (j + 1) * LANES]
            x = (x * cos2 + swap(x) * sin2) * (HEAD_DIM ** -0.5)
            r.q[:, at, j * LANES : (j + 1) * LANES] = x.astype(BF16).reshape(shape)
        for j in range(z.kvw // LANES):
            x = kv_pre[:, j * LANES : (j + 1) * LANES]
            keys = min(max(hw - j * LANES, 0), LANES)
            if keys > 0:
                turned = x * cos2 + swap(x) * sin2
                x = turned if keys == LANES else jnp.where(lanes_of(x.shape) < keys, turned, x)
            r.kv[c, :, at, j * LANES : (j + 1) * LANES] = x.astype(BF16).reshape(shape)

        def send_kv(to):
            mine = r.kv.at[c, :, at, :]
            remote(mine, mine, r.s_kv.at[to, idx], r.r_kv.at[c, idx], ctx=to).start()

        each(nc, send_kv, c + 1)

    cp_tok.wait()
    make_qkv(t)
    mod2 = mod_part(first_cols, z.mod, 1, cp_wm2)
    line_rest(r.tok, r.s_tok, r.r_tok, make_qkv)

    cp_cot.wait()
    for k in range(1, nt):
        to = (t + k) % nt
        remote(r.cot_in, slot(r.cot, t), r.s_cot.at[0, to], r.s_cot.at[1, t], tp=to).start()
    mod_take(first_cols, z.mod, mod2)
    for i in range(3, 6):
        cp_w[i].wait()
        send_w[i].wait_recv()

    eye = (lanes_of((WIN, WIN), 0) == lanes_of((WIN, WIN))).astype(BF16)

    def head_of(x, h, off=0):
        lane = lanes_of(x.shape)
        lo = off + h * HEAD_DIM
        return jnp.where((lane >= lo) & (lane < lo + HEAD_DIM), x, jnp.zeros_like(x))

    def attend_seq(s):
        r.stat[0] = jnp.full((8, block), NEG, F32)
        r.stat[1] = jnp.zeros((8, block), F32)
        r.acc[...] = jnp.zeros((hw, block), F32)
        q = r.q[s]

        def one_block(back):
            j = c - back

            @pl.when((back > 0) & (s == 0))
            def _():
                def take(idx):
                    there = r.kv.at[j, :, span(idx), :]
                    remote(there, there, r.s_kv.at[j, idx], r.r_kv.at[j, idx], ctx=j).wait_recv()

                each(nt, take)

            keys = r.kv[j, s, :, 0:WIN]
            r.vt[...] = mm(eye, r.kv[j, s, :, z.vlo : z.vlo + WIN], NT).astype(BF16)
            for h in range(z.heads):
                scores = mm(keys, head_of(q, h), NT)
                old = r.stat[0, h : h + 1, :]
                top = jnp.maximum(old, jnp.max(scores, axis=0, keepdims=True))
                prob = jnp.exp(scores - top)
                fade = jnp.exp(old - top)
                r.stat[0, h : h + 1, :] = top
                r.stat[1, h : h + 1, :] = r.stat[1, h : h + 1, :] * fade + jnp.sum(
                    prob, axis=0, keepdims=True
                )
                lo = h * HEAD_DIM
                vt = r.vt[z.voff + lo : z.voff + lo + HEAD_DIM, :]
                r.acc[lo : lo + HEAD_DIM, :] = r.acc[lo : lo + HEAD_DIM, :] * fade + mm(
                    vt, prob.astype(BF16)
                )

        each(c + 1, one_block)
        for h in range(z.heads):
            lo = h * HEAD_DIM
            denom = r.stat[1, h : h + 1, :]
            r.lse[s, h : h + 1, :] = r.stat[0, h : h + 1, :] + jnp.log(denom)
            r.att[s, lo : lo + HEAD_DIM, :] = r.acc[lo : lo + HEAD_DIM, :] / denom
        low = jnp.transpose(r.att[s]).astype(BF16)
        r.attl[s, :, 0:hw] = low
        r.attl[s, :, hw:WIN] = jnp.zeros((block, WIN - hw), BF16)
        r.part[s] = mm(low, r.wot[z.voff : z.voff + hw, :]).astype(BF16)
        for k in range(1, nt):
            to = (t + k) % nt
            remote(
                r.part.at[s, span(to), :], r.br_r.at[t, s], r.s_br.at[s, to], r.r_br.at[s, t], tp=to
            ).start()

    each(seqs, attend_seq)

    for s in range(seqs):
        for k in range(1, nt):
            fr = (t + k) % nt
            remote(
                r.br_r.at[fr, s], r.br_r.at[fr, s], r.s_br.at[s, fr], r.r_br.at[s, fr], tp=fr
            ).wait_recv()
    branch = summed(r.part, r.br_r)
    r.branch[...] = branch
    middle = r.tok[:, span(t), :].astype(F32) + vec(2) * branch
    r.middle[...] = middle
    unit, _ = norm_parts(middle)
    r.n2[:, span(t), :] = (unit * (1.0 + vec(4)) + vec(3)).astype(BF16)
    line_open(slot(r.n2, t), r.n2, r.s_n2, r.r_n2)

    for k in range(1, nt):
        fr = (t + k) % nt
        there = slot(r.cot, fr)
        remote(there, there, r.s_cot.at[0, fr], r.s_cot.at[1, fr], tp=fr).wait_recv()

    def feed(idx):
        at = span(idx)
        hid = mm(flat(r.n2[:, at, :]), r.wu[...])
        square = hid * hid
        tanh = jnp.tanh(GELU_C * (hid + GELU_A * (hid * square)))
        r.act[:, at, :] = (0.5 * hid * (1.0 + tanh)).astype(BF16).reshape(seqs, rows, z.ff)
        slope = 0.5 * (1.0 + tanh) + 0.5 * hid * (1.0 - tanh * tanh) * (
            GELU_C * (1.0 + 3.0 * GELU_A * square)
        )
        low = (vec(5) * r.cot[:, at, :].astype(F32)).astype(BF16)
        r.mgrad[:, at, :] = low
        hgrad = (slope * mm(flat(low), r.wd[...])).astype(BF16)
        r.hgrad[:, at, :] = hgrad.reshape(seqs, rows, z.ff)
        r.g2p[:, at, :] = mm(hgrad, r.wu[...], NT).astype(BF16).reshape(seqs, rows, width)

    def feed_push(idx):
        feed(idx)
        push(lambda i: slot(r.g2p, i), r.g2_r, r.s_g2, idx)

    feed(t)
    line_rest(r.n2, r.s_n2, r.r_n2, feed_push)

    def mlp_rows(idx):
        at = span(idx)
        r.mlp[:, at, :] = (
            mm(flat(r.act[:, at, :]), r.wd[...], NT).astype(BF16).reshape(seqs, rows, width)
        )

    def mlp_push(k):
        idx = (t + k) % nt
        mlp_rows(idx)
        push(lambda i: slot(r.mlp, i), r.ml_r, r.s_ml, idx)

    each(nt, mlp_push, 1)
    mlp_rows(t)

    r.msum[...] = jnp.zeros((8, z.mod), F32)

    def keep_sum(slot_idx, value):
        lo = slot_idx * width
        r.msum[0:seqs, lo : lo + width] = jnp.sum(value, axis=1)

    for k in range(1, nt):
        pull(r.g2_r, r.s_g2, (t + k) % nt)
    grad2 = summed(r.g2p, r.g2_r)
    unit, rstd = norm_parts(r.middle[...])
    keep_sum(3, grad2)
    keep_sum(4, grad2 * unit)
    mid_grad = r.cot[:, span(t), :].astype(F32) + norm_back(grad2, unit, rstd, vec(4))
    r.midg[...] = mid_grad
    keep_sum(2, mid_grad * r.branch[...])
    r.bg[:, span(t), :] = (vec(2) * mid_grad).astype(BF16)
    line_open(slot(r.bg, t), r.bg, r.s_bg, r.r_bg)

    def pair_grads(lhs, rhs, mine, sent, lo, hi):
        right = flat(rhs[...])
        for which, dst in ((other, sent), (d, mine)):
            cols = pl.ds(pl.multiple_of(which * half, half), half)
            left = flat(lhs[:, :, cols])
            dst[:, lo:hi] = mm(left, right, TN).astype(BF16)

    pair_grads(r.mgrad, r.act, r.ga_o, r.ga_s, z.ff, 2 * z.ff)
    pair_grads(r.n2, r.hgrad, r.ga_o, r.ga_s, 0, z.ff)
    send_ga = remote(r.ga_s, r.ga_r, r.s_ga.at[0], r.s_ga.at[1], dp=other)
    send_ga.start()

    def out_grads(idx):
        at = span(idx)
        r.do[:, at, :] = (
            mm(flat(r.bg[:, at, :]), r.wot[...], NT).astype(BF16).reshape(seqs, rows, WIN)
        )

    out_grads(t)
    line_rest(r.bg, r.s_bg, r.r_bg, out_grads)

    class Reduction:
        def __init__(self, got, mine, theirs, buf, total, sems, sems_all):
            self.got, self.mine, self.theirs, self.buf, self.total = got, mine, theirs, buf, total
            self.sems, self.sems_all = sems, sems_all
            self.chunk = buf.shape[1]
            self.owners = mine.shape[0] // self.chunk

        def rows(self, o):
            return pl.ds(pl.multiple_of(o * self.chunk, 16), self.chunk)

        def part(self, o):
            return remote(
                self.mine.at[self.rows(o), :],
                self.buf.at[c],
                self.sems.at[0, o],
                self.sems.at[1, c],
                ctx=o,
            )

        def share(self, owner, to):
            here = self.total.at[self.rows(owner), :]
            return remote(here, here, self.sems_all.at[0, to], self.sems_all.at[1, owner], ctx=to)

        def to_owners(self, body):
            def one(k):
                o = (c + k) % nc

                @pl.when(o < self.owners)
                def _():
                    body(o)

            each(nc, one, 1)

        def as_owner(self, body):
            @pl.when(c < self.owners)
            def _():
                body()

        def send(self):
            self.got.wait()
            self.mine[...] = (self.mine[...].astype(F32) + self.theirs[...].astype(F32)).astype(
                BF16
            )
            self.to_owners(lambda o: self.part(o).start())

        def sum(self):
            def body():
                def add(k, acc):
                    fr = (c + k) % nc
                    there = self.buf.at[fr]
                    remote(
                        there, there, self.sems.at[0, fr], self.sems.at[1, fr], ctx=fr
                    ).wait_recv()
                    return acc + self.buf[fr].astype(F32)

                acc = self.mine[self.rows(c), :].astype(F32)
                if nc <= 4:
                    for k in range(1, nc):
                        acc = add(k, acc)
                else:
                    acc = lax.fori_loop(1, nc, add, acc)
                self.total[self.rows(c), :] = acc.astype(BF16)
                each(nc, lambda k: self.share(c, (c + k) % nc).start(), 1)

            self.as_owner(body)

        def take(self):
            def one(o):
                self.share(o, o).wait_recv()
                self.part(o).wait_send()

            self.to_owners(one)
            self.as_owner(
                lambda: each(nc, lambda k: self.share(c, (c + k) % nc).wait_send(), 1)
            )

    red_a = Reduction(send_ga, r.ga_o, r.ga_r, r.ga_c, r.ga_t, r.s_gac, r.s_gag)
    red_a.send()

    def back_seq(s):
        do = r.do[s]
        r.dot[...] = mm(eye, do, NT).astype(BF16)
        for h in range(z.heads):
            lo = h * HEAD_DIM
            r.delta[s, h : h + 1, :] = jnp.sum(
                r.dot[z.voff + lo : z.voff + lo + HEAD_DIM, :].astype(F32)
                * r.att[s, lo : lo + HEAD_DIM, :],
                axis=0,
                keepdims=True,
            )
        r.dqt[...] = jnp.zeros((hw, block), F32)
        q = r.q[s]

        def one_block(j):
            keys = r.kv[j, s, :, 0:WIN]
            vals = r.kv[j, s, :, z.vlo : z.vlo + WIN]
            r.vt[...] = mm(eye, keys, NT).astype(BF16)
            dk = jnp.zeros((block, WIN), F32)
            dv = jnp.zeros((block, WIN), F32)
            for h in range(z.heads):
                lo = h * HEAD_DIM
                qh = head_of(q, h)
                doh = head_of(do, h, z.voff)
                prob = jnp.exp(mm(keys, qh, NT) - r.lse[s, h : h + 1, :])
                dprob = mm(vals, doh, NT)
                dsc = (prob * (dprob - r.delta[s, h : h + 1, :])).astype(BF16)
                dv = dv + mm(prob.astype(BF16), doh)
                dk = dk + mm(dsc, qh)
                r.dqt[lo : lo + HEAD_DIM, :] += mm(r.vt[lo : lo + HEAD_DIM, :], dsc)
            over = WIN - z.vlo
            pieces = (
                (0, z.vlo, dk[:, 0 : z.vlo]),
                (z.vlo, WIN, dk[:, z.vlo : WIN] + dv[:, 0:over]),
                (WIN, z.kvw, dv[:, over:WIN]),
            )

            @pl.when(j < c)
            def _():
                for lo, hi, piece in pieces:
                    r.kv[j, s, :, lo:hi] = piece.astype(BF16)
                remote(
                    r.kv.at[j, s], r.dkv_r.at[c, s], r.s_dk.at[j, s], r.r_dk.at[c, s], ctx=j
                ).start()

            @pl.when(j == c)
            def _():
                for lo, hi, piece in pieces:
                    r.dkv[s, :, lo:hi] = piece

        each(c + 1, one_block)
        r.dq[s, :, 0:hw] = jnp.transpose(r.dqt[...]) * (HEAD_DIM ** -0.5)
        r.dq[s, :, hw:WIN] = jnp.zeros((block, WIN - hw), F32)

    def kv_sent(j):
        def one(idx):
            mine = r.kv.at[c, :, span(idx), :]
            remote(mine, mine, r.s_kv.at[j, idx], r.r_kv.at[c, idx], ctx=j).wait_send()

        each(nt, one)

    each(nc, kv_sent, c + 1)
    each(seqs, back_seq)

    def add_dkv(j):
        for s in range(seqs):
            there = r.dkv_r.at[j, s]
            remote(there, there, r.s_dk.at[j, s], r.r_dk.at[j, s], ctx=j).wait_recv()
        r.dkv[...] += r.dkv_r[j].astype(F32)

    each(nc, add_dkv, c + 1)

    cos1, sin1 = r.cosine[...], r.sine[...]
    for s in range(seqs):
        for j in range(WIN // LANES):
            x = r.dq[s, :, j * LANES : (j + 1) * LANES]
            r.qb[s, :, j * LANES : (j + 1) * LANES] = (x * cos1 - swap(x) * sin1).astype(BF16)
        for j in range(z.kvw // LANES):
            x = r.dkv[s, :, j * LANES : (j + 1) * LANES]
            keys = min(max(hw - j * LANES, 0), LANES)
            if keys > 0:
                turned = x * cos1 - swap(x) * sin1
                x = turned if keys == LANES else jnp.where(lanes_of(x.shape) < keys, turned, x)
            r.kvb[s, :, j * LANES : (j + 1) * LANES] = x.astype(BF16)

    def n1_rows(idx):
        at = span(idx)
        r.g2p[:, at, :] = (
            (
                mm(flat(r.qb[:, at, :]), r.wqt[...])
                + mm(flat(r.kvb[:, at, :]), r.wkvt[...])
            )
            .astype(BF16)
            .reshape(seqs, rows, width)
        )

    def n1_push(k):
        idx = (t + k) % nt
        n1_rows(idx)
        push(lambda i: slot(r.g2p, i), r.n1_r, r.s_n1, idx)

    push_done(lambda i: slot(r.g2p, i), r.g2_r, r.s_g2)
    each(nt, n1_push, 1)
    n1_rows(t)

    for which, dst in ((other, r.gb_s), (d, r.gb_o)):
        cols = pl.ds(pl.multiple_of(which * half, LANES), half)
        right = flat(r.nrm[:, :, cols])
        dst[0:hw, :] = mm(flat(r.qb[:, :, 0:hw]), right, TN).astype(BF16)
        dst[hw : 3 * hw, :] = mm(flat(r.kvb[...]), right, TN).astype(BF16)
        right = flat(r.bg[:, :, cols])
        dst[3 * hw : 4 * hw, :] = mm(flat(r.attl[:, :, 0:hw]), right, TN).astype(BF16)
    send_gb = remote(r.gb_s, r.gb_r, r.s_gb.at[0], r.s_gb.at[1], dp=other)
    send_gb.start()
    red_a.sum()

    for k in range(1, nt):
        pull(r.ml_r, r.s_ml, (t + k) % nt)
    mlp = summed(r.mlp, r.ml_r)
    r.res[...] = (r.middle[...] + vec(5) * mlp).astype(BF16)
    keep_sum(5, r.cot[:, span(t), :].astype(F32) * mlp)
    outs = []

    def store(src, dst):
        cp = pltpu.make_async_copy(src, dst, r.s_loc.at[len(local) + len(outs)])
        cp.start()
        outs.append(cp)

    store(r.res, r.res_out)
    red_b = Reduction(send_gb, r.gb_o, r.gb_r, r.gb_c, r.gb_t, r.s_gbc, r.s_gbg)
    red_b.send()

    for k in range(1, nt):
        pull(r.n1_r, r.s_n1, (t + k) % nt)
    grad1 = summed(r.g2p, r.n1_r)
    unit, rstd = norm_parts(r.tok[:, span(t), :].astype(F32))
    keep_sum(0, grad1)
    keep_sum(1, grad1 * unit)

    def mcol(idx):
        return pl.ds(pl.multiple_of(idx * z.mcols, LANES), z.mcols)

    for k in range(1, nt):
        to = (t + k) % nt
        remote(
            r.msum.at[:, mcol(to)], r.mt_r.at[t], r.s_mt.at[0, to], r.s_mt.at[1, t], tp=to
        ).start()
    r.gtok[...] = r.midg[...] + norm_back(grad1, unit, rstd, vec(1))
    store(r.gtok, r.gtok_out)
    red_b.sum()
    total = r.msum[:, mcol(t)]
    for k in range(1, nt):
        fr = (t + k) % nt
        pull(r.mt_r, r.s_mt, fr)
        total = total + r.mt_r[fr]
    r.md_s[...] = total
    send_md = remote(r.md_s, r.md_r, r.s_md.at[0], r.s_md.at[1], dp=other)
    send_md.start()
    send_md.wait()
    r.mg[pl.ds(c, 1), 0:2, :] = total[None, 0:2, :]
    r.mg[pl.ds(c, 1), 2:4, :] = r.md_r[0:2, :][None]
    r.mg[pl.ds(c, 1), 4:8, :] = jnp.zeros((1, 4, z.mcols), F32)

    def send_mg(k):
        to = (c + k) % nc
        remote(r.mg.at[c], r.mg.at[c], r.s_mc.at[0, to], r.s_mc.at[1, c], ctx=to).start()

    each(nc, send_mg, 1)
    red_a.take()
    store(r.ga_t, r.ga_out)
    red_b.take()
    store(r.gb_t, r.gb_out)

    def take_small(k):
        fr = (c + k) % nc
        for buf, sems in ((r.mg, r.s_mc), (r.emb, r.s_ec)):
            remote(buf.at[fr], buf.at[fr], sems.at[0, fr], sems.at[1, fr], ctx=fr).wait_recv()
            remote(buf.at[c], buf.at[c], sems.at[0, fr], sems.at[1, c], ctx=fr).wait_send()

    each(nc, take_small, 1)
    store(r.mg, r.mg_out)
    store(r.emb, r.emb_out)

    for cp in send_w:
        cp.wait_send()
    line_close(r.tok, r.s_tok, r.r_tok)
    line_close(r.n2, r.s_n2, r.r_n2)
    line_close(r.bg, r.s_bg, r.r_bg)
    for k in range(1, nt):
        to = (t + k) % nt
        remote(r.cot_in, slot(r.cot, t), r.s_cot.at[0, to], r.s_cot.at[1, t], tp=to).wait_send()
        for s in range(seqs):
            remote(
                r.part.at[s, span(to), :], r.br_r.at[t, s], r.s_br.at[s, to], r.r_br.at[s, t], tp=to
            ).wait_send()
        remote(
            r.msum.at[:, mcol(to)], r.mt_r.at[t], r.s_mt.at[0, to], r.s_mt.at[1, t], tp=to
        ).wait_send()
    push_done(lambda i: slot(r.mlp, i), r.ml_r, r.s_ml)
    push_done(lambda i: slot(r.g2p, i), r.n1_r, r.s_n1)

    def dkv_sent(j):
        for s in range(seqs):
            remote(
                r.kv.at[j, s], r.dkv_r.at[c, s], r.s_dk.at[j, s], r.r_dk.at[c, s], ctx=j
            ).wait_send()

    each(c, dkv_sent)
    for cp in outs:
        cp.wait()


def finish_kernel(z, ga, gb, emb, mg, res, gtok, *outs):
    res_o, gtok_o, gq, gk, gv, go, gu, gd, gm = outs
    hw = z.hw
    res_o[...] = res[...]
    gtok_o[...] = gtok[...]
    for i, out in enumerate((gq, gk, gv, go)):
        out[...] = gb[i * hw : (i + 1) * hw, :].astype(F32)
    gu[...] = ga[:, 0 : z.ff].astype(F32)
    gd[...] = ga[:, z.ff : 2 * z.ff].astype(F32)
    e = emb[...].reshape(z.nc * 8, z.half)
    m = mg[...].reshape(z.nc * 8, z.mcols)
    gm[...] = lax.dot_general(e, m, TN, precision=lax.Precision.HIGHEST, preferred_element_type=F32)


IN_NAMES = (
    "tok_in",
    "ts_in",
    "wq_in",
    "wk_in",
    "wv_in",
    "wo_in",
    "wu_in",
    "wd_in",
    "wm_in",
    "cot_in",
    "rate_in",
    "rope_in",
)
OUT_NAMES = ("res_out", "gtok_out", "ga_out", "gb_out", "emb_out", "mg_out")


def solution(mesh):
    def shards(tokens, steps, wq, wk, wv, wo, wu, wd, wm, cot):
        wq, wk, wv, wo = wq.T, wk.T, wv.T, wo.T
        z = Dims(mesh, tokens.shape, wq.shape, wu.shape, wm.shape)
        half_dim = z.width // 2
        rate = jnp.exp(jnp.arange(half_dim, dtype=F32) * (-math.log(10000.0) / half_dim))
        rope = jnp.exp(
            jnp.arange(HEAD_DIM // 2, dtype=F32) * (-2.0 * math.log(10000.0) / HEAD_DIM)
        )
        rope = jnp.tile(rope, LANES // (HEAD_DIM // 2))
        table = scratch_table(z)
        names = list(IN_NAMES) + list(OUT_NAMES) + list(table)
        hbm = pl.BlockSpec(memory_space=pl.ANY)
        vmem = pl.BlockSpec(memory_space=pltpu.VMEM)
        smem = pl.BlockSpec(memory_space=pltpu.SMEM)
        own = (z.seqs, z.rows, z.width)
        shape = jax.ShapeDtypeStruct
        outs = pl.pallas_call(
            functools.partial(layer_kernel, z, names),
            out_shape=(
                shape(own, BF16),
                shape(own, F32),
                shape((z.half, z.wide), BF16),
                shape((z.heads_rows, z.half), BF16),
                shape((z.nc, 8, z.half), F32),
                shape((z.nc, 8, z.mcols), F32),
            ),
            in_specs=[hbm, smem] + [hbm] * 8 + [vmem, vmem],
            out_specs=[hbm] * 6,
            scratch_shapes=list(table.values()),
            compiler_params=pltpu.CompilerParams(
                collective_id=0, has_side_effects=True, vmem_limit_bytes=VMEM_BYTES
            ),
            name="layer",
        )(tokens, steps, wq, wk, wv, wo, wu, wd, wm, cot, rate[None], rope[None])
        res, gtok, ga, gb, emb, mg = outs
        done = pl.pallas_call(
            functools.partial(finish_kernel, z),
            out_shape=(
                shape(own, BF16),
                shape(own, F32),
                shape((z.hw, z.half), F32),
                shape((z.hw, z.half), F32),
                shape((z.hw, z.half), F32),
                shape((z.hw, z.half), F32),
                shape((z.half, z.ff), F32),
                shape((z.half, z.ff), F32),
                shape((z.half, z.mcols), F32),
            ),
            in_specs=[vmem] * 6,
            out_specs=[vmem] * 9,
            compiler_params=pltpu.CompilerParams(vmem_limit_bytes=VMEM_BYTES),
            name="finish",
        )(ga, gb, emb, mg, res, gtok)
        return done[:2] + tuple(g.T for g in done[2:6]) + done[6:]

    rows = P("dp", ("ctx", "tp"), None)
    cols = P("dp", "tp")
    return jax.shard_map(
        shards,
        mesh=mesh,
        in_specs=(rows, P("dp", "ctx")) + (cols,) * 6 + (P("dp", None), rows),
        out_specs=(rows, rows) + (cols,) * 7,
        check_vma=False,
    )
```

time: 548 us -> 190 us (0.35)
  waiting for transfers between devices: 193 us -> 0 us
  Pallas kernels: 0 us -> 187 us
  blocking collectives: 182 us -> 0 us
  matrix products: 78.2 us -> 0 us
  local copies, waits for them, and re-layouts: 49.8 us -> 1.9 us
  other arithmetic: 18.6 us -> 0.59 us
  between operations: 15.4 us -> 0.66 us
  loops' own time: 8.35 us -> 0 us
    pallas_call x0 -> x2, Pallas kernels: none -> 187 us  [the longest x1 181 us: shards(): pl.pallas_call(functools.partial(layer_kernel, z, names), out_shape=(shap...]
    all_gather x14 -> x0, blocking collectives: 164 us -> none  [the longest x4 82.2 us: gather_rows(): return lax.all_gather(row_data, 'tp', axis=1, tiled=True)]
    psum x1 -> x0, waiting for transfers between devices: 147 us -> none  [shards(): lax.psum((grad_query, grad_key, grad_value, grad_out, grad_up, grad_down,...]
    dot_general x48 -> x0, matrix products: 78.2 us -> none  [the longest x4 11.2 us: query_one_block(): jnp.einsum('shqk,skhd->sqhd', score_grad, key_blk, preferred_element_type...]
    reduce_scatter x4 -> x0, waiting for transfers between devices: 32.5 us -> none  [share_sums(): lax.psum_scatter(row_data.astype(jnp.bfloat16), 'tp', scatter_dimension=1...]
    dynamic_slice x31 -> x0, local copies, waits for them, and re-layouts: 26.8 us -> none  [the longest x12 12.7 us: shards(): lax.scan(forward_one_block, carried, (key_blocks, value_blocks, block_ord...]
    psum x1 -> x0, blocking collectives: 17.5 us -> none  [shards(): lax.psum(modulation_grad.astype(jnp.bfloat16), 'tp').astype(jnp.float32)]
    all_gather x3 -> x0, waiting for transfers between devices: 11.7 us -> none  [the longest x1 11.6 us: shards(): lax.all_gather(modulation_weight, 'dp', axis=0, tiled=True)]
  transfers between devices with their start and end apart: 8 -> 0, of which waited for: 4 -> 0; matrix products, arithmetic and copies ran while one was open for 10% -> 0% of each run, Pallas kernels for 0% -> 0%
where the time goes in v1:
time: 190 us
  Pallas kernels  187 us (98%)
    pallas_call x1, Pallas kernels, shards(): pl.pallas_call(functools.partial(layer_kernel, z, names), out_shape=(shap...  181 us
    pallas_call x1, Pallas kernels, shards(): pl.pallas_call(functools.partial(finish_kernel, z), out_shape=(shape(own,...  5.74 us

profile of v1, /device:TPU:0, one launch (start us, length us, event | category | flops | bytes accessed | tf_op | source)
XLA Modules:
  0.0 190.1 jit_solution(15276232370130272740)
XLA Ops:
  0.7 1.3 copy.19.refs_1_
  2.0 0.6 broadcast_in_dim_tile.3.refs_11_
  2.6 0.6 multiply_exponential_fusion.refs_10_
  3.1 181.2 %layer.1 = (bf16[2,64,768]{2,1,0:T(8,128)(2,1)}, f32[2,64,768]{2,1,0:T(8,128)}, bf16[384,1536]{1,0:T(8,128)(2,1)}, bf16[768,384]{1,0:T(8,128)(2,1)}, f32[4,8,384]{2,1,0:T(8,128)}, /*index=5*/f32[4,8,1152]{2,1,0:T(8,128)}) custom-call(bf16[2,64,768]{2,1,0:T(8,128)(2,1)} %refs_0_.1, s32[2,1]{1,0:T(2,128)} %copy.19.refs_1_, bf16[192,384]{1,0:T(8,128)(2,1)} %bitcast.8, ...), custom_call_target="tpu_custom_call" | custom-call | tf_op jit(solution)/shard_map/layer/pallas_call | solution.py:931
  184.3 5.7 %finish.1 = (bf16[2,64,768]{2,1,0:T(8,128)(2,1)}, f32[2,64,768]{2,1,0:T(8,128)}, f32[192,384]{1,0:T(8,128)}, f32[192,384]{1,0:T(8,128)}, f32[192,384]{1,0:T(8,12...) custom-call(bf16[384,1536]{1,0:T(8,128)(2,1)} %get-tuple-element.24.ga, ...), custom_call_target="tpu_custom_call" | custom-call | tf_op jit(solution)/shard_map/finish/pallas_call | solution.py:950
  (2 shorter events, 0.0 us)

commit v2 on v1

--- a/solution.py
+++ b/solution.py
@@ -77,7 +77,7 @@
     sem = lambda *shape: pltpu.SemaphoreType.DMA(shape)
     full = (z.seqs, z.block, z.width)
     own = (z.seqs, z.rows, z.width)
-    parts = (z.nt,) + own
+    pair = (z.seqs, 2, z.rows, z.width)
     return dict(
         tok=vm(full),
         cot=vm(full),
@@ -105,18 +105,21 @@
         attl=vm((z.seqs, z.block, WIN)),
         lse=vm((z.seqs, 8, z.block), F32),
         delta=vm((z.seqs, 8, z.block), F32),
-        part=vm(full),
-        br_r=vm(parts),
+        br=vm(full),
+        br_m=vm(pair),
+        br_r=vm(pair),
         branch=vm(own, F32),
         middle=vm(own, F32),
         n2=vm(full),
         act=vm((z.seqs, z.block, z.ff)),
         hgrad=vm((z.seqs, z.block, z.ff)),
         mgrad=vm(full),
-        g2p=vm(full),
-        g2_r=vm(parts),
-        mlp=vm(full),
-        ml_r=vm(parts),
+        g2=vm(full),
+        g2_m=vm(pair),
+        g2_r=vm(pair),
+        ml=vm(full),
+        ml_m=vm(pair),
+        ml_r=vm(pair),
         midg=vm(own, F32),
         bg=vm(full),
         do=vm((z.seqs, z.block, WIN)),
@@ -127,7 +130,8 @@
         dkv_r=vm((z.nc, z.seqs, z.block, z.kvw)),
         qb=vm((z.seqs, z.block, WIN)),
         kvb=vm((z.seqs, z.block, z.kvw)),
-        n1_r=vm(parts),
+        n1_m=vm(pair),
+        n1_r=vm(pair),
         ga_s=vm((z.half, z.wide)),
         ga_o=vm((z.half, z.wide)),
         ga_r=vm((z.half, z.wide)),
@@ -150,22 +154,30 @@
         s_e=sem(2),
         s_ec=sem(2, z.nc),
         s_m=sem(2, 2),
-        s_tok=sem(2, z.nt),
-        r_tok=sem(z.nt),
-        s_cot=sem(2, z.nt),
-        s_kv=sem(z.nc, z.nt),
-        r_kv=sem(z.nc, z.nt),
-        s_br=sem(z.seqs, z.nt),
-        r_br=sem(z.seqs, z.nt),
-        s_n2=sem(2, z.nt),
-        r_n2=sem(z.nt),
-        s_g2=sem(2, z.nt),
-        s_ml=sem(2, z.nt),
-        s_bg=sem(2, z.nt),
-        r_bg=sem(z.nt),
+        s_tok=sem(z.seqs, 4),
+        r_tok=sem(z.seqs, z.nt),
+        s_cot=sem(z.seqs, 4),
+        r_cot=sem(z.seqs, z.nt),
+        s_kv=sem(z.nc, z.seqs, z.nt),
+        r_kv=sem(z.nc, z.seqs, z.nt),
+        s_br=sem(z.seqs, 4),
+        m_br=sem(z.seqs, 2),
+        r_br=sem(z.seqs, 2),
+        s_n2=sem(z.seqs, 4),
+        r_n2=sem(z.seqs, z.nt),
+        s_g2=sem(z.seqs, 4),
+        m_g2=sem(z.seqs, 2),
+        r_g2=sem(z.seqs, 2),
+        s_ml=sem(z.seqs, 4),
+        m_ml=sem(z.seqs, 2),
+        r_ml=sem(z.seqs, 2),
+        s_bg=sem(z.seqs, 4),
+        r_bg=sem(z.seqs, z.nt),
         s_dk=sem(z.nc, z.seqs),
         r_dk=sem(z.nc, z.seqs),
-        s_n1=sem(2, z.nt),
+        s_n1=sem(z.seqs, 4),
+        m_n1=sem(z.seqs, 2),
+        r_n1=sem(z.seqs, 2),
         s_ga=sem(2),
         s_gac=sem(2, z.nc),
         s_gag=sem(2, z.nc),
@@ -203,6 +215,9 @@
 
     def slot(ref, idx):
         return ref.at[:, span(idx), :]
+
+    def piece(ref, s, idx):
+        return ref.at[s, span(idx), :]
 
     def flat(x):
         return x.reshape(x.shape[0] * x.shape[1], x.shape[2])
@@ -249,9 +264,11 @@
 
     row8 = lanes_of((8, half), 0)
     step_of = jnp.where(
-        row8 % 2 == 0, r.ts_in[0, 0].astype(F32), r.ts_in[1, 0].astype(F32)
+        row8 % 2 == 0, r.ts_in[0, 0].astype(F32), r.ts_in[0, 1].astype(F32)
     )
-    angle = step_of * r.rate_in[...]
+    angle = step_of * jnp.exp(
+        lanes_of((8, half)).astype(F32) * (-math.log(10000.0) / half)
+    )
     sin_e, cos_e = jnp.sin(angle), jnp.cos(angle)
 
     def silu_low(v):
@@ -265,71 +282,139 @@
     )
     pl.semaphore_wait(bar, 1 + (nt - 1) + (nc - 1))
 
-    def line_send(src, buf, send, recv, idx, side):
-        to = t + 1 - 2 * side
-
-        @pl.when((to >= 0) & (to < nt))
-        def _():
-            remote(src, slot(buf, idx), send.at[side, idx], recv.at[idx], tp=to).start()
-
-    def line_open(src, buf, send, recv):
-        line_send(src, buf, send, recv, t, 0)
-        line_send(src, buf, send, recv, t, 1)
-
-    def line_rest(buf, send, recv, work):
-        def far(dist):
-            def take(side):
-                idx = t + (2 * side - 1) * dist
-
-                @pl.when((idx >= 0) & (idx < nt))
+    side = t // 2
+    mate = t + 1 - 2 * (t % 2)
+    cross = 2 - side
+    outer = t % 3 == 0
+    inner = t % 3 != 0
+
+    def peer(i):
+        far = i // 2
+        return (1 - far) * (t + i * (1 - 2 * (t % 2))) + far * ((1 - side) * i + side * (3 - i))
+
+    class Gather:
+        def __init__(self, buf, send, recv):
+            self.buf, self.sems, self.recv = buf, send, recv
+
+        def copy(self, src, s, idx, k, to):
+            return remote(
+                src, piece(self.buf, s, idx), self.sems.at[s, k], self.recv.at[s, idx], tp=to
+            )
+
+        def open(self, src, s):
+            self.copy(src, s, t, 0, mate).start()
+            self.copy(src, s, t, 1, cross).start()
+
+        def wait(self, s, idx):
+            self.copy(piece(self.buf, s, idx), s, idx, 0, mate).wait_recv()
+
+        def relay(self, s):
+            @pl.when(inner)
+            def _():
+                def one(i):
+                    idx = peer(i)
+                    self.wait(s, idx)
+                    self.copy(piece(self.buf, s, idx), s, idx, i, mate).start()
+
+                each(4, one, 2)
+
+        def collect(self, s, work):
+            def one(i):
+                idx = peer(i)
+
+                @pl.when(outer | (i == 1))
                 def _():
-                    here = slot(buf, idx)
-                    remote(here, here, send.at[side, idx], recv.at[idx], tp=idx).wait_recv()
-                    line_send(here, buf, send, recv, idx, side)
-
-            def run(side):
-                idx = t + (2 * side - 1) * dist
-
-                @pl.when((idx >= 0) & (idx < nt))
-                def _():
-                    work(idx)
-
-            each(2, take)
-            each(2, run)
-
-        each(nt, far, 1)
-
-    def line_close(buf, send, recv):
-        def one(j):
-            idx, side = j // 2, j % 2
-            to = t + 1 - 2 * side
-            passed = ((1 - 2 * side) * (t - idx) >= 0) & (to >= 0) & (to < nt)
-
-            @pl.when(passed)
+                    self.wait(s, idx)
+
+                if work is not None:
+                    work(s, idx, i)
+
+            each(4, one, 1)
+
+        def close(self, s):
+            mine = piece(self.buf, s, t)
+            self.copy(mine, s, t, 0, mate).wait_send()
+            self.copy(mine, s, t, 1, cross).wait_send()
+
+            @pl.when(inner)
             def _():
-                here = slot(buf, idx)
-                remote(here, here, send.at[side, idx], recv.at[idx], tp=to).wait_send()
-
-        each(2 * nt, one)
-
-    def push(src_of, buf, sems, idx):
-        remote(src_of(idx), buf.at[t], sems.at[0, idx], sems.at[1, t], tp=idx).start()
-
-    def pull(buf, sems, idx):
-        remote(buf.at[idx], buf.at[idx], sems.at[0, idx], sems.at[1, idx], tp=idx).wait_recv()
-
-    def push_done(src_of, buf, sems):
-        for k in range(1, nt):
-            idx = (t + k) % nt
-            remote(src_of(idx), buf.at[t], sems.at[0, idx], sems.at[1, t], tp=idx).wait_send()
-
-    def summed(part, buf):
-        total = part[:, span(t), :].astype(F32)
-        for k in range(1, nt):
-            total = total + buf[(t + k) % nt].astype(F32)
-        return total
-
-    line_open(r.tok_in, r.tok, r.s_tok, r.r_tok)
+                each(4, lambda i: self.copy(mine, s, t, i, mate).wait_send(), 2)
+
+    class Scatter:
+        def __init__(self, part, merge, got, send, msem, gsem):
+            self.part, self.merge, self.got = part, merge, got
+            self.sems, self.msem, self.gsem = send, msem, gsem
+
+        def to_got(self, s, idx, i, k):
+            return remote(
+                piece(self.part, s, idx),
+                self.got.at[s, k],
+                self.sems.at[s, i],
+                self.gsem.at[s, k],
+                tp=idx,
+            )
+
+        def to_merge(self, s, idx, i):
+            return remote(
+                piece(self.part, s, idx),
+                self.merge.at[s, i - 2],
+                self.sems.at[s, i],
+                self.msem.at[s, i - 2],
+                tp=mate,
+            )
+
+        def push(self, s, idx, i):
+            @pl.when(i == 1)
+            def _():
+                self.to_got(s, idx, i, 0).start()
+
+            @pl.when((i > 1) & outer)
+            def _():
+                self.to_merge(s, idx, i).start()
+
+        def push_all(self, s):
+            for i in (3, 2):
+                self.push(s, peer(i), i)
+            self.push(s, mate, 1)
+
+        def join(self, s):
+            @pl.when(inner)
+            def _():
+                def one(k):
+                    i = 3 - k
+                    idx = peer(i)
+                    self.to_merge(s, idx, i).wait_recv()
+                    at = span(idx)
+                    self.part[s, at, :] = (
+                        self.part[s, at, :].astype(F32) + self.merge[s, i - 2].astype(F32)
+                    ).astype(BF16)
+                    self.to_got(s, idx, i, 1).start()
+
+                each(2, one)
+
+        def total(self, s):
+            for k in range(2):
+                self.to_got(s, mate, 1, k).wait_recv()
+            return (
+                self.part[s, span(t), :].astype(F32)
+                + self.got[s, 0].astype(F32)
+                + self.got[s, 1].astype(F32)
+            )
+
+        def close(self, s):
+            each(4, lambda i: self.to_got(s, mate, i, 0).wait_send(), 1)
+
+    toks = Gather(r.tok, r.s_tok, r.r_tok)
+    cots = Gather(r.cot, r.s_cot, r.r_cot)
+    n2s = Gather(r.n2, r.s_n2, r.r_n2)
+    bgs = Gather(r.bg, r.s_bg, r.r_bg)
+    brs = Scatter(r.br, r.br_m, r.br_r, r.s_br, r.m_br, r.r_br)
+    g2s = Scatter(r.g2, r.g2_m, r.g2_r, r.s_g2, r.m_g2, r.r_g2)
+    mls = Scatter(r.ml, r.ml_m, r.ml_r, r.s_ml, r.m_ml, r.r_ml)
+    n1s = Scatter(r.g2, r.n1_m, r.n1_r, r.s_n1, r.m_n1, r.r_n1)
+
+    for s in range(seqs):
+        toks.open(r.tok_in.at[s], s)
     send_emb = remote(r.emb_s, r.emb_r, r.s_e.at[0], r.s_e.at[1], dp=other)
     send_emb.start()
     send_w = [
@@ -358,9 +443,9 @@
         for s in range(seqs):
             r.mod[s : s + 1, lo:hi] = r.mod_s[s : s + 1, lo:hi] + r.mod_r[s + 2 : s + 3, lo:hi]
 
-    def vec(slot_idx):
+    def vec(slot_idx, s):
         lo = slot_idx * width
-        return r.mod[0:seqs, lo : lo + width][:, None, :]
+        return r.mod[s : s + 1, lo : lo + width]
 
     mod1 = mod_part(0, first_cols, 0, cp_wm1)
     for cp in send_w[3:]:
@@ -373,7 +458,8 @@
     each(nc, send_ctx_emb, 1)
 
     place = (c * block + lanes_of((block, LANES), 0)).astype(F32)
-    turn = place * r.rope_in[...]
+    pair_of = (lanes_of((block, LANES)) % (HEAD_DIM // 2)).astype(F32)
+    turn = place * jnp.exp(pair_of * (-2.0 * math.log(10000.0) / HEAD_DIM))
     low_lane = lanes_of((block, LANES)) % HEAD_DIM < HEAD_DIM // 2
     r.cosine[...] = jnp.cos(turn)
     r.sine[...] = jnp.where(low_lane, -jnp.sin(turn), jnp.sin(turn))
@@ -391,45 +477,44 @@
         send_w[i].wait_recv()
     mod_take(0, first_cols, mod1)
 
-    def make_qkv(idx):
+    def make_qkv(s, idx, i):
         at = span(idx)
-        unit, _ = norm_parts(r.tok[:, at, :].astype(F32))
-        low = (unit * (1.0 + vec(1)) + vec(0)).astype(BF16)
-        r.nrm[:, at, :] = low
-        low = flat(low)
+        unit, _ = norm_parts(r.tok[s, at, :].astype(F32))
+        low = (unit * (1.0 + vec(1, s)) + vec(0, s)).astype(BF16)
+        r.nrm[s, at, :] = low
         cos1, sin1 = r.cosine[at, :], r.sine[at, :]
-        cos2 = jnp.concatenate([cos1] * seqs, axis=0)
-        sin2 = jnp.concatenate([sin1] * seqs, axis=0)
         q_pre = mm(low, r.wqt[...], NT)
         kv_pre = mm(low, r.wkvt[...], NT)
-        shape = (seqs, rows, LANES)
         for j in range(WIN // LANES):
             x = q_pre[:, j * LANES : (j + 1) * LANES]
-            x = (x * cos2 + swap(x) * sin2) * (HEAD_DIM ** -0.5)
-            r.q[:, at, j * LANES : (j + 1) * LANES] = x.astype(BF16).reshape(shape)
+            x = (x * cos1 + swap(x) * sin1) * (HEAD_DIM ** -0.5)
+            r.q[s, at, j * LANES : (j + 1) * LANES] = x.astype(BF16)
         for j in range(z.kvw // LANES):
             x = kv_pre[:, j * LANES : (j + 1) * LANES]
             keys = min(max(hw - j * LANES, 0), LANES)
             if keys > 0:
-                turned = x * cos2 + swap(x) * sin2
+                turned = x * cos1 + swap(x) * sin1
                 x = turned if keys == LANES else jnp.where(lanes_of(x.shape) < keys, turned, x)
-            r.kv[c, :, at, j * LANES : (j + 1) * LANES] = x.astype(BF16).reshape(shape)
+            r.kv[c, s, at, j * LANES : (j + 1) * LANES] = x.astype(BF16)
 
         def send_kv(to):
-            mine = r.kv.at[c, :, at, :]
-            remote(mine, mine, r.s_kv.at[to, idx], r.r_kv.at[c, idx], ctx=to).start()
+            mine = r.kv.at[c, s, at, :]
+            remote(mine, mine, r.s_kv.at[to, s, idx], r.r_kv.at[c, s, idx], ctx=to).start()
 
         each(nc, send_kv, c + 1)
 
     cp_tok.wait()
-    make_qkv(t)
+    for s in range(seqs):
+        make_qkv(s, t, 0)
     mod2 = mod_part(first_cols, z.mod, 1, cp_wm2)
-    line_rest(r.tok, r.s_tok, r.r_tok, make_qkv)
-
+    for s in range(seqs):
+        toks.relay(s)
+        toks.collect(s, make_qkv)
+    for s in range(seqs):
+        toks.close(s)
     cp_cot.wait()
-    for k in range(1, nt):
-        to = (t + k) % nt
-        remote(r.cot_in, slot(r.cot, t), r.s_cot.at[0, to], r.s_cot.at[1, t], tp=to).start()
+    for s in range(seqs):
+        cots.open(r.cot_in.at[s], s)
     mod_take(first_cols, z.mod, mod2)
     for i in range(3, 6):
         cp_w[i].wait()
@@ -451,11 +536,13 @@
         def one_block(back):
             j = c - back
 
-            @pl.when((back > 0) & (s == 0))
+            @pl.when(back > 0)
             def _():
                 def take(idx):
-                    there = r.kv.at[j, :, span(idx), :]
-                    remote(there, there, r.s_kv.at[j, idx], r.r_kv.at[j, idx], ctx=j).wait_recv()
+                    there = r.kv.at[j, s, span(idx), :]
+                    remote(
+                        there, there, r.s_kv.at[j, s, idx], r.r_kv.at[j, s, idx], ctx=j
+                    ).wait_recv()
 
                 each(nt, take)
 
@@ -486,87 +573,47 @@
         low = jnp.transpose(r.att[s]).astype(BF16)
         r.attl[s, :, 0:hw] = low
         r.attl[s, :, hw:WIN] = jnp.zeros((block, WIN - hw), BF16)
-        r.part[s] = mm(low, r.wot[z.voff : z.voff + hw, :]).astype(BF16)
-        for k in range(1, nt):
-            to = (t + k) % nt
-            remote(
-                r.part.at[s, span(to), :], r.br_r.at[t, s], r.s_br.at[s, to], r.r_br.at[s, t], tp=to
-            ).start()
+        r.br[s] = mm(low, r.wot[z.voff : z.voff + hw, :]).astype(BF16)
+        brs.push_all(s)
 
     each(seqs, attend_seq)
-
-    for s in range(seqs):
-        for k in range(1, nt):
-            fr = (t + k) % nt
-            remote(
-                r.br_r.at[fr, s], r.br_r.at[fr, s], r.s_br.at[s, fr], r.r_br.at[s, fr], tp=fr
-            ).wait_recv()
-    branch = summed(r.part, r.br_r)
-    r.branch[...] = branch
-    middle = r.tok[:, span(t), :].astype(F32) + vec(2) * branch
-    r.middle[...] = middle
-    unit, _ = norm_parts(middle)
-    r.n2[:, span(t), :] = (unit * (1.0 + vec(4)) + vec(3)).astype(BF16)
-    line_open(slot(r.n2, t), r.n2, r.s_n2, r.r_n2)
-
-    for k in range(1, nt):
-        fr = (t + k) % nt
-        there = slot(r.cot, fr)
-        remote(there, there, r.s_cot.at[0, fr], r.s_cot.at[1, fr], tp=fr).wait_recv()
-
-    def feed(idx):
+    for s in range(seqs):
+        brs.join(s)
+    for s in range(seqs):
+        cots.relay(s)
+
+    for s in range(seqs):
+        branch = brs.total(s)
+        r.branch[s] = branch
+        middle = r.tok[s, span(t), :].astype(F32) + vec(2, s) * branch
+        r.middle[s] = middle
+        unit, _ = norm_parts(middle)
+        r.n2[s, span(t), :] = (unit * (1.0 + vec(4, s)) + vec(3, s)).astype(BF16)
+        n2s.open(piece(r.n2, s, t), s)
+
+    def feed(s, idx, i):
         at = span(idx)
-        hid = mm(flat(r.n2[:, at, :]), r.wu[...])
+        hid = mm(r.n2[s, at, :], r.wu[...])
         square = hid * hid
         tanh = jnp.tanh(GELU_C * (hid + GELU_A * (hid * square)))
-        r.act[:, at, :] = (0.5 * hid * (1.0 + tanh)).astype(BF16).reshape(seqs, rows, z.ff)
+        r.act[s, at, :] = (0.5 * hid * (1.0 + tanh)).astype(BF16)
         slope = 0.5 * (1.0 + tanh) + 0.5 * hid * (1.0 - tanh * tanh) * (
             GELU_C * (1.0 + 3.0 * GELU_A * square)
         )
-        low = (vec(5) * r.cot[:, at, :].astype(F32)).astype(BF16)
-        r.mgrad[:, at, :] = low
-        hgrad = (slope * mm(flat(low), r.wd[...])).astype(BF16)
-        r.hgrad[:, at, :] = hgrad.reshape(seqs, rows, z.ff)
-        r.g2p[:, at, :] = mm(hgrad, r.wu[...], NT).astype(BF16).reshape(seqs, rows, width)
-
-    def feed_push(idx):
-        feed(idx)
-        push(lambda i: slot(r.g2p, i), r.g2_r, r.s_g2, idx)
-
-    feed(t)
-    line_rest(r.n2, r.s_n2, r.r_n2, feed_push)
-
-    def mlp_rows(idx):
-        at = span(idx)
-        r.mlp[:, at, :] = (
-            mm(flat(r.act[:, at, :]), r.wd[...], NT).astype(BF16).reshape(seqs, rows, width)
-        )
-
-    def mlp_push(k):
-        idx = (t + k) % nt
-        mlp_rows(idx)
-        push(lambda i: slot(r.mlp, i), r.ml_r, r.s_ml, idx)
-
-    each(nt, mlp_push, 1)
-    mlp_rows(t)
-
-    r.msum[...] = jnp.zeros((8, z.mod), F32)
-
-    def keep_sum(slot_idx, value):
-        lo = slot_idx * width
-        r.msum[0:seqs, lo : lo + width] = jnp.sum(value, axis=1)
-
-    for k in range(1, nt):
-        pull(r.g2_r, r.s_g2, (t + k) % nt)
-    grad2 = summed(r.g2p, r.g2_r)
-    unit, rstd = norm_parts(r.middle[...])
-    keep_sum(3, grad2)
-    keep_sum(4, grad2 * unit)
-    mid_grad = r.cot[:, span(t), :].astype(F32) + norm_back(grad2, unit, rstd, vec(4))
-    r.midg[...] = mid_grad
-    keep_sum(2, mid_grad * r.branch[...])
-    r.bg[:, span(t), :] = (vec(2) * mid_grad).astype(BF16)
-    line_open(slot(r.bg, t), r.bg, r.s_bg, r.r_bg)
+        low = (vec(5, s) * r.cot[s, at, :].astype(F32)).astype(BF16)
+        r.mgrad[s, at, :] = low
+        hgrad = (slope * mm(low, r.wd[...])).astype(BF16)
+        r.hgrad[s, at, :] = hgrad
+        r.g2[s, at, :] = mm(hgrad, r.wu[...], NT).astype(BF16)
+        g2s.push(s, idx, i)
+
+    for s in range(seqs):
+        feed(s, t, 0)
+    for s in range(seqs):
+        cots.collect(s, None)
+        n2s.relay(s)
+        n2s.collect(s, feed)
+    g2s.join(0)
 
     def pair_grads(lhs, rhs, mine, sent, lo, hi):
         right = flat(rhs[...])
@@ -579,15 +626,35 @@
     pair_grads(r.n2, r.hgrad, r.ga_o, r.ga_s, 0, z.ff)
     send_ga = remote(r.ga_s, r.ga_r, r.s_ga.at[0], r.s_ga.at[1], dp=other)
     send_ga.start()
-
-    def out_grads(idx):
+    g2s.join(1)
+    for s in range(seqs):
+        r.ml[s] = mm(r.act[s], r.wd[...], NT).astype(BF16)
+
+    r.msum[...] = jnp.zeros((8, z.mod), F32)
+
+    def keep_sum(slot_idx, s, value):
+        lo = slot_idx * width
+        r.msum[s : s + 1, lo : lo + width] = jnp.sum(value, axis=0, keepdims=True)
+
+    for s in range(seqs):
+        grad2 = g2s.total(s)
+        unit, rstd = norm_parts(r.middle[s])
+        mid_grad = r.cot[s, span(t), :].astype(F32) + norm_back(grad2, unit, rstd, vec(4, s))
+        r.midg[s] = mid_grad
+        r.bg[s, span(t), :] = (vec(2, s) * mid_grad).astype(BF16)
+        bgs.open(piece(r.bg, s, t), s)
+        keep_sum(3, s, grad2)
+        keep_sum(4, s, grad2 * unit)
+        keep_sum(2, s, mid_grad * r.branch[s])
+
+    def out_grads(s, idx, i):
         at = span(idx)
-        r.do[:, at, :] = (
-            mm(flat(r.bg[:, at, :]), r.wot[...], NT).astype(BF16).reshape(seqs, rows, WIN)
-        )
-
-    out_grads(t)
-    line_rest(r.bg, r.s_bg, r.r_bg, out_grads)
+        r.do[s, at, :] = mm(r.bg[s, at, :], r.wot[...], NT).astype(BF16)
+
+    for s in range(seqs):
+        out_grads(s, t, 0)
+    bgs.relay(0)
+    bgs.collect(0, out_grads)
 
     class Reduction:
         def __init__(self, got, mine, theirs, buf, total, sems, sems_all):
@@ -667,6 +734,7 @@
 
     red_a = Reduction(send_ga, r.ga_o, r.ga_r, r.ga_c, r.ga_t, r.s_gac, r.s_gag)
     red_a.send()
+    bgs.relay(1)
 
     def back_seq(s):
         do = r.do[s]
@@ -723,25 +791,42 @@
         r.dq[s, :, hw:WIN] = jnp.zeros((block, WIN - hw), F32)
 
     def kv_sent(j):
-        def one(idx):
-            mine = r.kv.at[c, :, span(idx), :]
-            remote(mine, mine, r.s_kv.at[j, idx], r.r_kv.at[c, idx], ctx=j).wait_send()
-
-        each(nt, one)
+        for s in range(seqs):
+            each(
+                nt,
+                lambda idx: remote(
+                    r.kv.at[c, s, span(idx), :],
+                    r.kv.at[c, s, span(idx), :],
+                    r.s_kv.at[j, s, idx],
+                    r.r_kv.at[c, s, idx],
+                    ctx=j,
+                ).wait_send(),
+            )
 
     each(nc, kv_sent, c + 1)
-    each(seqs, back_seq)
-
-    def add_dkv(j):
-        for s in range(seqs):
+
+    def back_step(s):
+        @pl.when(s == 1)
+        def _():
+            bgs.collect(1, out_grads)
+            for i in range(seqs):
+                mls.push_all(i)
+
+        back_seq(s)
+
+    each(seqs, back_step)
+
+    for s in range(seqs):
+        g2s.close(s)
+    cos1, sin1 = r.cosine[...], r.sine[...]
+    for s in range(seqs):
+
+        def add_dkv(j):
             there = r.dkv_r.at[j, s]
             remote(there, there, r.s_dk.at[j, s], r.r_dk.at[j, s], ctx=j).wait_recv()
-        r.dkv[...] += r.dkv_r[j].astype(F32)
-
-    each(nc, add_dkv, c + 1)
-
-    cos1, sin1 = r.cosine[...], r.sine[...]
-    for s in range(seqs):
+            r.dkv[s] += r.dkv_r[j, s].astype(F32)
+
+        each(nc, add_dkv, c + 1)
         for j in range(WIN // LANES):
             x = r.dq[s, :, j * LANES : (j + 1) * LANES]
             r.qb[s, :, j * LANES : (j + 1) * LANES] = (x * cos1 - swap(x) * sin1).astype(BF16)
@@ -752,26 +837,8 @@
                 turned = x * cos1 - swap(x) * sin1
                 x = turned if keys == LANES else jnp.where(lanes_of(x.shape) < keys, turned, x)
             r.kvb[s, :, j * LANES : (j + 1) * LANES] = x.astype(BF16)
-
-    def n1_rows(idx):
-        at = span(idx)
-        r.g2p[:, at, :] = (
-            (
-                mm(flat(r.qb[:, at, :]), r.wqt[...])
-                + mm(flat(r.kvb[:, at, :]), r.wkvt[...])
-            )
-            .astype(BF16)
-            .reshape(seqs, rows, width)
-        )
-
-    def n1_push(k):
-        idx = (t + k) % nt
-        n1_rows(idx)
-        push(lambda i: slot(r.g2p, i), r.n1_r, r.s_n1, idx)
-
-    push_done(lambda i: slot(r.g2p, i), r.g2_r, r.s_g2)
-    each(nt, n1_push, 1)
-    n1_rows(t)
+        r.g2[s] = (mm(r.qb[s], r.wqt[...]) + mm(r.kvb[s], r.wkvt[...])).astype(BF16)
+        n1s.push_all(s)
 
     for which, dst in ((other, r.gb_s), (d, r.gb_o)):
         cols = pl.ds(pl.multiple_of(which * half, LANES), half)
@@ -783,12 +850,11 @@
     send_gb = remote(r.gb_s, r.gb_r, r.s_gb.at[0], r.s_gb.at[1], dp=other)
     send_gb.start()
     red_a.sum()
-
-    for k in range(1, nt):
-        pull(r.ml_r, r.s_ml, (t + k) % nt)
-    mlp = summed(r.mlp, r.ml_r)
-    r.res[...] = (r.middle[...] + vec(5) * mlp).astype(BF16)
-    keep_sum(5, r.cot[:, span(t), :].astype(F32) * mlp)
+    for s in range(seqs):
+        n1s.join(s)
+
+    for s in range(seqs):
+        mls.join(s)
     outs = []
 
     def store(src, dst):
@@ -796,16 +862,17 @@
         cp.start()
         outs.append(cp)
 
-    store(r.res, r.res_out)
+    for s in range(seqs):
+        grad1 = n1s.total(s)
+        unit, rstd = norm_parts(r.tok[s, span(t), :].astype(F32))
+        keep_sum(0, s, grad1)
+        keep_sum(1, s, grad1 * unit)
+        r.gtok[s] = r.midg[s] + norm_back(grad1, unit, rstd, vec(1, s))
+        mlp = mls.total(s)
+        r.res[s] = (r.middle[s] + vec(5, s) * mlp).astype(BF16)
+        keep_sum(5, s, r.cot[s, span(t), :].astype(F32) * mlp)
     red_b = Reduction(send_gb, r.gb_o, r.gb_r, r.gb_c, r.gb_t, r.s_gbc, r.s_gbg)
     red_b.send()
-
-    for k in range(1, nt):
-        pull(r.n1_r, r.s_n1, (t + k) % nt)
-    grad1 = summed(r.g2p, r.n1_r)
-    unit, rstd = norm_parts(r.tok[:, span(t), :].astype(F32))
-    keep_sum(0, grad1)
-    keep_sum(1, grad1 * unit)
 
     def mcol(idx):
         return pl.ds(pl.multiple_of(idx * z.mcols, LANES), z.mcols)
@@ -815,13 +882,14 @@
         remote(
             r.msum.at[:, mcol(to)], r.mt_r.at[t], r.s_mt.at[0, to], r.s_mt.at[1, t], tp=to
         ).start()
-    r.gtok[...] = r.midg[...] + norm_back(grad1, unit, rstd, vec(1))
+    store(r.res, r.res_out)
     store(r.gtok, r.gtok_out)
     red_b.sum()
     total = r.msum[:, mcol(t)]
     for k in range(1, nt):
         fr = (t + k) % nt
-        pull(r.mt_r, r.s_mt, fr)
+        there = r.mt_r.at[fr]
+        remote(there, there, r.s_mt.at[0, fr], r.s_mt.at[1, fr], tp=fr).wait_recv()
         total = total + r.mt_r[fr]
     r.md_s[...] = total
     send_md = remote(r.md_s, r.md_r, r.s_md.at[0], r.s_md.at[1], dp=other)
@@ -853,21 +921,14 @@
 
     for cp in send_w:
         cp.wait_send()
-    line_close(r.tok, r.s_tok, r.r_tok)
-    line_close(r.n2, r.s_n2, r.r_n2)
-    line_close(r.bg, r.s_bg, r.r_bg)
+    for s in range(seqs):
+        for group in (cots, n2s, bgs, brs, mls, n1s):
+            group.close(s)
     for k in range(1, nt):
         to = (t + k) % nt
-        remote(r.cot_in, slot(r.cot, t), r.s_cot.at[0, to], r.s_cot.at[1, t], tp=to).wait_send()
-        for s in range(seqs):
-            remote(
-                r.part.at[s, span(to), :], r.br_r.at[t, s], r.s_br.at[s, to], r.r_br.at[s, t], tp=to
-            ).wait_send()
         remote(
             r.msum.at[:, mcol(to)], r.mt_r.at[t], r.s_mt.at[0, to], r.s_mt.at[1, t], tp=to
         ).wait_send()
-    push_done(lambda i: slot(r.mlp, i), r.ml_r, r.s_ml)
-    push_done(lambda i: slot(r.g2p, i), r.n1_r, r.s_n1)
 
     def dkv_sent(j):
         for s in range(seqs):
@@ -880,18 +941,33 @@
         cp.wait()
 
 
-def finish_kernel(z, ga, gb, emb, mg, res, gtok, *outs):
-    res_o, gtok_o, gq, gk, gv, go, gu, gd, gm = outs
+def finish_kernel(z, ga, gb, emb, mg, res, gtok, *refs):
+    outs, stage, sems = refs[:9], refs[9:18], refs[18]
     hw = z.hw
-    res_o[...] = res[...]
-    gtok_o[...] = gtok[...]
-    for i, out in enumerate((gq, gk, gv, go)):
-        out[...] = gb[i * hw : (i + 1) * hw, :].astype(F32)
-    gu[...] = ga[:, 0 : z.ff].astype(F32)
-    gd[...] = ga[:, z.ff : 2 * z.ff].astype(F32)
+    copies = []
+
+    def put(i, value):
+        stage[i][...] = value
+        cp = pltpu.make_async_copy(stage[i], outs[i], sems.at[i])
+        cp.start()
+        copies.append(cp)
+
+    put(6, ga[:, 0 : z.ff].astype(F32))
+    put(7, ga[:, z.ff : 2 * z.ff].astype(F32))
+    for i in range(4):
+        put(2 + i, gb[i * hw : (i + 1) * hw, :].astype(F32))
+    put(0, res[...])
+    put(1, gtok[...])
     e = emb[...].reshape(z.nc * 8, z.half)
     m = mg[...].reshape(z.nc * 8, z.mcols)
-    gm[...] = lax.dot_general(e, m, TN, precision=lax.Precision.HIGHEST, preferred_element_type=F32)
+    put(
+        8,
+        lax.dot_general(
+            e, m, TN, precision=lax.Precision.HIGHEST, preferred_element_type=F32
+        ),
+    )
+    for cp in copies:
+        cp.wait()
 
 
 IN_NAMES = (
@@ -905,8 +981,6 @@
     "wd_in",
     "wm_in",
     "cot_in",
-    "rate_in",
-    "rope_in",
 )
 OUT_NAMES = ("res_out", "gtok_out", "ga_out", "gb_out", "emb_out", "mg_out")
 
@@ -915,12 +989,6 @@
     def shards(tokens, steps, wq, wk, wv, wo, wu, wd, wm, cot):
         wq, wk, wv, wo = wq.T, wk.T, wv.T, wo.T
         z = Dims(mesh, tokens.shape, wq.shape, wu.shape, wm.shape)
-        half_dim = z.width // 2
-        rate = jnp.exp(jnp.arange(half_dim, dtype=F32) * (-math.log(10000.0) / half_dim))
-        rope = jnp.exp(
-            jnp.arange(HEAD_DIM // 2, dtype=F32) * (-2.0 * math.log(10000.0) / HEAD_DIM)
-        )
-        rope = jnp.tile(rope, LANES // (HEAD_DIM // 2))
         table = scratch_table(z)
         names = list(IN_NAMES) + list(OUT_NAMES) + list(table)
         hbm = pl.BlockSpec(memory_space=pl.ANY)
@@ -938,30 +1006,32 @@
                 shape((z.nc, 8, z.half), F32),
                 shape((z.nc, 8, z.mcols), F32),
             ),
-            in_specs=[hbm, smem] + [hbm] * 8 + [vmem, vmem],
+            in_specs=[hbm, smem] + [hbm] * 8,
             out_specs=[hbm] * 6,
             scratch_shapes=list(table.values()),
             compiler_params=pltpu.CompilerParams(
                 collective_id=0, has_side_effects=True, vmem_limit_bytes=VMEM_BYTES
             ),
             name="layer",
-        )(tokens, steps, wq, wk, wv, wo, wu, wd, wm, cot, rate[None], rope[None])
+        )(tokens, steps.T, wq, wk, wv, wo, wu, wd, wm, cot)
         res, gtok, ga, gb, emb, mg = outs
+        shapes = (
+            (own, BF16),
+            (own, F32),
+            ((z.hw, z.half), F32),
+            ((z.hw, z.half), F32),
+            ((z.hw, z.half), F32),
+            ((z.hw, z.half), F32),
+            ((z.half, z.ff), F32),
+            ((z.half, z.ff), F32),
+            ((z.half, z.mcols), F32),
+        )
         done = pl.pallas_call(
             functools.partial(finish_kernel, z),
-            out_shape=(
-                shape(own, BF16),
-                shape(own, F32),
-                shape((z.hw, z.half), F32),
-                shape((z.hw, z.half), F32),
-                shape((z.hw, z.half), F32),
-                shape((z.hw, z.half), F32),
-                shape((z.half, z.ff), F32),
-                shape((z.half, z.ff), F32),
-                shape((z.half, z.mcols), F32),
-            ),
+            out_shape=tuple(shape(*o) for o in shapes),
             in_specs=[vmem] * 6,
-            out_specs=[vmem] * 9,
+            out_specs=[hbm] * 9,
+            scratch_shapes=[pltpu.VMEM(*o) for o in shapes] + [pltpu.SemaphoreType.DMA((9,))],
             compiler_params=pltpu.CompilerParams(vmem_limit_bytes=VMEM_BYTES),
             name="finish",
         )(ga, gb, emb, mg, res, gtok)

time: 190 us -> 156 us (0.82)
  Pallas kernels: 187 us -> 155 us
    pallas_call x1, Pallas kernels: 181 us -> 149 us  [shards(): pl.pallas_call(functools.partial(layer_kernel, z, names), out_shape=(shap...]
where the time goes in v2:
time: 156 us
  Pallas kernels  155 us (99%)
    pallas_call x1, Pallas kernels, shards(): pl.pallas_call(functools.partial(layer_kernel, z, names), out_shape=(shap...  149 us
    pallas_call x1, Pallas kernels, shards(): pl.pallas_call(functools.partial(finish_kernel, z), out_shape=tuple((shap...  5.88 us

profile of v2, /device:TPU:0, one launch (start us, length us, event | category | flops | bytes accessed | tf_op | source)
XLA Modules:
  0.0 155.7 jit_solution(3408675311629632841)
XLA Ops:
  0.6 149.0 %layer.1 = (bf16[2,64,768]{2,1,0:T(8,128)(2,1)}, f32[2,64,768]{2,1,0:T(8,128)}, bf16[384,1536]{1,0:T(8,128)(2,1)}, bf16[768,384]{1,0:T(8,128)(2,1)}, f32[4,8,384]{2,1,0:T(8,128)}, /*index=5*/f32[4,8,1152]{2,1,0:T(8,128)}) custom-call(bf16[2,64,768]{2,1,0:T(8,128)(2,1)} %refs_0_.1, s32[1,2]{1,0:T(1,128)} %bitcast.13, bf16[192,384]{1,0:T(8,128)(2,1)} %bitcast.9, ...), custom_call_target="tpu_custom_call" | custom-call | tf_op jit(solution)/shard_map/layer/pallas_call | solution.py:999
  149.7 5.9 %finish.1 = (bf16[2,64,768]{2,1,0:T(8,128)(2,1)}, f32[2,64,768]{2,1,0:T(8,128)}, f32[192,384]{1,0:T(8,128)}, f32[192,384]{1,0:T(8,128)}, f32[192,384]{1,0:T(8,12...) custom-call(bf16[384,1536]{1,0:T(8,128)(2,1)} %get-tuple-element.24.ga, ...), custom_call_target="tpu_custom_call" | custom-call | tf_op jit(solution)/shard_map/finish/pallas_call | solution.py:1029

commit v3 on v2

--- a/solution.py
+++ b/solution.py
@@ -415,6 +415,12 @@
 
     for s in range(seqs):
         toks.open(r.tok_in.at[s], s)
+
+    @pl.when(outer)
+    def _():
+        for s in range(seqs):
+            cots.open(r.cot_in.at[s], s)
+
     send_emb = remote(r.emb_s, r.emb_r, r.s_e.at[0], r.s_e.at[1], dp=other)
     send_emb.start()
     send_w = [
@@ -510,11 +516,13 @@
     for s in range(seqs):
         toks.relay(s)
         toks.collect(s, make_qkv)
-    for s in range(seqs):
-        toks.close(s)
+
+    @pl.when(inner)
+    def _():
+        for s in range(seqs):
+            cots.open(r.cot_in.at[s], s)
+
     cp_cot.wait()
-    for s in range(seqs):
-        cots.open(r.cot_in.at[s], s)
     mod_take(first_cols, z.mod, mod2)
     for i in range(3, 6):
         cp_w[i].wait()
@@ -578,9 +586,9 @@
 
     each(seqs, attend_seq)
     for s in range(seqs):
+        cots.relay(s)
+    for s in range(seqs):
         brs.join(s)
-    for s in range(seqs):
-        cots.relay(s)
 
     for s in range(seqs):
         branch = brs.total(s)
@@ -615,6 +623,82 @@
         n2s.collect(s, feed)
     g2s.join(0)
 
+    class Reduction:
+        def __init__(self, got, mine, theirs, buf, total, sems, sems_all):
+            self.got, self.mine, self.theirs, self.buf, self.total = got, mine, theirs, buf, total
+            self.sems, self.sems_all = sems, sems_all
+            self.chunk = buf.shape[1]
+            self.owners = mine.shape[0] // self.chunk
+
+        def rows(self, o):
+            return pl.ds(pl.multiple_of(o * self.chunk, 16), self.chunk)
+
+        def part(self, o):
+            return remote(
+                self.mine.at[self.rows(o), :],
+                self.buf.at[c],
+                self.sems.at[0, o],
+                self.sems.at[1, c],
+                ctx=o,
+            )
+
+        def share(self, owner, to):
+            here = self.total.at[self.rows(owner), :]
+            return remote(here, here, self.sems_all.at[0, to], self.sems_all.at[1, owner], ctx=to)
+
+        def to_owners(self, body):
+            def one(k):
+                o = (c + k) % nc
+
+                @pl.when(o < self.owners)
+                def _():
+                    body(o)
+
+            each(nc, one, 1)
+
+        def as_owner(self, body):
+            @pl.when(c < self.owners)
+            def _():
+                body()
+
+        def send(self):
+            self.got.wait()
+            self.mine[...] = (self.mine[...].astype(F32) + self.theirs[...].astype(F32)).astype(
+                BF16
+            )
+            self.to_owners(lambda o: self.part(o).start())
+
+        def sum(self):
+            def body():
+                def add(k, acc):
+                    fr = (c + k) % nc
+                    there = self.buf.at[fr]
+                    remote(
+                        there, there, self.sems.at[0, fr], self.sems.at[1, fr], ctx=fr
+                    ).wait_recv()
+                    return acc + self.buf[fr].astype(F32)
+
+                acc = self.mine[self.rows(c), :].astype(F32)
+                if nc <= 4:
+                    for k in range(1, nc):
+                        acc = add(k, acc)
+                else:
+                    acc = lax.fori_loop(1, nc, add, acc)
+                self.total[self.rows(c), :] = acc.astype(BF16)
+                each(nc, lambda k: self.share(c, (c + k) % nc).start(), 1)
+
+            self.as_owner(body)
+
+        def take(self):
+            def one(o):
+                self.share(o, o).wait_recv()
+                self.part(o).wait_send()
+
+            self.to_owners(one)
+            self.as_owner(
+                lambda: each(nc, lambda k: self.share(c, (c + k) % nc).wait_send(), 1)
+            )
+
     def pair_grads(lhs, rhs, mine, sent, lo, hi):
         right = flat(rhs[...])
         for which, dst in ((other, sent), (d, mine)):
@@ -629,6 +713,9 @@
     g2s.join(1)
     for s in range(seqs):
         r.ml[s] = mm(r.act[s], r.wd[...], NT).astype(BF16)
+
+    red_a = Reduction(send_ga, r.ga_o, r.ga_r, r.ga_c, r.ga_t, r.s_gac, r.s_gag)
+    red_a.send()
 
     r.msum[...] = jnp.zeros((8, z.mod), F32)
 
@@ -656,84 +743,6 @@
     bgs.relay(0)
     bgs.collect(0, out_grads)
 
-    class Reduction:
-        def __init__(self, got, mine, theirs, buf, total, sems, sems_all):
-            self.got, self.mine, self.theirs, self.buf, self.total = got, mine, theirs, buf, total
-            self.sems, self.sems_all = sems, sems_all
-            self.chunk = buf.shape[1]
-            self.owners = mine.shape[0] // self.chunk
-
-        def rows(self, o):
-            return pl.ds(pl.multiple_of(o * self.chunk, 16), self.chunk)
-
-        def part(self, o):
-            return remote(
-                self.mine.at[self.rows(o), :],
-                self.buf.at[c],
-                self.sems.at[0, o],
-                self.sems.at[1, c],
-                ctx=o,
-            )
-
-        def share(self, owner, to):
-            here = self.total.at[self.rows(owner), :]
-            return remote(here, here, self.sems_all.at[0, to], self.sems_all.at[1, owner], ctx=to)
-
-        def to_owners(self, body):
-            def one(k):
-                o = (c + k) % nc
-
-                @pl.when(o < self.owners)
-                def _():
-                    body(o)
-
-            each(nc, one, 1)
-
-        def as_owner(self, body):
-            @pl.when(c < self.owners)
-            def _():
-                body()
-
-        def send(self):
-            self.got.wait()
-            self.mine[...] = (self.mine[...].astype(F32) + self.theirs[...].astype(F32)).astype(
-                BF16
-            )
-            self.to_owners(lambda o: self.part(o).start())
-
-        def sum(self):
-            def body():
-                def add(k, acc):
-                    fr = (c + k) % nc
-                    there = self.buf.at[fr]
-                    remote(
-                        there, there, self.sems.at[0, fr], self.sems.at[1, fr], ctx=fr
-                    ).wait_recv()
-                    return acc + self.buf[fr].astype(F32)
-
-                acc = self.mine[self.rows(c), :].astype(F32)
-                if nc <= 4:
-                    for k in range(1, nc):
-                        acc = add(k, acc)
-                else:
-                    acc = lax.fori_loop(1, nc, add, acc)
-                self.total[self.rows(c), :] = acc.astype(BF16)
-                each(nc, lambda k: self.share(c, (c + k) % nc).start(), 1)
-
-            self.as_owner(body)
-
-        def take(self):
-            def one(o):
-                self.share(o, o).wait_recv()
-                self.part(o).wait_send()
-
-            self.to_owners(one)
-            self.as_owner(
-                lambda: each(nc, lambda k: self.share(c, (c + k) % nc).wait_send(), 1)
-            )
-
-    red_a = Reduction(send_ga, r.ga_o, r.ga_r, r.ga_c, r.ga_t, r.s_gac, r.s_gag)
-    red_a.send()
     bgs.relay(1)
 
     def back_seq(s):
@@ -815,6 +824,7 @@
         back_seq(s)
 
     each(seqs, back_step)
+    red_a.sum()
 
     for s in range(seqs):
         g2s.close(s)
@@ -849,9 +859,10 @@
         dst[3 * hw : 4 * hw, :] = mm(flat(r.attl[:, :, 0:hw]), right, TN).astype(BF16)
     send_gb = remote(r.gb_s, r.gb_r, r.s_gb.at[0], r.s_gb.at[1], dp=other)
     send_gb.start()
-    red_a.sum()
-    for s in range(seqs):
-        n1s.join(s)
+    red_b = Reduction(send_gb, r.gb_o, r.gb_r, r.gb_c, r.gb_t, r.s_gbc, r.s_gbg)
+    n1s.join(0)
+    red_b.send()
+    n1s.join(1)
 
     for s in range(seqs):
         mls.join(s)
@@ -868,12 +879,11 @@
         keep_sum(0, s, grad1)
         keep_sum(1, s, grad1 * unit)
         r.gtok[s] = r.midg[s] + norm_back(grad1, unit, rstd, vec(1, s))
+        if s == 0:
+            red_b.sum()
         mlp = mls.total(s)
         r.res[s] = (r.middle[s] + vec(5, s) * mlp).astype(BF16)
         keep_sum(5, s, r.cot[s, span(t), :].astype(F32) * mlp)
-    red_b = Reduction(send_gb, r.gb_o, r.gb_r, r.gb_c, r.gb_t, r.s_gbc, r.s_gbg)
-    red_b.send()
-
     def mcol(idx):
         return pl.ds(pl.multiple_of(idx * z.mcols, LANES), z.mcols)
 
@@ -884,7 +894,6 @@
         ).start()
     store(r.res, r.res_out)
     store(r.gtok, r.gtok_out)
-    red_b.sum()
     total = r.msum[:, mcol(t)]
     for k in range(1, nt):
         fr = (t + k) % nt
@@ -922,7 +931,7 @@
     for cp in send_w:
         cp.wait_send()
     for s in range(seqs):
-        for group in (cots, n2s, bgs, brs, mls, n1s):
+        for group in (toks, cots, n2s, bgs, brs, mls, n1s):
             group.close(s)
     for k in range(1, nt):
         to = (t + k) % nt

time: 156 us -> 144 us (0.923)
  Pallas kernels: 155 us -> 143 us
    pallas_call x1, Pallas kernels: 149 us -> 137 us  [shards(): pl.pallas_call(functools.partial(layer_kernel, z, names), out_shape=(shap...]
where the time goes in v3:
time: 144 us
  Pallas kernels  143 us (99%)
    pallas_call x1, Pallas kernels, shards(): pl.pallas_call(functools.partial(layer_kernel, z, names), out_shape=(shap...  137 us
    pallas_call x1, Pallas kernels, shards(): pl.pallas_call(functools.partial(finish_kernel, z), out_shape=tuple((shap...  5.88 us

profile of v3, /device:TPU:0, one launch (start us, length us, event | category | flops | bytes accessed | tf_op | source)
XLA Modules:
  0.0 144.2 jit_solution(13104419141986675565)
XLA Ops:
  0.6 137.5 %layer.1 = (bf16[2,64,768]{2,1,0:T(8,128)(2,1)}, f32[2,64,768]{2,1,0:T(8,128)}, bf16[384,1536]{1,0:T(8,128)(2,1)}, bf16[768,384]{1,0:T(8,128)(2,1)}, f32[4,8,384]{2,1,0:T(8,128)}, /*index=5*/f32[4,8,1152]{2,1,0:T(8,128)}) custom-call(bf16[2,64,768]{2,1,0:T(8,128)(2,1)} %refs_0_.1, s32[1,2]{1,0:T(1,128)} %bitcast.13, bf16[192,384]{1,0:T(8,128)(2,1)} %bitcast.9, ...), custom_call_target="tpu_custom_call" | custom-call | tf_op jit(solution)/shard_map/layer/pallas_call | solution.py:1008
  138.2 5.9 %finish.1 = (bf16[2,64,768]{2,1,0:T(8,128)(2,1)}, f32[2,64,768]{2,1,0:T(8,128)}, f32[192,384]{1,0:T(8,128)}, f32[192,384]{1,0:T(8,128)}, f32[192,384]{1,0:T(8,12...) custom-call(bf16[384,1536]{1,0:T(8,128)(2,1)} %get-tuple-element.24.ga, ...), custom_call_target="tpu_custom_call" | custom-call | tf_op jit(solution)/shard_map/finish/pallas_call | solution.py:1038

commit v4 on v3

--- a/solution.py
+++ b/solution.py
@@ -96,15 +96,15 @@
         cosine=vm((z.block, LANES), F32),
         sine=vm((z.block, LANES), F32),
         nrm=vm(full),
-        q=vm((z.seqs, z.block, WIN)),
+        qd=vm((z.seqs, z.block, z.kvw)),
         kv=vm((z.nc, z.seqs, z.block, z.kvw)),
         vt=vm((WIN, z.block)),
         stat=vm((2, 8, z.block), F32),
         acc=vm((z.hw, z.block), F32),
         att=vm((z.seqs, z.hw, z.block), F32),
         attl=vm((z.seqs, z.block, WIN)),
-        lse=vm((z.seqs, 8, z.block), F32),
-        delta=vm((z.seqs, 8, z.block), F32),
+        lse=vm((z.nc, z.seqs, 8, z.block), F32),
+        delta=vm((z.nc, z.seqs, 8, z.block), F32),
         br=vm(full),
         br_m=vm(pair),
         br_r=vm(pair),
@@ -122,12 +122,13 @@
         ml_r=vm(pair),
         midg=vm(own, F32),
         bg=vm(full),
-        do=vm((z.seqs, z.block, WIN)),
+        seen=vm((z.block, z.kvw)),
         dot=vm((WIN, z.block)),
-        dqt=vm((z.hw, z.block), F32),
+        dqt=vm((z.seqs, z.hw, z.block), F32),
+        dq_s=vm((z.nc, z.seqs, z.hw, z.block)),
+        dq_r=vm((z.nc, z.seqs, z.hw, z.block)),
         dq=vm((z.seqs, z.block, WIN), F32),
         dkv=vm((z.seqs, z.block, z.kvw), F32),
-        dkv_r=vm((z.nc, z.seqs, z.block, z.kvw)),
         qb=vm((z.seqs, z.block, WIN)),
         kvb=vm((z.seqs, z.block, z.kvw)),
         n1_m=vm(pair),
@@ -173,17 +174,23 @@
         r_ml=sem(z.seqs, 2),
         s_bg=sem(z.seqs, 4),
         r_bg=sem(z.seqs, z.nt),
-        s_dk=sem(z.nc, z.seqs),
-        r_dk=sem(z.nc, z.seqs),
+        s_q=sem(z.nc, z.seqs),
+        r_q=sem(z.nc, z.seqs),
+        s_do=sem(z.nc, z.seqs, z.nt),
+        r_do=sem(z.nc, z.seqs, z.nt),
+        s_st=sem(2, z.nc, z.seqs),
+        r_st=sem(2, z.nc, z.seqs),
+        s_dq=sem(z.nc, z.seqs),
+        r_dq=sem(z.nc, z.seqs),
         s_n1=sem(z.seqs, 4),
         m_n1=sem(z.seqs, 2),
         r_n1=sem(z.seqs, 2),
         s_ga=sem(2),
-        s_gac=sem(2, z.nc),
-        s_gag=sem(2, z.nc),
+        s_gac=sem(2, max(z.nc, 12)),
+        s_gag=sem(2, max(z.nc, 12)),
         s_gb=sem(2),
-        s_gbc=sem(2, z.nc),
-        s_gbg=sem(2, z.nc),
+        s_gbc=sem(2, max(z.nc, 12)),
+        s_gbg=sem(2, max(z.nc, 12)),
         s_mt=sem(2, z.nt),
         s_md=sem(2),
         s_mc=sem(2, z.nc),
@@ -302,8 +309,8 @@
             )
 
         def open(self, src, s):
+            self.copy(src, s, t, 1, cross).start()
             self.copy(src, s, t, 0, mate).start()
-            self.copy(src, s, t, 1, cross).start()
 
         def wait(self, s, idx):
             self.copy(piece(self.buf, s, idx), s, idx, 0, mate).wait_recv()
@@ -494,7 +501,7 @@
         for j in range(WIN // LANES):
             x = q_pre[:, j * LANES : (j + 1) * LANES]
             x = (x * cos1 + swap(x) * sin1) * (HEAD_DIM ** -0.5)
-            r.q[s, at, j * LANES : (j + 1) * LANES] = x.astype(BF16)
+            r.qd[s, at, j * LANES : (j + 1) * LANES] = x.astype(BF16)
         for j in range(z.kvw // LANES):
             x = kv_pre[:, j * LANES : (j + 1) * LANES]
             keys = min(max(hw - j * LANES, 0), LANES)
@@ -539,7 +546,7 @@
         r.stat[0] = jnp.full((8, block), NEG, F32)
         r.stat[1] = jnp.zeros((8, block), F32)
         r.acc[...] = jnp.zeros((hw, block), F32)
-        q = r.q[s]
+        q = r.qd[s, :, 0:WIN]
 
         def one_block(back):
             j = c - back
@@ -576,7 +583,7 @@
         for h in range(z.heads):
             lo = h * HEAD_DIM
             denom = r.stat[1, h : h + 1, :]
-            r.lse[s, h : h + 1, :] = r.stat[0, h : h + 1, :] + jnp.log(denom)
+            r.lse[c, s, h : h + 1, :] = r.stat[0, h : h + 1, :] + jnp.log(denom)
             r.att[s, lo : lo + HEAD_DIM, :] = r.acc[lo : lo + HEAD_DIM, :] / denom
         low = jnp.transpose(r.att[s]).astype(BF16)
         r.attl[s, :, 0:hw] = low
@@ -585,12 +592,30 @@
         brs.push_all(s)
 
     each(seqs, attend_seq)
+
+    def query_copy(j, s, to):
+        return remote(
+            r.qd.at[s, :, 0:LANES],
+            r.kv.at[j, s, :, 0:LANES],
+            r.s_q.at[to, s],
+            r.r_q.at[j, s],
+            ctx=to,
+        )
+
+    def stat_copy(buf, which, j, s, to):
+        return remote(
+            buf.at[j, s], buf.at[j, s], r.s_st.at[which, to, s], r.r_st.at[which, j, s], ctx=to
+        )
+
+    def send_queries(to):
+        for s in range(seqs):
+            query_copy(c, s, to).start()
+            stat_copy(r.lse, 0, c, s, to).start()
+
+    each(c, send_queries)
     for s in range(seqs):
         cots.relay(s)
-    for s in range(seqs):
-        brs.join(s)
-
-    for s in range(seqs):
+    def middle_rows(s):
         branch = brs.total(s)
         r.branch[s] = branch
         middle = r.tok[s, span(t), :].astype(F32) + vec(2, s) * branch
@@ -598,6 +623,12 @@
         unit, _ = norm_parts(middle)
         r.n2[s, span(t), :] = (unit * (1.0 + vec(4, s)) + vec(3, s)).astype(BF16)
         n2s.open(piece(r.n2, s, t), s)
+
+    brs.join(0)
+    middle_rows(0)
+    brs.join(1)
+    n2s.relay(0)
+    middle_rows(1)
 
     def feed(s, idx, i):
         at = span(idx)
@@ -619,7 +650,8 @@
         feed(s, t, 0)
     for s in range(seqs):
         cots.collect(s, None)
-        n2s.relay(s)
+        if s > 0:
+            n2s.relay(s)
         n2s.collect(s, feed)
     g2s.join(0)
 
@@ -661,14 +693,22 @@
             def _():
                 body()
 
-        def send(self):
+        def pair(self):
             self.got.wait()
             self.mine[...] = (self.mine[...].astype(F32) + self.theirs[...].astype(F32)).astype(
                 BF16
             )
+
+        def step1(self):
             self.to_owners(lambda o: self.part(o).start())
 
-        def sum(self):
+        def step2(self):
+            pass
+
+        def step4(self):
+            pass
+
+        def step3(self):
             def body():
                 def add(k, acc):
                     fr = (c + k) % nc
@@ -699,23 +739,102 @@
                 lambda: each(nc, lambda k: self.share(c, (c + k) % nc).wait_send(), 1)
             )
 
-    def pair_grads(lhs, rhs, mine, sent, lo, hi):
-        right = flat(rhs[...])
-        for which, dst in ((other, sent), (d, mine)):
-            cols = pl.ds(pl.multiple_of(which * half, half), half)
-            left = flat(lhs[:, :, cols])
-            dst[:, lo:hi] = mm(left, right, TN).astype(BF16)
-
-    pair_grads(r.mgrad, r.act, r.ga_o, r.ga_s, z.ff, 2 * z.ff)
-    pair_grads(r.n2, r.hgrad, r.ga_o, r.ga_s, 0, z.ff)
-    send_ga = remote(r.ga_s, r.ga_r, r.s_ga.at[0], r.s_ga.at[1], dp=other)
-    send_ga.start()
-    g2s.join(1)
-    for s in range(seqs):
-        r.ml[s] = mm(r.act[s], r.wd[...], NT).astype(BF16)
-
-    red_a = Reduction(send_ga, r.ga_o, r.ga_r, r.ga_c, r.ga_t, r.s_gac, r.s_gag)
-    red_a.send()
+    class Square:
+        def __init__(self, got, mine, theirs, buf, total, sems, sems_all):
+            self.got, self.mine, self.theirs, self.buf, self.total = got, mine, theirs, buf, total
+            self.sems = sems
+            self.part = buf.shape[1] // 2
+            by_x = c + 1 - 2 * (c % 2)
+            by_y = (c + 2) % 4
+            self.near = (by_x, by_y)
+            self.next = (by_y, by_x)
+            self.far = 3 - c
+
+        def rows(self, o, h):
+            return pl.ds(pl.multiple_of((2 * o + h) * self.part, 16), self.part)
+
+        def first(self, h, k):
+            o = (self.near[h], self.far)[k]
+            return remote(
+                self.mine.at[self.rows(o, h), :],
+                self.buf.at[2 * h + k, 0 : self.part, :],
+                self.sems.at[0, 2 * h + k],
+                self.sems.at[1, 2 * h + k],
+                ctx=self.near[h],
+            )
+
+        def second(self, h):
+            o = self.next[h]
+            return remote(
+                self.mine.at[self.rows(o, h), :],
+                self.buf.at[2 * h, self.part : 2 * self.part, :],
+                self.sems.at[0, 4 + h],
+                self.sems.at[1, 4 + h],
+                ctx=o,
+            )
+
+        def spread(self, h, o, to, which, landed):
+            at = self.total.at[self.rows(landed, h), :]
+            src = self.total.at[self.rows(o, h), :]
+            return remote(src, at, self.sems.at[0, which], self.sems.at[1, which], ctx=to)
+
+        def third(self, h, landed):
+            return self.spread(h, landed, self.next[h], 6 + h, landed)
+
+        def fourth(self, h, k, landed):
+            return self.spread(h, landed, self.near[h], 8 + 2 * h + k, landed)
+
+        def pair(self):
+            self.got.wait()
+            self.mine[...] = (self.mine[...].astype(F32) + self.theirs[...].astype(F32)).astype(
+                BF16
+            )
+
+        def step1(self):
+            for k in (1, 0):
+                for h in range(2):
+                    self.first(h, k).start()
+
+        def step2(self):
+            for k in (1, 0):
+                for h in range(2):
+                    self.first(h, k).wait_recv()
+                    at = self.rows((c, self.next[h])[k], h)
+                    self.mine[at, :] = (
+                        self.mine[at, :].astype(F32)
+                        + self.buf[2 * h + k, 0 : self.part, :].astype(F32)
+                    ).astype(BF16)
+                    if k == 1:
+                        self.second(h).start()
+
+        def step3(self):
+            for h in range(2):
+                self.second(h).wait_recv()
+                at = self.rows(c, h)
+                self.total[at, :] = (
+                    self.mine[at, :].astype(F32)
+                    + self.buf[2 * h, self.part : 2 * self.part, :].astype(F32)
+                ).astype(BF16)
+                self.third(h, c).start()
+            for h in range(2):
+                self.fourth(h, 0, c).start()
+
+        def step4(self):
+            for h in range(2):
+                self.third(h, self.next[h]).wait_recv()
+                self.fourth(h, 1, self.next[h]).start()
+
+        def take(self):
+            for h in range(2):
+                self.fourth(h, 0, self.near[h]).wait_recv()
+                self.fourth(h, 1, self.far).wait_recv()
+                for k in range(2):
+                    self.first(h, k).wait_send()
+                    self.fourth(h, k, c).wait_send()
+                self.second(h).wait_send()
+                self.third(h, c).wait_send()
+
+    Sums = Square if nc == 4 else Reduction
 
     r.msum[...] = jnp.zeros((8, z.mod), F32)
 
@@ -723,7 +842,7 @@
         lo = slot_idx * width
         r.msum[s : s + 1, lo : lo + width] = jnp.sum(value, axis=0, keepdims=True)
 
-    for s in range(seqs):
+    def middle_back(s):
         grad2 = g2s.total(s)
         unit, rstd = norm_parts(r.middle[s])
         mid_grad = r.cot[s, span(t), :].astype(F32) + norm_back(grad2, unit, rstd, vec(4, s))
@@ -734,109 +853,147 @@
         keep_sum(4, s, grad2 * unit)
         keep_sum(2, s, mid_grad * r.branch[s])
 
+    middle_back(0)
+
+    def pair_grads(lhs, rhs, mine, sent, lo, hi):
+        right = flat(rhs[...])
+        for which, dst in ((other, sent), (d, mine)):
+            cols = pl.ds(pl.multiple_of(which * half, half), half)
+            left = flat(lhs[:, :, cols])
+            dst[:, lo:hi] = mm(left, right, TN).astype(BF16)
+
+    pair_grads(r.mgrad, r.act, r.ga_o, r.ga_s, z.ff, 2 * z.ff)
+    pair_grads(r.n2, r.hgrad, r.ga_o, r.ga_s, 0, z.ff)
+    send_ga = remote(r.ga_s, r.ga_r, r.s_ga.at[0], r.s_ga.at[1], dp=other)
+    send_ga.start()
+    g2s.join(1)
+    bgs.relay(0)
+    red_a = Sums(send_ga, r.ga_o, r.ga_r, r.ga_c, r.ga_t, r.s_gac, r.s_gag)
+    red_a.pair()
+    red_a.step1()
+    middle_back(1)
+    for s in range(seqs):
+        r.ml[s] = mm(r.act[s], r.wd[...], NT).astype(BF16)
+
+    def grad_copy(j, s, idx, to):
+        at = span(idx)
+        return remote(
+            r.qd.at[s, at, LANES : z.kvw],
+            r.kv.at[j, s, at, LANES : z.kvw],
+            r.s_do.at[to, s, idx],
+            r.r_do.at[j, s, idx],
+            ctx=to,
+        )
+
     def out_grads(s, idx, i):
         at = span(idx)
-        r.do[s, at, :] = mm(r.bg[s, at, :], r.wot[...], NT).astype(BF16)
-
-    for s in range(seqs):
-        out_grads(s, t, 0)
-    bgs.relay(0)
-    bgs.collect(0, out_grads)
-
-    bgs.relay(1)
-
-    def back_seq(s):
-        do = r.do[s]
-        r.dot[...] = mm(eye, do, NT).astype(BF16)
+        do = mm(r.bg[s, at, :], r.wot[...], NT).astype(BF16)
+        over = WIN - z.vlo
+        r.qd[s, at, z.vlo : WIN] = r.qd[s, at, z.vlo : WIN] + do[:, 0:over]
+        r.qd[s, at, WIN : z.kvw] = do[:, over:WIN]
+        each(c, lambda to: grad_copy(c, s, idx, to).start())
+
+    def deltas(s):
+        r.dot[...] = mm(eye, r.qd[s, :, z.vlo : z.vlo + WIN], NT).astype(BF16)
         for h in range(z.heads):
             lo = h * HEAD_DIM
-            r.delta[s, h : h + 1, :] = jnp.sum(
+            r.delta[c, s, h : h + 1, :] = jnp.sum(
                 r.dot[z.voff + lo : z.voff + lo + HEAD_DIM, :].astype(F32)
                 * r.att[s, lo : lo + HEAD_DIM, :],
                 axis=0,
                 keepdims=True,
             )
-        r.dqt[...] = jnp.zeros((hw, block), F32)
-        q = r.q[s]
-
-        def one_block(j):
-            keys = r.kv[j, s, :, 0:WIN]
-            vals = r.kv[j, s, :, z.vlo : z.vlo + WIN]
-            r.vt[...] = mm(eye, keys, NT).astype(BF16)
+        each(c, lambda to: stat_copy(r.delta, 1, c, s, to).start())
+
+    def query_back_copy(j, s, to):
+        return remote(
+            r.dq_s.at[to, s], r.dq_r.at[j, s], r.s_dq.at[to, s], r.r_dq.at[j, s], ctx=to
+        )
+
+    def back_seq(s):
+        keys = r.kv[c, s, :, 0:WIN]
+        vals = r.kv[c, s, :, z.vlo : z.vlo + WIN]
+        r.vt[...] = mm(eye, keys, NT).astype(BF16)
+        r.dkv[s] = jnp.zeros((block, z.kvw), F32)
+
+        def one_block(k):
+            j = c + (nc - c - k) % (nc - c)
+
+            @pl.when(k == 0)
+            def _():
+                r.seen[...] = r.qd[s]
+
+            @pl.when(k > 0)
+            def _():
+                query_copy(j, s, j).wait_recv()
+                each(nt, lambda idx: grad_copy(j, s, idx, j).wait_recv())
+                stat_copy(r.lse, 0, j, s, j).wait_recv()
+                stat_copy(r.delta, 1, j, s, j).wait_recv()
+                r.seen[...] = r.kv[j, s]
+
+            q = r.seen[:, 0:WIN]
+            do = r.seen[:, z.vlo : z.vlo + WIN]
             dk = jnp.zeros((block, WIN), F32)
             dv = jnp.zeros((block, WIN), F32)
             for h in range(z.heads):
                 lo = h * HEAD_DIM
                 qh = head_of(q, h)
                 doh = head_of(do, h, z.voff)
-                prob = jnp.exp(mm(keys, qh, NT) - r.lse[s, h : h + 1, :])
+                prob = jnp.exp(mm(keys, qh, NT) - r.lse[j, s, h : h + 1, :])
                 dprob = mm(vals, doh, NT)
-                dsc = (prob * (dprob - r.delta[s, h : h + 1, :])).astype(BF16)
+                dsc = (prob * (dprob - r.delta[j, s, h : h + 1, :])).astype(BF16)
                 dv = dv + mm(prob.astype(BF16), doh)
                 dk = dk + mm(dsc, qh)
-                r.dqt[lo : lo + HEAD_DIM, :] += mm(r.vt[lo : lo + HEAD_DIM, :], dsc)
+                dqt = mm(r.vt[lo : lo + HEAD_DIM, :], dsc)
+
+                @pl.when(k == 0)
+                def _():
+                    r.dqt[s, lo : lo + HEAD_DIM, :] = dqt
+
+                @pl.when(k > 0)
+                def _():
+                    r.dq_s[j, s, lo : lo + HEAD_DIM, :] = dqt.astype(BF16)
+
             over = WIN - z.vlo
-            pieces = (
-                (0, z.vlo, dk[:, 0 : z.vlo]),
-                (z.vlo, WIN, dk[:, z.vlo : WIN] + dv[:, 0:over]),
-                (WIN, z.kvw, dv[:, over:WIN]),
-            )
-
-            @pl.when(j < c)
+            r.dkv[s, :, 0 : z.vlo] += dk[:, 0 : z.vlo]
+            r.dkv[s, :, z.vlo : WIN] += dk[:, z.vlo : WIN] + dv[:, 0:over]
+            r.dkv[s, :, WIN : z.kvw] += dv[:, over:WIN]
+
+            @pl.when(k > 0)
             def _():
-                for lo, hi, piece in pieces:
-                    r.kv[j, s, :, lo:hi] = piece.astype(BF16)
-                remote(
-                    r.kv.at[j, s], r.dkv_r.at[c, s], r.s_dk.at[j, s], r.r_dk.at[c, s], ctx=j
-                ).start()
-
-            @pl.when(j == c)
-            def _():
-                for lo, hi, piece in pieces:
-                    r.dkv[s, :, lo:hi] = piece
-
-        each(c + 1, one_block)
-        r.dq[s, :, 0:hw] = jnp.transpose(r.dqt[...]) * (HEAD_DIM ** -0.5)
-        r.dq[s, :, hw:WIN] = jnp.zeros((block, WIN - hw), F32)
-
-    def kv_sent(j):
-        for s in range(seqs):
-            each(
-                nt,
-                lambda idx: remote(
-                    r.kv.at[c, s, span(idx), :],
-                    r.kv.at[c, s, span(idx), :],
-                    r.s_kv.at[j, s, idx],
-                    r.r_kv.at[c, s, idx],
-                    ctx=j,
-                ).wait_send(),
-            )
-
-    each(nc, kv_sent, c + 1)
-
-    def back_step(s):
-        @pl.when(s == 1)
-        def _():
-            bgs.collect(1, out_grads)
-            for i in range(seqs):
-                mls.push_all(i)
-
-        back_seq(s)
-
-    each(seqs, back_step)
-    red_a.sum()
+                query_back_copy(c, s, j).start()
+
+        each(nc - c, one_block)
+
+    for s in range(seqs):
+        out_grads(s, t, 0)
+    bgs.collect(0, out_grads)
+    deltas(0)
+    red_a.step2()
+    bgs.relay(1)
+    for s in range(seqs):
+        mls.push_all(s)
+    back_seq(0)
+    bgs.collect(1, out_grads)
+    deltas(1)
+    red_a.step3()
+    back_seq(1)
+    red_a.step4()
+    for s in range(seqs):
+        mls.join(s)
 
     for s in range(seqs):
         g2s.close(s)
     cos1, sin1 = r.cosine[...], r.sine[...]
     for s in range(seqs):
 
-        def add_dkv(j):
-            there = r.dkv_r.at[j, s]
-            remote(there, there, r.s_dk.at[j, s], r.r_dk.at[j, s], ctx=j).wait_recv()
-            r.dkv[s] += r.dkv_r[j, s].astype(F32)
-
-        each(nc, add_dkv, c + 1)
+        def add_dq(j):
+            query_back_copy(j, s, j).wait_recv()
+            r.dqt[s] += r.dq_r[j, s].astype(F32)
+
+        each(c, add_dq)
+        r.dq[s, :, 0:hw] = jnp.transpose(r.dqt[s]) * (HEAD_DIM ** -0.5)
+        r.dq[s, :, hw:WIN] = jnp.zeros((block, WIN - hw), F32)
         for j in range(WIN // LANES):
             x = r.dq[s, :, j * LANES : (j + 1) * LANES]
             r.qb[s, :, j * LANES : (j + 1) * LANES] = (x * cos1 - swap(x) * sin1).astype(BF16)
@@ -859,13 +1016,13 @@
         dst[3 * hw : 4 * hw, :] = mm(flat(r.attl[:, :, 0:hw]), right, TN).astype(BF16)
     send_gb = remote(r.gb_s, r.gb_r, r.s_gb.at[0], r.s_gb.at[1], dp=other)
     send_gb.start()
-    red_b = Reduction(send_gb, r.gb_o, r.gb_r, r.gb_c, r.gb_t, r.s_gbc, r.s_gbg)
+    red_b = Sums(send_gb, r.gb_o, r.gb_r, r.gb_c, r.gb_t, r.s_gbc, r.s_gbg)
     n1s.join(0)
-    red_b.send()
+    red_b.pair()
+    red_b.step1()
     n1s.join(1)
-
-    for s in range(seqs):
-        mls.join(s)
+    red_b.step2()
+
     outs = []
 
     def store(src, dst):
@@ -880,7 +1037,7 @@
         keep_sum(1, s, grad1 * unit)
         r.gtok[s] = r.midg[s] + norm_back(grad1, unit, rstd, vec(1, s))
         if s == 0:
-            red_b.sum()
+            red_b.step3()
         mlp = mls.total(s)
         r.res[s] = (r.middle[s] + vec(5, s) * mlp).astype(BF16)
         keep_sum(5, s, r.cot[s, span(t), :].astype(F32) * mlp)
@@ -894,6 +1051,7 @@
         ).start()
     store(r.res, r.res_out)
     store(r.gtok, r.gtok_out)
+    red_b.step4()
     total = r.msum[:, mcol(t)]
     for k in range(1, nt):
         fr = (t + k) % nt
@@ -939,42 +1097,74 @@
             r.msum.at[:, mcol(to)], r.mt_r.at[t], r.s_mt.at[0, to], r.s_mt.at[1, t], tp=to
         ).wait_send()
 
-    def dkv_sent(j):
+    def kv_sent(to):
         for s in range(seqs):
-            remote(
-                r.kv.at[j, s], r.dkv_r.at[c, s], r.s_dk.at[j, s], r.r_dk.at[c, s], ctx=j
-            ).wait_send()
-
-    each(c, dkv_sent)
+
+            def one(idx):
+                mine = r.kv.at[c, s, span(idx), :]
+                remote(
+                    mine, mine, r.s_kv.at[to, s, idx], r.r_kv.at[c, s, idx], ctx=to
+                ).wait_send()
+
+            each(nt, one)
+            query_back_copy(c, s, to).wait_send()
+
+    each(nc, kv_sent, c + 1)
+
+    def query_sent(to):
+        for s in range(seqs):
+            query_copy(c, s, to).wait_send()
+            each(nt, lambda idx: grad_copy(c, s, idx, to).wait_send())
+            stat_copy(r.lse, 0, c, s, to).wait_send()
+            stat_copy(r.delta, 1, c, s, to).wait_send()
+
+    each(c, query_sent)
     for cp in outs:
         cp.wait()
 
 
-def finish_kernel(z, ga, gb, emb, mg, res, gtok, *refs):
-    outs, stage, sems = refs[:9], refs[9:18], refs[18]
+def finish_kernel(z, *refs):
+    ins, outs, refs = refs[:6], refs[6:15], refs[15:]
+    held, stage, sems = refs[:6], refs[6:15], refs[15]
     hw = z.hw
+    fetches = [
+        pltpu.make_async_copy(src, dst, sems.at[i]) for i, (src, dst) in enumerate(zip(ins, held))
+    ]
+    for cp in fetches:
+        cp.start()
+    ga, gb, emb, mg, res, gtok = held
     copies = []
 
     def put(i, value):
         stage[i][...] = value
-        cp = pltpu.make_async_copy(stage[i], outs[i], sems.at[i])
+        cp = pltpu.make_async_copy(stage[i], outs[i], sems.at[6 + i])
         cp.start()
         copies.append(cp)
 
+    def through(i, src):
+        cp = pltpu.make_async_copy(src, outs[i], sems.at[6 + i])
+        cp.start()
+        copies.append(cp)
+
+    fetches[0].wait()
     put(6, ga[:, 0 : z.ff].astype(F32))
     put(7, ga[:, z.ff : 2 * z.ff].astype(F32))
+    fetches[1].wait()
     for i in range(4):
         put(2 + i, gb[i * hw : (i + 1) * hw, :].astype(F32))
-    put(0, res[...])
-    put(1, gtok[...])
-    e = emb[...].reshape(z.nc * 8, z.half)
-    m = mg[...].reshape(z.nc * 8, z.mcols)
-    put(
-        8,
-        lax.dot_general(
-            e, m, TN, precision=lax.Precision.HIGHEST, preferred_element_type=F32
-        ),
-    )
+    fetches[2].wait()
+    fetches[3].wait()
+    e = emb[...].reshape(z.nc * 8, z.half).astype(BF16)
+    rest = mg[...].reshape(z.nc * 8, z.mcols)
+    terms = []
+    for _ in range(3):
+        terms.append(rest.astype(BF16))
+        rest = rest - terms[-1].astype(F32)
+    put(8, mm(jnp.concatenate([e] * 3, axis=0), jnp.concatenate(terms, axis=0), TN))
+    fetches[4].wait()
+    through(0, res)
+    fetches[5].wait()
+    through(1, gtok)
     for cp in copies:
         cp.wait()
 
@@ -1001,7 +1191,6 @@
         table = scratch_table(z)
         names = list(IN_NAMES) + list(OUT_NAMES) + list(table)
         hbm = pl.BlockSpec(memory_space=pl.ANY)
-        vmem = pl.BlockSpec(memory_space=pltpu.VMEM)
         smem = pl.BlockSpec(memory_space=pltpu.SMEM)
         own = (z.seqs, z.rows, z.width)
         shape = jax.ShapeDtypeStruct
@@ -1023,7 +1212,7 @@
             ),
             name="layer",
         )(tokens, steps.T, wq, wk, wv, wo, wu, wd, wm, cot)
-        res, gtok, ga, gb, emb, mg = outs
+        outs = outs[2:] + outs[:2]
         shapes = (
             (own, BF16),
             (own, F32),
@@ -1038,12 +1227,14 @@
         done = pl.pallas_call(
             functools.partial(finish_kernel, z),
             out_shape=tuple(shape(*o) for o in shapes),
-            in_specs=[vmem] * 6,
+            in_specs=[hbm] * 6,
             out_specs=[hbm] * 9,
-            scratch_shapes=[pltpu.VMEM(*o) for o in shapes] + [pltpu.SemaphoreType.DMA((9,))],
+            scratch_shapes=[pltpu.VMEM(o.shape, o.dtype) for o in outs]
+            + [pltpu.VMEM(*o) for o in shapes]
+            + [pltpu.SemaphoreType.DMA((15,))],
             compiler_params=pltpu.CompilerParams(vmem_limit_bytes=VMEM_BYTES),
             name="finish",
-        )(ga, gb, emb, mg, res, gtok)
+        )(*outs)
         return done[:2] + tuple(g.T for g in done[2:6]) + done[6:]
 
     rows = P("dp", ("ctx", "tp"), None)

time: 144 us -> 137 us (0.951)
  Pallas kernels: 143 us -> 136 us
    pallas_call x1, Pallas kernels: 137 us -> 132 us  [shards(): pl.pallas_call(functools.partial(layer_kernel, z, names), out_shape=(shap...]
    pallas_call x1, Pallas kernels: 5.88 us -> 4.03 us  [shards(): pl.pallas_call(functools.partial(finish_kernel, z), out_shape=tuple((shap...]
where the time goes in v4:
time: 137 us
  Pallas kernels  136 us (99%)
    pallas_call x1, Pallas kernels, shards(): pl.pallas_call(functools.partial(layer_kernel, z, names), out_shape=(shap...  132 us
    pallas_call x1, Pallas kernels, shards(): pl.pallas_call(functools.partial(finish_kernel, z), out_shape=tuple((shap...  4.03 us

profile of v4, /device:TPU:0, one launch (start us, length us, event | category | flops | bytes accessed | tf_op | source)
XLA Modules:
  0.0 137.1 jit_solution(7792838006109937298)
XLA Ops:
  0.6 132.2 %layer.1 = (bf16[2,64,768]{2,1,0:T(8,128)(2,1)}, f32[2,64,768]{2,1,0:T(8,128)}, bf16[384,1536]{1,0:T(8,128)(2,1)}, bf16[768,384]{1,0:T(8,128)(2,1)}, f32[4,8,384]{2,1,0:T(8,128)}, /*index=5*/f32[4,8,1152]{2,1,0:T(8,128)}) custom-call(bf16[2,64,768]{2,1,0:T(8,128)(2,1)} %refs_0_.1, s32[1,2]{1,0:T(1,128)} %bitcast.13, bf16[192,384]{1,0:T(8,128)(2,1)} %bitcast.9, ...), custom_call_target="tpu_custom_call" | custom-call | tf_op jit(solution)/shard_map/layer/pallas_call | solution.py:1197
  132.9 4.0 %finish.1 = (bf16[2,64,768]{2,1,0:T(8,128)(2,1)}, f32[2,64,768]{2,1,0:T(8,128)}, f32[192,384]{1,0:T(8,128)}, f32[192,384]{1,0:T(8,128)}, f32[192,384]{1,0:T(8,12...) custom-call(bf16[384,1536]{1,0:T(8,128)(2,1)} %get-tuple-element.24.refs_0_, ...), custom_call_target="tpu_custom_call" | custom-call | tf_op jit(solution)/shard_map/finish/pallas_call | solution.py:1227

commit v5 on v4

--- a/solution.py
+++ b/solution.py
@@ -70,6 +70,7 @@
         self.wide = 2 * self.ff
         self.heads_rows = 4 * self.hw
         self.mcols = self.mod // self.nt
+        self.thirds = self.mcols // self.half
 
 
 def scratch_table(z):
@@ -143,11 +144,11 @@
         gb_r=vm((z.heads_rows, z.half)),
         gb_c=vm((z.nc, chunk_rows(z.heads_rows, z.nc), z.half)),
         gb_t=vm((z.heads_rows, z.half)),
-        msum=vm((8, z.mod), F32),
-        mt_r=vm((z.nt, 8, z.mcols), F32),
-        md_s=vm((8, z.mcols), F32),
-        md_r=vm((8, z.mcols), F32),
-        mg=vm((z.nc, 8, z.mcols), F32),
+        msum=vm((z.nt, 8, z.half), F32),
+        mt_r=vm((z.nt, 8, z.half), F32),
+        md_s=vm((8, z.half), F32),
+        md_r=vm((8, z.half), F32),
+        mg=vm((z.nc, 2, 8, z.half), F32),
         res=vm(own),
         gtok=vm(own, F32),
         s_loc=sem(16),
@@ -593,6 +594,10 @@
 
     each(seqs, attend_seq)
 
+    split = nc == 4
+    last = c == nc - 1
+    skip = c // (nc - 1) if split else 0
+
     def query_copy(j, s, to):
         return remote(
             r.qd.at[s, :, 0:LANES],
@@ -612,7 +617,7 @@
             query_copy(c, s, to).start()
             stat_copy(r.lse, 0, c, s, to).start()
 
-    each(c, send_queries)
+    each(c, send_queries, skip)
     for s in range(seqs):
         cots.relay(s)
     def middle_rows(s):
@@ -816,10 +821,10 @@
                     + self.buf[2 * h, self.part : 2 * self.part, :].astype(F32)
                 ).astype(BF16)
                 self.third(h, c).start()
+
+        def step4(self):
             for h in range(2):
                 self.fourth(h, 0, c).start()
-
-        def step4(self):
             for h in range(2):
                 self.third(h, self.next[h]).wait_recv()
                 self.fourth(h, 1, self.next[h]).start()
@@ -836,11 +841,14 @@
 
     Sums = Square if nc == 4 else Reduction
 
-    r.msum[...] = jnp.zeros((8, z.mod), F32)
+    r.msum[...] = jnp.zeros((nt, 8, half), F32)
 
     def keep_sum(slot_idx, s, value):
-        lo = slot_idx * width
-        r.msum[s : s + 1, lo : lo + width] = jnp.sum(value, axis=0, keepdims=True)
+        value = jnp.sum(value, axis=0, keepdims=True)
+        for k in range(width // half):
+            to, row = divmod(slot_idx * (width // half) + k, z.thirds)
+            row = s * z.thirds + row
+            r.msum[to, row : row + 1, :] = value[:, k * half : (k + 1) * half]
 
     def middle_back(s):
         grad2 = g2s.total(s)
@@ -891,7 +899,7 @@
         over = WIN - z.vlo
         r.qd[s, at, z.vlo : WIN] = r.qd[s, at, z.vlo : WIN] + do[:, 0:over]
         r.qd[s, at, WIN : z.kvw] = do[:, over:WIN]
-        each(c, lambda to: grad_copy(c, s, idx, to).start())
+        each(c, lambda to: grad_copy(c, s, idx, to).start(), skip)
 
     def deltas(s):
         r.dot[...] = mm(eye, r.qd[s, :, z.vlo : z.vlo + WIN], NT).astype(BF16)
@@ -903,25 +911,73 @@
                 axis=0,
                 keepdims=True,
             )
-        each(c, lambda to: stat_copy(r.delta, 1, c, s, to).start())
+        each(c, lambda to: stat_copy(r.delta, 1, c, s, to).start(), skip)
 
     def query_back_copy(j, s, to):
         return remote(
             r.dq_s.at[to, s], r.dq_r.at[j, s], r.s_dq.at[to, s], r.r_dq.at[j, s], ctx=to
         )
 
-    def back_seq(s):
+    over = WIN - z.vlo
+
+    def pair_back(s, keys, vals, q, do, j, keep):
+        dk = jnp.zeros((block, WIN), F32)
+        dv = jnp.zeros((block, WIN), F32)
+        for h in range(z.heads):
+            lo = h * HEAD_DIM
+            qh = head_of(q, h)
+            doh = head_of(do, h, z.voff)
+            prob = jnp.exp(mm(keys, qh, NT) - r.lse[j, s, h : h + 1, :])
+            dprob = mm(vals, doh, NT)
+            dsc = (prob * (dprob - r.delta[j, s, h : h + 1, :])).astype(BF16)
+            dv = dv + mm(prob.astype(BF16), doh)
+            dk = dk + mm(dsc, qh)
+            keep(lo, mm(r.vt[lo : lo + HEAD_DIM, :], dsc))
+        return (
+            (0, z.vlo, dk[:, 0 : z.vlo]),
+            (z.vlo, WIN, dk[:, z.vlo : WIN] + dv[:, 0:over]),
+            (WIN, z.kvw, dv[:, over:WIN]),
+        )
+
+    def far_copy(s):
+        return remote(
+            r.kv.at[0, s], r.kv.at[nc - 1, s], r.s_q.at[0, s], r.r_q.at[nc - 1, s], ctx=0
+        )
+
+    def back_seq(s, after_own):
+        r.dkv[s] = jnp.zeros((block, z.kvw), F32)
+        r.dqt[s] = jnp.zeros((hw, block), F32)
+        if split:
+
+            @pl.when(last)
+            def _():
+                keys = r.kv[0, s, :, 0:WIN]
+                vals = r.kv[0, s, :, z.vlo : z.vlo + WIN]
+                r.vt[...] = mm(eye, keys, NT).astype(BF16)
+
+                def keep(lo, dqt):
+                    r.dqt[s, lo : lo + HEAD_DIM, :] += dqt
+
+                q = r.qd[s, :, 0:WIN]
+                do = r.qd[s, :, z.vlo : z.vlo + WIN]
+                for lo, hi, value in pair_back(s, keys, vals, q, do, c, keep):
+                    r.kv[0, s, :, lo:hi] = value.astype(BF16)
+                far_copy(s).start()
+
         keys = r.kv[c, s, :, 0:WIN]
         vals = r.kv[c, s, :, z.vlo : z.vlo + WIN]
         r.vt[...] = mm(eye, keys, NT).astype(BF16)
-        r.dkv[s] = jnp.zeros((block, z.kvw), F32)
 
         def one_block(k):
-            j = c + (nc - c - k) % (nc - c)
+            j = c + k
 
             @pl.when(k == 0)
             def _():
                 r.seen[...] = r.qd[s]
+
+            @pl.when(k == 1)
+            def _():
+                after_own()
 
             @pl.when(k > 0)
             def _():
@@ -931,69 +987,49 @@
                 stat_copy(r.delta, 1, j, s, j).wait_recv()
                 r.seen[...] = r.kv[j, s]
 
-            q = r.seen[:, 0:WIN]
-            do = r.seen[:, z.vlo : z.vlo + WIN]
-            dk = jnp.zeros((block, WIN), F32)
-            dv = jnp.zeros((block, WIN), F32)
-            for h in range(z.heads):
-                lo = h * HEAD_DIM
-                qh = head_of(q, h)
-                doh = head_of(do, h, z.voff)
-                prob = jnp.exp(mm(keys, qh, NT) - r.lse[j, s, h : h + 1, :])
-                dprob = mm(vals, doh, NT)
-                dsc = (prob * (dprob - r.delta[j, s, h : h + 1, :])).astype(BF16)
-                dv = dv + mm(prob.astype(BF16), doh)
-                dk = dk + mm(dsc, qh)
-                dqt = mm(r.vt[lo : lo + HEAD_DIM, :], dsc)
-
+            def keep(lo, dqt):
                 @pl.when(k == 0)
                 def _():
-                    r.dqt[s, lo : lo + HEAD_DIM, :] = dqt
+                    r.dqt[s, lo : lo + HEAD_DIM, :] += dqt
 
                 @pl.when(k > 0)
                 def _():
                     r.dq_s[j, s, lo : lo + HEAD_DIM, :] = dqt.astype(BF16)
 
-            over = WIN - z.vlo
-            r.dkv[s, :, 0 : z.vlo] += dk[:, 0 : z.vlo]
-            r.dkv[s, :, z.vlo : WIN] += dk[:, z.vlo : WIN] + dv[:, 0:over]
-            r.dkv[s, :, WIN : z.kvw] += dv[:, over:WIN]
+            q = r.seen[:, 0:WIN]
+            do = r.seen[:, z.vlo : z.vlo + WIN]
+            for lo, hi, value in pair_back(s, keys, vals, q, do, j, keep):
+                r.dkv[s, :, lo:hi] += value
 
             @pl.when(k > 0)
             def _():
                 query_back_copy(c, s, j).start()
 
-        each(nc - c, one_block)
+        each(nc - c - ((nc - 1 - c) // (nc - 1) if split else 0), one_block)
+
+        @pl.when(last)
+        def _():
+            after_own()
 
     for s in range(seqs):
         out_grads(s, t, 0)
-    bgs.collect(0, out_grads)
-    deltas(0)
-    red_a.step2()
-    bgs.relay(1)
-    for s in range(seqs):
-        mls.push_all(s)
-    back_seq(0)
-    bgs.collect(1, out_grads)
-    deltas(1)
-    red_a.step3()
-    back_seq(1)
-    red_a.step4()
-    for s in range(seqs):
-        mls.join(s)
-
-    for s in range(seqs):
+    def input_back(s):
         g2s.close(s)
-    cos1, sin1 = r.cosine[...], r.sine[...]
-    for s in range(seqs):
+        if split:
+
+            @pl.when(c == 0)
+            def _():
+                far_copy(s).wait_recv()
+                r.dkv[s] += r.kv[nc - 1, s].astype(F32)
 
         def add_dq(j):
             query_back_copy(j, s, j).wait_recv()
             r.dqt[s] += r.dq_r[j, s].astype(F32)
 
-        each(c, add_dq)
+        each(c, add_dq, skip)
         r.dq[s, :, 0:hw] = jnp.transpose(r.dqt[s]) * (HEAD_DIM ** -0.5)
         r.dq[s, :, hw:WIN] = jnp.zeros((block, WIN - hw), F32)
+        cos1, sin1 = r.cosine[...], r.sine[...]
         for j in range(WIN // LANES):
             x = r.dq[s, :, j * LANES : (j + 1) * LANES]
             r.qb[s, :, j * LANES : (j + 1) * LANES] = (x * cos1 - swap(x) * sin1).astype(BF16)
@@ -1007,6 +1043,40 @@
         r.g2[s] = (mm(r.qb[s], r.wqt[...]) + mm(r.kvb[s], r.wkvt[...])).astype(BF16)
         n1s.push_all(s)
 
+    bgs.collect(0, out_grads)
+    deltas(0)
+    bgs.relay(1)
+
+    @pl.when(outer)
+    def _():
+        for s in range(seqs):
+            mls.push_all(s)
+
+    back_seq(0, red_a.step2)
+    bgs.collect(1, out_grads)
+    deltas(1)
+
+    @pl.when(inner)
+    def _():
+        for s in range(seqs):
+            mls.push_all(s)
+
+    @pl.when(c < nc - 1)
+    def _():
+        input_back(0)
+
+    mls.join(0)
+    back_seq(1, red_a.step3)
+    mls.join(1)
+
+    @pl.when(last)
+    def _():
+        input_back(0)
+
+    input_back(1)
+    red_a.step4()
+    n1s.join(0)
+
     for which, dst in ((other, r.gb_s), (d, r.gb_o)):
         cols = pl.ds(pl.multiple_of(which * half, LANES), half)
         right = flat(r.nrm[:, :, cols])
@@ -1017,11 +1087,9 @@
     send_gb = remote(r.gb_s, r.gb_r, r.s_gb.at[0], r.s_gb.at[1], dp=other)
     send_gb.start()
     red_b = Sums(send_gb, r.gb_o, r.gb_r, r.gb_c, r.gb_t, r.s_gbc, r.s_gbg)
-    n1s.join(0)
     red_b.pair()
     red_b.step1()
     n1s.join(1)
-    red_b.step2()
 
     outs = []
 
@@ -1030,29 +1098,26 @@
         cp.start()
         outs.append(cp)
 
+    red_b.step2()
+    for s in range(seqs):
+        mlp = mls.total(s)
+        r.res[s] = (r.middle[s] + vec(5, s) * mlp).astype(BF16)
+        keep_sum(5, s, r.cot[s, span(t), :].astype(F32) * mlp)
+    store(r.res, r.res_out)
     for s in range(seqs):
         grad1 = n1s.total(s)
         unit, rstd = norm_parts(r.tok[s, span(t), :].astype(F32))
         keep_sum(0, s, grad1)
         keep_sum(1, s, grad1 * unit)
         r.gtok[s] = r.midg[s] + norm_back(grad1, unit, rstd, vec(1, s))
-        if s == 0:
-            red_b.step3()
-        mlp = mls.total(s)
-        r.res[s] = (r.middle[s] + vec(5, s) * mlp).astype(BF16)
-        keep_sum(5, s, r.cot[s, span(t), :].astype(F32) * mlp)
-    def mcol(idx):
-        return pl.ds(pl.multiple_of(idx * z.mcols, LANES), z.mcols)
 
     for k in range(1, nt):
         to = (t + k) % nt
-        remote(
-            r.msum.at[:, mcol(to)], r.mt_r.at[t], r.s_mt.at[0, to], r.s_mt.at[1, t], tp=to
-        ).start()
-    store(r.res, r.res_out)
+        remote(r.msum.at[to], r.mt_r.at[t], r.s_mt.at[0, to], r.s_mt.at[1, t], tp=to).start()
     store(r.gtok, r.gtok_out)
+    red_b.step3()
     red_b.step4()
-    total = r.msum[:, mcol(t)]
+    total = r.msum[t]
     for k in range(1, nt):
         fr = (t + k) % nt
         there = r.mt_r.at[fr]
@@ -1061,10 +1126,9 @@
     r.md_s[...] = total
     send_md = remote(r.md_s, r.md_r, r.s_md.at[0], r.s_md.at[1], dp=other)
     send_md.start()
+    r.mg[c, 0] = total
     send_md.wait()
-    r.mg[pl.ds(c, 1), 0:2, :] = total[None, 0:2, :]
-    r.mg[pl.ds(c, 1), 2:4, :] = r.md_r[0:2, :][None]
-    r.mg[pl.ds(c, 1), 4:8, :] = jnp.zeros((1, 4, z.mcols), F32)
+    r.mg[c, 1] = r.md_r[...]
 
     def send_mg(k):
         to = (c + k) % nc
@@ -1094,7 +1158,7 @@
     for k in range(1, nt):
         to = (t + k) % nt
         remote(
-            r.msum.at[:, mcol(to)], r.mt_r.at[t], r.s_mt.at[0, to], r.s_mt.at[1, t], tp=to
+            r.msum.at[to], r.mt_r.at[t], r.s_mt.at[0, to], r.s_mt.at[1, t], tp=to
         ).wait_send()
 
     def kv_sent(to):
@@ -1107,9 +1171,20 @@
                 ).wait_send()
 
             each(nt, one)
+
+    each(nc, kv_sent, c + 1)
+
+    def parts_sent(to):
+        for s in range(seqs):
             query_back_copy(c, s, to).wait_send()
 
-    each(nc, kv_sent, c + 1)
+    each(nc - ((nc - 1 - c) // (nc - 1) if split else 0), parts_sent, c + 1)
+    if split:
+
+        @pl.when(last)
+        def _():
+            for s in range(seqs):
+                far_copy(s).wait_send()
 
     def query_sent(to):
         for s in range(seqs):
@@ -1118,7 +1193,7 @@
             stat_copy(r.lse, 0, c, s, to).wait_send()
             stat_copy(r.delta, 1, c, s, to).wait_send()
 
-    each(c, query_sent)
+    each(c, query_sent, skip)
     for cp in outs:
         cp.wait()
 
@@ -1154,13 +1229,25 @@
         put(2 + i, gb[i * hw : (i + 1) * hw, :].astype(F32))
     fetches[2].wait()
     fetches[3].wait()
-    e = emb[...].reshape(z.nc * 8, z.half).astype(BF16)
-    rest = mg[...].reshape(z.nc * 8, z.mcols)
+    rest = mg[...].reshape(z.nc * 16, z.half)
     terms = []
     for _ in range(3):
         terms.append(rest.astype(BF16))
         rest = rest - terms[-1].astype(F32)
-    put(8, mm(jnp.concatenate([e] * 3, axis=0), jnp.concatenate(terms, axis=0), TN))
+    terms = jnp.concatenate(terms, axis=0)
+    row = lax.broadcasted_iota(jnp.int32, (8, z.half), 0)
+    columns = []
+    for k in range(z.thirds):
+        left = []
+        for c in range(z.nc):
+            for d in range(2):
+                one, two = emb[c, 2 * d : 2 * d + 1, :], emb[c, 2 * d + 1 : 2 * d + 2, :]
+                left.append(
+                    jnp.where(row == k, one, jnp.where(row == z.thirds + k, two, 0.0))
+                )
+        left = jnp.concatenate(left, axis=0).astype(BF16)
+        columns.append(mm(jnp.concatenate([left] * 3, axis=0), terms, TN))
+    put(8, jnp.concatenate(columns, axis=1))
     fetches[4].wait()
     through(0, res)
     fetches[5].wait()
@@ -1202,7 +1289,7 @@
                 shape((z.half, z.wide), BF16),
                 shape((z.heads_rows, z.half), BF16),
                 shape((z.nc, 8, z.half), F32),
-                shape((z.nc, 8, z.mcols), F32),
+                shape((z.nc, 2, 8, z.half), F32),
             ),
             in_specs=[hbm, smem] + [hbm] * 8,
             out_specs=[hbm] * 6,

time: 137 us -> 130 us (0.949)
  Pallas kernels: 136 us -> 129 us
    pallas_call x1, Pallas kernels: 132 us -> 125 us  [shards(): pl.pallas_call(functools.partial(layer_kernel, z, names), out_shape=(shap...]
where the time goes in v5:
time: 130 us
  Pallas kernels  129 us (99%)
    pallas_call x1, Pallas kernels, shards(): pl.pallas_call(functools.partial(layer_kernel, z, names), out_shape=(shap...  125 us
    pallas_call x1, Pallas kernels, shards(): pl.pallas_call(functools.partial(finish_kernel, z), out_shape=tuple((shap...  4.03 us

profile of v5, /device:TPU:0, one launch (start us, length us, event | category | flops | bytes accessed | tf_op | source)
XLA Modules:
  0.0 130.1 jit_solution(6772390059910376223)
XLA Ops:
  0.6 125.2 %layer.1 = (bf16[2,64,768]{2,1,0:T(8,128)(2,1)}, f32[2,64,768]{2,1,0:T(8,128)}, bf16[384,1536]{1,0:T(8,128)(2,1)}, bf16[768,384]{1,0:T(8,128)(2,1)}, f32[4,8,384]{2,1,0:T(8,128)}, /*index=5*/f32[4,2,8,384]{3,2,1,0:T(8,128)}) custom-call(bf16[2,64,768]{2,1,0:T(8,128)(2,1)} %refs_0_.1, s32[1,2]{1,0:T(1,128)} %bitcast.13, bf16[192,384]{1,0:T(8,128)(2,1)} %bitcast.9, ...), custom_call_target="tpu_custom_call" | custom-call | tf_op jit(solution)/shard_map/layer/pallas_call | solution.py:1284
  125.9 4.0 %finish.1 = (bf16[2,64,768]{2,1,0:T(8,128)(2,1)}, f32[2,64,768]{2,1,0:T(8,128)}, f32[192,384]{1,0:T(8,128)}, f32[192,384]{1,0:T(8,128)}, f32[192,384]{1,0:T(8,12...) custom-call(bf16[384,1536]{1,0:T(8,128)(2,1)} %get-tuple-element.24.refs_0_, ...), custom_call_target="tpu_custom_call" | custom-call | tf_op jit(solution)/shard_map/finish/pallas_call | solution.py:1314

commit v6 on v5

--- a/solution.py
+++ b/solution.py
@@ -154,47 +154,48 @@
         s_loc=sem(16),
         s_w=sem(2, 6),
         s_e=sem(2),
-        s_ec=sem(2, z.nc),
+        s_ec=sem(z.nc),
+        s_all=sem(3),
         s_m=sem(2, 2),
-        s_tok=sem(z.seqs, 4),
+        s_tok=sem(z.seqs),
         r_tok=sem(z.seqs, z.nt),
-        s_cot=sem(z.seqs, 4),
+        s_cot=sem(z.seqs),
         r_cot=sem(z.seqs, z.nt),
-        s_kv=sem(z.nc, z.seqs, z.nt),
-        r_kv=sem(z.nc, z.seqs, z.nt),
-        s_br=sem(z.seqs, 4),
+        s_kv=sem(z.nc),
+        r_kv=sem(z.nc, z.seqs),
+        s_br=sem(z.seqs),
         m_br=sem(z.seqs, 2),
         r_br=sem(z.seqs, 2),
-        s_n2=sem(z.seqs, 4),
+        s_n2=sem(z.seqs),
         r_n2=sem(z.seqs, z.nt),
-        s_g2=sem(z.seqs, 4),
+        s_g2=sem(z.seqs),
         m_g2=sem(z.seqs, 2),
         r_g2=sem(z.seqs, 2),
-        s_ml=sem(z.seqs, 4),
+        s_ml=sem(z.seqs),
         m_ml=sem(z.seqs, 2),
         r_ml=sem(z.seqs, 2),
-        s_bg=sem(z.seqs, 4),
+        s_bg=sem(z.seqs),
         r_bg=sem(z.seqs, z.nt),
-        s_q=sem(z.nc, z.seqs),
+        s_q=sem(z.nc),
         r_q=sem(z.nc, z.seqs),
-        s_do=sem(z.nc, z.seqs, z.nt),
-        r_do=sem(z.nc, z.seqs, z.nt),
-        s_st=sem(2, z.nc, z.seqs),
+        s_do=sem(z.nc),
+        r_do=sem(z.nc, z.seqs),
+        s_st=sem(2, z.nc),
         r_st=sem(2, z.nc, z.seqs),
-        s_dq=sem(z.nc, z.seqs),
+        s_dq=sem(z.nc),
         r_dq=sem(z.nc, z.seqs),
-        s_n1=sem(z.seqs, 4),
+        s_n1=sem(z.seqs),
         m_n1=sem(z.seqs, 2),
         r_n1=sem(z.seqs, 2),
         s_ga=sem(2),
-        s_gac=sem(2, max(z.nc, 12)),
-        s_gag=sem(2, max(z.nc, 12)),
+        s_gac=sem(12) if z.nc == 4 else sem(2, z.nc),
+        s_gag=sem(2) if z.nc == 4 else sem(2, z.nc),
         s_gb=sem(2),
-        s_gbc=sem(2, max(z.nc, 12)),
-        s_gbg=sem(2, max(z.nc, 12)),
-        s_mt=sem(2, z.nt),
+        s_gbc=sem(12) if z.nc == 4 else sem(2, z.nc),
+        s_gbg=sem(2) if z.nc == 4 else sem(2, z.nc),
+        s_mt=sem(z.nt),
         s_md=sem(2),
-        s_mc=sem(2, z.nc),
+        s_mc=sem(z.nc),
     )
 
 
@@ -304,17 +305,17 @@
         def __init__(self, buf, send, recv):
             self.buf, self.sems, self.recv = buf, send, recv
 
-        def copy(self, src, s, idx, k, to):
+        def copy(self, src, s, idx, to):
             return remote(
-                src, piece(self.buf, s, idx), self.sems.at[s, k], self.recv.at[s, idx], tp=to
+                src, piece(self.buf, s, idx), self.sems.at[s], self.recv.at[s, idx], tp=to
             )
 
         def open(self, src, s):
-            self.copy(src, s, t, 1, cross).start()
-            self.copy(src, s, t, 0, mate).start()
+            self.copy(src, s, t, cross).start()
+            self.copy(src, s, t, mate).start()
 
         def wait(self, s, idx):
-            self.copy(piece(self.buf, s, idx), s, idx, 0, mate).wait_recv()
+            self.copy(piece(self.buf, s, idx), s, idx, mate).wait_recv()
 
         def relay(self, s):
             @pl.when(inner)
@@ -322,7 +323,7 @@
                 def one(i):
                     idx = peer(i)
                     self.wait(s, idx)
-                    self.copy(piece(self.buf, s, idx), s, idx, i, mate).start()
+                    self.copy(piece(self.buf, s, idx), s, idx, mate).start()
 
                 each(4, one, 2)
 
@@ -340,24 +341,28 @@
             each(4, one, 1)
 
         def close(self, s):
-            mine = piece(self.buf, s, t)
-            self.copy(mine, s, t, 0, mate).wait_send()
-            self.copy(mine, s, t, 1, cross).wait_send()
+            def sent(count):
+                all_sent = self.buf.at[s, 0 : count * rows, :]
+                remote(all_sent, all_sent, self.sems.at[s], self.recv.at[s, t], tp=mate).wait_send()
+
+            @pl.when(outer)
+            def _():
+                sent(2)
 
             @pl.when(inner)
             def _():
-                each(4, lambda i: self.copy(mine, s, t, i, mate).wait_send(), 2)
+                sent(4)
 
     class Scatter:
         def __init__(self, part, merge, got, send, msem, gsem):
             self.part, self.merge, self.got = part, merge, got
             self.sems, self.msem, self.gsem = send, msem, gsem
 
-        def to_got(self, s, idx, i, k):
+        def to_got(self, s, idx, k):
             return remote(
                 piece(self.part, s, idx),
                 self.got.at[s, k],
-                self.sems.at[s, i],
+                self.sems.at[s],
                 self.gsem.at[s, k],
                 tp=idx,
             )
@@ -366,7 +371,7 @@
             return remote(
                 piece(self.part, s, idx),
                 self.merge.at[s, i - 2],
-                self.sems.at[s, i],
+                self.sems.at[s],
                 self.msem.at[s, i - 2],
                 tp=mate,
             )
@@ -374,7 +379,7 @@
         def push(self, s, idx, i):
             @pl.when(i == 1)
             def _():
-                self.to_got(s, idx, i, 0).start()
+                self.to_got(s, idx, 0).start()
 
             @pl.when((i > 1) & outer)
             def _():
@@ -396,13 +401,13 @@
                     self.part[s, at, :] = (
                         self.part[s, at, :].astype(F32) + self.merge[s, i - 2].astype(F32)
                     ).astype(BF16)
-                    self.to_got(s, idx, i, 1).start()
+                    self.to_got(s, idx, 1).start()
 
                 each(2, one)
 
         def total(self, s):
             for k in range(2):
-                self.to_got(s, mate, 1, k).wait_recv()
+                self.to_got(s, mate, k).wait_recv()
             return (
                 self.part[s, span(t), :].astype(F32)
                 + self.got[s, 0].astype(F32)
@@ -410,7 +415,8 @@
             )
 
         def close(self, s):
-            each(4, lambda i: self.to_got(s, mate, i, 0).wait_send(), 1)
+            all_sent = self.part.at[s, 0 : 3 * rows, :]
+            remote(all_sent, all_sent, self.sems.at[s], self.gsem.at[s, 0], tp=mate).wait_send()
 
     toks = Gather(r.tok, r.s_tok, r.r_tok)
     cots = Gather(r.cot, r.s_cot, r.r_cot)
@@ -467,7 +473,7 @@
 
     def send_ctx_emb(k):
         to = (c + k) % nc
-        remote(r.emb.at[c], r.emb.at[c], r.s_ec.at[0, to], r.s_ec.at[1, c], ctx=to).start()
+        remote(r.emb.at[c], r.emb.at[c], r.s_all.at[2], r.s_ec.at[c], ctx=to).start()
 
     each(nc, send_ctx_emb, 1)
 
@@ -513,7 +519,7 @@
 
         def send_kv(to):
             mine = r.kv.at[c, s, at, :]
-            remote(mine, mine, r.s_kv.at[to, s, idx], r.r_kv.at[c, s, idx], ctx=to).start()
+            remote(mine, mine, r.s_kv.at[to], r.r_kv.at[c, s], ctx=to).start()
 
         each(nc, send_kv, c + 1)
 
@@ -554,13 +560,8 @@
 
             @pl.when(back > 0)
             def _():
-                def take(idx):
-                    there = r.kv.at[j, s, span(idx), :]
-                    remote(
-                        there, there, r.s_kv.at[j, s, idx], r.r_kv.at[j, s, idx], ctx=j
-                    ).wait_recv()
-
-                each(nt, take)
+                there = r.kv.at[j, s]
+                remote(there, there, r.s_kv.at[j], r.r_kv.at[j, s], ctx=j).wait_recv()
 
             keys = r.kv[j, s, :, 0:WIN]
             r.vt[...] = mm(eye, r.kv[j, s, :, z.vlo : z.vlo + WIN], NT).astype(BF16)
@@ -602,14 +603,14 @@
         return remote(
             r.qd.at[s, :, 0:LANES],
             r.kv.at[j, s, :, 0:LANES],
-            r.s_q.at[to, s],
+            r.s_q.at[to],
             r.r_q.at[j, s],
             ctx=to,
         )
 
     def stat_copy(buf, which, j, s, to):
         return remote(
-            buf.at[j, s], buf.at[j, s], r.s_st.at[which, to, s], r.r_st.at[which, j, s], ctx=to
+            buf.at[j, s], buf.at[j, s], r.s_st.at[which, to], r.r_st.at[which, j, s], ctx=to
         )
 
     def send_queries(to):
@@ -747,7 +748,7 @@
     class Square:
         def __init__(self, got, mine, theirs, buf, total, sems, sems_all):
             self.got, self.mine, self.theirs, self.buf, self.total = got, mine, theirs, buf, total
-            self.sems = sems
+            self.sems, self.sems_all = sems, sems_all
             self.part = buf.shape[1] // 2
             by_x = c + 1 - 2 * (c % 2)
             by_y = (c + 2) % 4
@@ -763,8 +764,8 @@
             return remote(
                 self.mine.at[self.rows(o, h), :],
                 self.buf.at[2 * h + k, 0 : self.part, :],
-                self.sems.at[0, 2 * h + k],
-                self.sems.at[1, 2 * h + k],
+                self.sems_all.at[0],
+                self.sems.at[2 * h + k],
                 ctx=self.near[h],
             )
 
@@ -773,15 +774,15 @@
             return remote(
                 self.mine.at[self.rows(o, h), :],
                 self.buf.at[2 * h, self.part : 2 * self.part, :],
-                self.sems.at[0, 4 + h],
-                self.sems.at[1, 4 + h],
+                self.sems_all.at[0],
+                self.sems.at[4 + h],
                 ctx=o,
             )
 
         def spread(self, h, o, to, which, landed):
             at = self.total.at[self.rows(landed, h), :]
             src = self.total.at[self.rows(o, h), :]
-            return remote(src, at, self.sems.at[0, which], self.sems.at[1, which], ctx=to)
+            return remote(src, at, self.sems_all.at[1], self.sems.at[which], ctx=to)
 
         def third(self, h, landed):
             return self.spread(h, landed, self.next[h], 6 + h, landed)
@@ -833,11 +834,9 @@
             for h in range(2):
                 self.fourth(h, 0, self.near[h]).wait_recv()
                 self.fourth(h, 1, self.far).wait_recv()
-                for k in range(2):
-                    self.first(h, k).wait_send()
-                    self.fourth(h, k, c).wait_send()
-                self.second(h).wait_send()
-                self.third(h, c).wait_send()
+            for k, ref in enumerate((self.mine, self.total)):
+                part = ref.at[0 : 6 * self.part, :]
+                remote(part, part, self.sems_all.at[k], self.sems.at[0], ctx=self.far).wait_send()
 
     Sums = Square if nc == 4 else Reduction
 
@@ -888,8 +887,8 @@
         return remote(
             r.qd.at[s, at, LANES : z.kvw],
             r.kv.at[j, s, at, LANES : z.kvw],
-            r.s_do.at[to, s, idx],
-            r.r_do.at[j, s, idx],
+            r.s_do.at[to],
+            r.r_do.at[j, s],
             ctx=to,
         )
 
@@ -915,7 +914,7 @@
 
     def query_back_copy(j, s, to):
         return remote(
-            r.dq_s.at[to, s], r.dq_r.at[j, s], r.s_dq.at[to, s], r.r_dq.at[j, s], ctx=to
+            r.dq_s.at[to, s], r.dq_r.at[j, s], r.s_dq.at[to], r.r_dq.at[j, s], ctx=to
         )
 
     over = WIN - z.vlo
@@ -941,7 +940,7 @@
 
     def far_copy(s):
         return remote(
-            r.kv.at[0, s], r.kv.at[nc - 1, s], r.s_q.at[0, s], r.r_q.at[nc - 1, s], ctx=0
+            r.kv.at[0, s], r.kv.at[nc - 1, s], r.s_q.at[0], r.r_q.at[nc - 1, s], ctx=0
         )
 
     def back_seq(s, after_own):
@@ -982,7 +981,8 @@
             @pl.when(k > 0)
             def _():
                 query_copy(j, s, j).wait_recv()
-                each(nt, lambda idx: grad_copy(j, s, idx, j).wait_recv())
+                there = r.kv.at[j, s, :, LANES : z.kvw]
+                remote(there, there, r.s_do.at[j], r.r_do.at[j, s], ctx=j).wait_recv()
                 stat_copy(r.lse, 0, j, s, j).wait_recv()
                 stat_copy(r.delta, 1, j, s, j).wait_recv()
                 r.seen[...] = r.kv[j, s]
@@ -1068,13 +1068,13 @@
     mls.join(0)
     back_seq(1, red_a.step3)
     mls.join(1)
+    red_a.step4()
 
     @pl.when(last)
     def _():
         input_back(0)
 
     input_back(1)
-    red_a.step4()
     n1s.join(0)
 
     for which, dst in ((other, r.gb_s), (d, r.gb_o)):
@@ -1113,7 +1113,7 @@
 
     for k in range(1, nt):
         to = (t + k) % nt
-        remote(r.msum.at[to], r.mt_r.at[t], r.s_mt.at[0, to], r.s_mt.at[1, t], tp=to).start()
+        remote(r.msum.at[to], r.mt_r.at[t], r.s_all.at[0], r.s_mt.at[t], tp=to).start()
     store(r.gtok, r.gtok_out)
     red_b.step3()
     red_b.step4()
@@ -1121,7 +1121,7 @@
     for k in range(1, nt):
         fr = (t + k) % nt
         there = r.mt_r.at[fr]
-        remote(there, there, r.s_mt.at[0, fr], r.s_mt.at[1, fr], tp=fr).wait_recv()
+        remote(there, there, r.s_all.at[0], r.s_mt.at[fr], tp=fr).wait_recv()
         total = total + r.mt_r[fr]
     r.md_s[...] = total
     send_md = remote(r.md_s, r.md_r, r.s_md.at[0], r.s_md.at[1], dp=other)
@@ -1132,7 +1132,7 @@
 
     def send_mg(k):
         to = (c + k) % nc
-        remote(r.mg.at[c], r.mg.at[c], r.s_mc.at[0, to], r.s_mc.at[1, c], ctx=to).start()
+        remote(r.mg.at[c], r.mg.at[c], r.s_all.at[1], r.s_mc.at[c], ctx=to).start()
 
     each(nc, send_mg, 1)
     red_a.take()
@@ -1143,8 +1143,7 @@
     def take_small(k):
         fr = (c + k) % nc
         for buf, sems in ((r.mg, r.s_mc), (r.emb, r.s_ec)):
-            remote(buf.at[fr], buf.at[fr], sems.at[0, fr], sems.at[1, fr], ctx=fr).wait_recv()
-            remote(buf.at[c], buf.at[c], sems.at[0, fr], sems.at[1, c], ctx=fr).wait_send()
+            remote(buf.at[fr], buf.at[fr], r.s_all.at[1], sems.at[fr], ctx=fr).wait_recv()
 
     each(nc, take_small, 1)
     store(r.mg, r.mg_out)
@@ -1155,43 +1154,36 @@
     for s in range(seqs):
         for group in (toks, cots, n2s, bgs, brs, mls, n1s):
             group.close(s)
-    for k in range(1, nt):
-        to = (t + k) % nt
-        remote(
-            r.msum.at[to], r.mt_r.at[t], r.s_mt.at[0, to], r.s_mt.at[1, t], tp=to
-        ).wait_send()
+    for k, (buf, count) in enumerate(((r.msum, nt), (r.mg, nc), (r.emb, nc))):
+        part = buf.at[0 : count - 1]
+        remote(part, part, r.s_all.at[k], r.s_mc.at[c], dp=other).wait_send()
 
     def kv_sent(to):
-        for s in range(seqs):
-
-            def one(idx):
-                mine = r.kv.at[c, s, span(idx), :]
-                remote(
-                    mine, mine, r.s_kv.at[to, s, idx], r.r_kv.at[c, s, idx], ctx=to
-                ).wait_send()
-
-            each(nt, one)
+        mine = r.kv.at[c]
+        remote(mine, mine, r.s_kv.at[to], r.r_kv.at[c, 0], ctx=to).wait_send()
 
     each(nc, kv_sent, c + 1)
 
     def parts_sent(to):
-        for s in range(seqs):
-            query_back_copy(c, s, to).wait_send()
+        mine = r.dq_s.at[to]
+        remote(mine, mine, r.s_dq.at[to], r.r_dq.at[c, 0], ctx=to).wait_send()
 
     each(nc - ((nc - 1 - c) // (nc - 1) if split else 0), parts_sent, c + 1)
     if split:
 
         @pl.when(last)
         def _():
-            for s in range(seqs):
-                far_copy(s).wait_send()
+            mine = r.kv.at[0]
+            remote(mine, mine, r.s_q.at[0], r.r_q.at[nc - 1, 0], ctx=0).wait_send()
 
     def query_sent(to):
-        for s in range(seqs):
-            query_copy(c, s, to).wait_send()
-            each(nt, lambda idx: grad_copy(c, s, idx, to).wait_send())
-            stat_copy(r.lse, 0, c, s, to).wait_send()
-            stat_copy(r.delta, 1, c, s, to).wait_send()
+        for src, sems, recv in (
+            (r.qd.at[:, :, 0:LANES], r.s_q.at[to], r.r_q.at[c, 0]),
+            (r.qd.at[:, :, LANES : z.kvw], r.s_do.at[to], r.r_do.at[c, 0]),
+            (r.lse.at[c], r.s_st.at[0, to], r.r_st.at[0, c, 0]),
+            (r.delta.at[c], r.s_st.at[1, to], r.r_st.at[1, c, 0]),
+        ):
+            remote(src, src, sems, recv, ctx=to).wait_send()
 
     each(c, query_sent, skip)
     for cp in outs:

time: 130 us -> 129 us (level)
    pallas_call x1, Pallas kernels: 125 us -> 124 us  [shards(): pl.pallas_call(functools.partial(layer_kernel, z, names), out_shape=(shap...]
where the time goes in v6:
time: 129 us; the launch traced here: 128 us
  Pallas kernels  128 us (99%)
    pallas_call x1, Pallas kernels, shards(): pl.pallas_call(functools.partial(layer_kernel, z, names), out_shape=(shap...  124 us
    pallas_call x1, Pallas kernels, shards(): pl.pallas_call(functools.partial(finish_kernel, z), out_shape=tuple((shap...  4.03 us

profile of v6, /device:TPU:0, one launch (start us, length us, event | category | flops | bytes accessed | tf_op | source)
XLA Modules:
  0.0 128.5 jit_solution(18278760847935013738)
XLA Ops:
  0.6 123.6 %layer.1 = (bf16[2,64,768]{2,1,0:T(8,128)(2,1)}, f32[2,64,768]{2,1,0:T(8,128)}, bf16[384,1536]{1,0:T(8,128)(2,1)}, bf16[768,384]{1,0:T(8,128)(2,1)}, f32[4,8,384]{2,1,0:T(8,128)}, /*index=5*/f32[4,2,8,384]{3,2,1,0:T(8,128)}) custom-call(bf16[2,64,768]{2,1,0:T(8,128)(2,1)} %refs_0_.1, s32[1,2]{1,0:T(1,128)} %bitcast.13, bf16[192,384]{1,0:T(8,128)(2,1)} %bitcast.9, ...), custom_call_target="tpu_custom_call" | custom-call | tf_op jit(solution)/shard_map/layer/pallas_call | solution.py:1276
  124.3 4.0 %finish.1 = (bf16[2,64,768]{2,1,0:T(8,128)(2,1)}, f32[2,64,768]{2,1,0:T(8,128)}, f32[192,384]{1,0:T(8,128)}, f32[192,384]{1,0:T(8,128)}, f32[192,384]{1,0:T(8,12...) custom-call(bf16[384,1536]{1,0:T(8,128)(2,1)} %get-tuple-element.24.refs_0_, ...), custom_call_target="tpu_custom_call" | custom-call | tf_op jit(solution)/shard_map/finish/pallas_call | solution.py:1306

commit v7 on v6

--- a/solution.py
+++ b/solution.py
@@ -234,6 +234,16 @@
     def lanes_of(shape, axis=1):
         return lax.broadcasted_iota(jnp.int32, shape, axis)
 
+    bar = pltpu.get_barrier_semaphore()
+    pl.semaphore_signal(bar, inc=1, device_id={"dp": other}, device_id_type=MESH)
+    for k in range(1, nt):
+        pl.semaphore_signal(bar, inc=1, device_id={"tp": (t + k) % nt}, device_id_type=MESH)
+
+    def greet(k):
+        pl.semaphore_signal(bar, inc=1, device_id={"ctx": (c + k) % nc}, device_id_type=MESH)
+
+    each(nc, greet, 1)
+
     local = []
 
     def fetch(src, dst):
@@ -260,16 +270,6 @@
 
     r.wqt[hw:WIN, :] = jnp.zeros((WIN - hw, width), BF16)
     r.wot[0 : z.voff, :] = jnp.zeros((z.voff, width), BF16)
-
-    bar = pltpu.get_barrier_semaphore()
-    pl.semaphore_signal(bar, inc=1, device_id={"dp": other}, device_id_type=MESH)
-    for k in range(1, nt):
-        pl.semaphore_signal(bar, inc=1, device_id={"tp": (t + k) % nt}, device_id_type=MESH)
-
-    def greet(k):
-        pl.semaphore_signal(bar, inc=1, device_id={"ctx": (c + k) % nc}, device_id_type=MESH)
-
-    each(nc, greet, 1)
 
     row8 = lanes_of((8, half), 0)
     step_of = jnp.where(
@@ -527,15 +527,16 @@
     for s in range(seqs):
         make_qkv(s, t, 0)
     mod2 = mod_part(first_cols, z.mod, 1, cp_wm2)
-    for s in range(seqs):
-        toks.relay(s)
-        toks.collect(s, make_qkv)
+    toks.relay(0)
+    toks.collect(0, make_qkv)
+    toks.relay(1)
 
     @pl.when(inner)
     def _():
         for s in range(seqs):
             cots.open(r.cot_in.at[s], s)
 
+    toks.collect(1, make_qkv)
     cp_cot.wait()
     mod_take(first_cols, z.mod, mod2)
     for i in range(3, 6):
@@ -862,17 +863,16 @@
 
     middle_back(0)
 
-    def pair_grads(lhs, rhs, mine, sent, lo, hi):
-        right = flat(rhs[...])
-        for which, dst in ((other, sent), (d, mine)):
-            cols = pl.ds(pl.multiple_of(which * half, half), half)
-            left = flat(lhs[:, :, cols])
-            dst[:, lo:hi] = mm(left, right, TN).astype(BF16)
-
-    pair_grads(r.mgrad, r.act, r.ga_o, r.ga_s, z.ff, 2 * z.ff)
-    pair_grads(r.n2, r.hgrad, r.ga_o, r.ga_s, 0, z.ff)
+    def pair_grads(which, dst):
+        cols = pl.ds(pl.multiple_of(which * half, half), half)
+        for k, (lhs, rhs) in enumerate(((r.n2, r.hgrad), (r.mgrad, r.act))):
+            grad = mm(flat(lhs[:, :, cols]), flat(rhs[...]), TN)
+            dst[:, k * z.ff : (k + 1) * z.ff] = grad.astype(BF16)
+
     send_ga = remote(r.ga_s, r.ga_r, r.s_ga.at[0], r.s_ga.at[1], dp=other)
+    pair_grads(other, r.ga_s)
     send_ga.start()
+    pair_grads(d, r.ga_o)
     g2s.join(1)
     bgs.relay(0)
     red_a = Sums(send_ga, r.ga_o, r.ga_r, r.ga_c, r.ga_t, r.s_gac, r.s_gag)
@@ -1077,15 +1077,18 @@
     input_back(1)
     n1s.join(0)
 
-    for which, dst in ((other, r.gb_s), (d, r.gb_o)):
+    def head_grads(which, dst):
         cols = pl.ds(pl.multiple_of(which * half, LANES), half)
         right = flat(r.nrm[:, :, cols])
         dst[0:hw, :] = mm(flat(r.qb[:, :, 0:hw]), right, TN).astype(BF16)
         dst[hw : 3 * hw, :] = mm(flat(r.kvb[...]), right, TN).astype(BF16)
         right = flat(r.bg[:, :, cols])
         dst[3 * hw : 4 * hw, :] = mm(flat(r.attl[:, :, 0:hw]), right, TN).astype(BF16)
+
     send_gb = remote(r.gb_s, r.gb_r, r.s_gb.at[0], r.s_gb.at[1], dp=other)
+    head_grads(other, r.gb_s)
     send_gb.start()
+    head_grads(d, r.gb_o)
     red_b = Sums(send_gb, r.gb_o, r.gb_r, r.gb_c, r.gb_t, r.s_gbc, r.s_gbg)
     red_b.pair()
     red_b.step1()
@@ -1197,8 +1200,8 @@
     fetches = [
         pltpu.make_async_copy(src, dst, sems.at[i]) for i, (src, dst) in enumerate(zip(ins, held))
     ]
-    for cp in fetches:
-        cp.start()
+    for i in (2, 3, 1, 0, 4, 5):
+        fetches[i].start()
     ga, gb, emb, mg, res, gtok = held
     copies = []
 
@@ -1213,12 +1216,6 @@
         cp.start()
         copies.append(cp)
 
-    fetches[0].wait()
-    put(6, ga[:, 0 : z.ff].astype(F32))
-    put(7, ga[:, z.ff : 2 * z.ff].astype(F32))
-    fetches[1].wait()
-    for i in range(4):
-        put(2 + i, gb[i * hw : (i + 1) * hw, :].astype(F32))
     fetches[2].wait()
     fetches[3].wait()
     rest = mg[...].reshape(z.nc * 16, z.half)
@@ -1240,6 +1237,12 @@
         left = jnp.concatenate(left, axis=0).astype(BF16)
         columns.append(mm(jnp.concatenate([left] * 3, axis=0), terms, TN))
     put(8, jnp.concatenate(columns, axis=1))
+    fetches[0].wait()
+    put(6, ga[:, 0 : z.ff].astype(F32))
+    put(7, ga[:, z.ff : 2 * z.ff].astype(F32))
+    fetches[1].wait()
+    for i in range(4):
+        put(2 + i, gb[i * hw : (i + 1) * hw, :].astype(F32))
     fetches[4].wait()
     through(0, res)
     fetches[5].wait()

time: 129 us -> 128 us (level)
  no operation moved by 1% of the time
where the time goes in v7:
time: 128 us; the launch traced here: 127 us
  Pallas kernels  127 us (99%)
    pallas_call x1, Pallas kernels, shards(): pl.pallas_call(functools.partial(layer_kernel, z, names), out_shape=(shap...  123 us
    pallas_call x1, Pallas kernels, shards(): pl.pallas_call(functools.partial(finish_kernel, z), out_shape=tuple((shap...  4.09 us

profile of v7, /device:TPU:0, one launch (start us, length us, event | category | flops | bytes accessed | tf_op | source)
XLA Modules:
  0.0 127.5 jit_solution(1843100215389519621)
XLA Ops:
  0.6 122.6 %layer.1 = (bf16[2,64,768]{2,1,0:T(8,128)(2,1)}, f32[2,64,768]{2,1,0:T(8,128)}, bf16[384,1536]{1,0:T(8,128)(2,1)}, bf16[768,384]{1,0:T(8,128)(2,1)}, f32[4,8,384]{2,1,0:T(8,128)}, /*index=5*/f32[4,2,8,384]{3,2,1,0:T(8,128)}) custom-call(bf16[2,64,768]{2,1,0:T(8,128)(2,1)} %refs_0_.1, s32[1,2]{1,0:T(1,128)} %bitcast.13, bf16[192,384]{1,0:T(8,128)(2,1)} %bitcast.9, ...), custom_call_target="tpu_custom_call" | custom-call | tf_op jit(solution)/shard_map/layer/pallas_call | solution.py:1279
  123.2 4.1 %finish.1 = (bf16[2,64,768]{2,1,0:T(8,128)(2,1)}, f32[2,64,768]{2,1,0:T(8,128)}, f32[192,384]{1,0:T(8,128)}, f32[192,384]{1,0:T(8,128)}, f32[192,384]{1,0:T(8,12...) custom-call(bf16[384,1536]{1,0:T(8,128)(2,1)} %get-tuple-element.24.refs_0_, ...), custom_call_target="tpu_custom_call" | custom-call | tf_op jit(solution)/shard_map/finish/pallas_call | solution.py:1309
